TPU v7x, 1024 devices: a whole 8x8x8 slice. The times are simulated.
1024 devices in a mesh: hb: 16 (over x, core), wb: 8 (over y), hd: 8 (over z).
Axes of the slice: x: 8, y: 8, z: 8, core: 2. Of those that a mesh axis runs over, the one named last changes fastest.
Arguments:
- query_rows: bfloat16 [24, 16, 16, 64, 128], P('hd', 'hb', 'wb'), may hold values from -180 to 180
- key_rows: bfloat16 [24, 16, 16, 64, 128], P('hd', 'hb', 'wb'), may hold values from -6 to 6
- value_rows: bfloat16 [24, 16, 16, 64, 128], P('hd', 'hb', 'wb'), may hold values from -6 to 6
- grad_out: bfloat16 [24, 16, 16, 64, 128], P('hd', 'hb', 'wb'), may hold values from -6 to 6
- sel_tiles: int32 [16, 16, 8], P(None, 'wb'), may hold values from 0 to 31
- sel_count: int32 [16, 16], P(None, 'wb'), may hold values from 1 to 8, as said below
- tile_radius: int32 [24], P('hd'), may hold values from 0 to 1
Outputs:
- grad_query: bfloat16 [24, 16, 16, 64, 128], P('hd', 'hb', 'wb')
- grad_key: bfloat16 [24, 16, 16, 64, 128], P('hd', 'hb', 'wb')
- grad_value: bfloat16 [24, 16, 16, 64, 128], P('hd', 'hb', 'wb')
Inputs may be any that keep to these rules, and one draw needn't show every extreme that they name: sel_count[r, c] is the number of live entries of that query tile's list, from 1 to 8; entries of sel_tiles at positions sel_count or beyond are ignored, and entries may repeat.
All inputs are finite; a program needn't handle non-finite values.
Results may differ from a plain program's by a relative error of at most 0.022.
Values may be sent and summed in bfloat16 or wider, within the bound.
No kernel may reach another device: no remote copies, remote signals or barrier semaphores. Data moves between devices by JAX's collectives and lax.ppermute only.
A program may use at most 64 MiB of HBM per device.

v0:
```python
import jax
import jax.numpy as jnp
from jax import lax
from jax.sharding import PartitionSpec as P


def with_halo(x, sides, width):
    for axis, dim in sides:
        size, length = (lax.axis_size(axis), x.shape[dim])
        up = [(i, (i + 1) % size) for i in range(size - 1)]
        down = [(j, i) for i, j in up]
        last = lax.slice_in_dim(x, length - width, length, axis=dim)
        first = lax.slice_in_dim(x, 0, width, axis=dim)
        before = lax.ppermute(last, axis, up)
        after = lax.ppermute(first, axis, down)
        x = jnp.concatenate([before, x, after], axis=dim)
    return x


def in_one_piece(arrays, axis, dim, along):
    both = jnp.concatenate(arrays, axis=along)
    result, at, outs = (lax.all_gather(both, axis, axis=dim, tiled=True), 0, [])
    for a in arrays:
        outs.append(lax.slice_in_dim(result, at, at + a.shape[along], axis=along))
        at += a.shape[along]
    return tuple(outs)


def settle(values):
    return lax.optimization_barrier(values.astype(jnp.bfloat16)).astype(jnp.float32)


def tile_masks(tile_radius, sel_tiles, sel_count):
    band_rows, band_cols, picks = sel_tiles.shape
    tile_total = band_rows * band_cols
    tile_index = jnp.arange(tile_total, dtype=jnp.int32)
    row_of = tile_index // band_cols
    col_of = tile_index % band_cols
    spread = jnp.abs(row_of[:, None] - row_of[None, :]) + jnp.abs(col_of[:, None] - col_of[None, :])
    nearby = spread[None] <= tile_radius[:, None, None]
    live_pick = jnp.arange(picks, dtype=jnp.int32)[None, :] < sel_count.reshape(tile_total, 1)
    matches = (sel_tiles.reshape(tile_total, picks, 1) == tile_index[None, None, :]) & live_pick[
        :, :, None
    ]
    return nearby | jnp.any(matches, axis=1)[None]


def side_scores(queries, keyside, is_open, factor):
    scores = (
        jnp.einsum("hrid,hrjd->hrij", queries, keyside, preferred_element_type=jnp.float32) * factor
    )
    return jnp.where(is_open[:, None, None, None], scores, -jnp.inf)


def side_grad(probs, cotan, valside, delta, factor):
    slopes = jnp.einsum("hrid,hrjd->hrij", cotan, valside, preferred_element_type=jnp.float32)
    return (probs * (slopes - delta[..., None]) * factor).astype(jnp.bfloat16)


def edge_terms(queries, cotan, log_sum, delta, keyside, valside, is_open, factor):
    scores = (
        jnp.einsum("hrid,hrjd->hrij", queries, keyside, preferred_element_type=jnp.float32) * factor
    )
    probs = jnp.where(is_open[:, None, None, None], jnp.exp(scores - log_sum[..., None]), 0.0)
    slopes = jnp.einsum("hrid,hrjd->hrij", cotan, valside, preferred_element_type=jnp.float32)
    score_grad = (probs * (slopes - delta[..., None]) * factor).astype(jnp.bfloat16)
    key_term = jnp.einsum(
        "hrij,hrid->hrjd", score_grad, queries, preferred_element_type=jnp.float32
    )
    value_term = jnp.einsum(
        "hrij,hrid->hrjd", probs.astype(jnp.bfloat16), cotan, preferred_element_type=jnp.float32
    )
    return (key_term, value_term)


def on_device(query_rows, key_rows, value_rows, grad_out, sel_tiles, sel_count, tile_radius):
    head_count, tile_rows, tile_cols, tile_len, head_dim = query_rows.shape
    dev_tiles = tile_rows * tile_cols
    dev_rows = dev_tiles * tile_len
    factor = head_dim ** (-0.5)
    grid_shape = (head_count, tile_rows, tile_cols, tile_len)
    hb_index = lax.axis_index("hb")
    wb_index = lax.axis_index("wb")
    wb_count = lax.axis_size("wb")
    fringe = with_halo(jnp.stack((key_rows, value_rows, query_rows, grad_out)), (("wb", 3),), 1)
    band_keys, band_values, band_queries, band_cotan = in_one_piece(
        (key_rows, value_rows, query_rows, grad_out), "hb", 1, 0
    )
    band_tiles = band_keys.shape[1] * tile_cols
    allowed_all = tile_masks(tile_radius, sel_tiles, sel_count)
    own_start = hb_index * dev_tiles
    allowed_own = lax.dynamic_slice_in_dim(allowed_all, own_start, dev_tiles, 1)
    own_query = query_rows.reshape(head_count, dev_rows, head_dim)
    own_cotan = grad_out.reshape(head_count, dev_rows, head_dim)
    key_flat = band_keys.reshape(head_count, -1, head_dim)
    value_flat = band_values.reshape(head_count, -1, head_dim)
    shaped = (head_count, dev_tiles, tile_len, band_tiles, tile_len)
    scores = (
        jnp.einsum("hqd,hkd->hqk", own_query, key_flat, preferred_element_type=jnp.float32) * factor
    )
    scores = jnp.where(allowed_own[:, :, None, :, None], scores.reshape(shaped), -jnp.inf).reshape(
        head_count, dev_rows, -1
    )
    reach = tile_radius >= 1
    left_open = reach & (wb_index >= 1)
    right_open = reach & (wb_index < wb_count - 1)
    left_keys = fringe[0][:, :, 0]
    right_keys = fringe[0][:, :, -1]
    left_vals = fringe[1][:, :, 0]
    right_vals = fringe[1][:, :, -1]
    left_scores = side_scores(query_rows[:, :, 0], left_keys, left_open, factor)
    right_scores = side_scores(query_rows[:, :, -1], right_keys, right_open, factor)
    top = jnp.max(scores, axis=-1).reshape(grid_shape)
    top = top.at[:, :, 0].max(jnp.max(left_scores, axis=-1))
    top = top.at[:, :, -1].max(jnp.max(right_scores, axis=-1))
    total = jnp.sum(jnp.exp(scores - top.reshape(head_count, dev_rows, 1)), axis=-1).reshape(
        grid_shape
    )
    total = total.at[:, :, 0].add(jnp.sum(jnp.exp(left_scores - top[:, :, 0, :, None]), axis=-1))
    total = total.at[:, :, -1].add(jnp.sum(jnp.exp(right_scores - top[:, :, -1, :, None]), axis=-1))
    log_sum = top + jnp.log(total)
    probs = jnp.exp(scores - log_sum.reshape(head_count, dev_rows, 1))
    left_probs = jnp.exp(left_scores - log_sum[:, :, 0, :, None])
    right_probs = jnp.exp(right_scores - log_sum[:, :, -1, :, None])
    prob_half = probs.astype(jnp.bfloat16)
    output = jnp.einsum(
        "hqk,hkd->hqd", prob_half, value_flat, preferred_element_type=jnp.float32
    ).reshape(grid_shape + (head_dim,))
    output = output.at[:, :, 0].add(
        jnp.einsum(
            "hrij,hrjd->hrid",
            left_probs.astype(jnp.bfloat16),
            left_vals,
            preferred_element_type=jnp.float32,
        )
    )
    output = output.at[:, :, -1].add(
        jnp.einsum(
            "hrij,hrjd->hrid",
            right_probs.astype(jnp.bfloat16),
            right_vals,
            preferred_element_type=jnp.float32,
        )
    )
    delta = jnp.sum(grad_out.astype(jnp.float32) * output, axis=-1)
    edge_stats = with_halo(jnp.stack((log_sum, delta)), (("wb", 3),), 1)
    slopes = jnp.einsum("hqd,hkd->hqk", own_cotan, value_flat, preferred_element_type=jnp.float32)
    score_grad = (probs * (slopes - delta.reshape(head_count, dev_rows, 1)) * factor).astype(
        jnp.bfloat16
    )
    left_grad = side_grad(left_probs, grad_out[:, :, 0], left_vals, delta[:, :, 0], factor)
    right_grad = side_grad(right_probs, grad_out[:, :, -1], right_vals, delta[:, :, -1], factor)
    grad_query = jnp.einsum(
        "hqk,hkd->hqd", score_grad, key_flat, preferred_element_type=jnp.float32
    ).reshape(grid_shape + (head_dim,))
    grad_query = grad_query.at[:, :, 0].add(
        jnp.einsum("hrij,hrjd->hrid", left_grad, left_keys, preferred_element_type=jnp.float32)
    )
    grad_query = grad_query.at[:, :, -1].add(
        jnp.einsum("hrij,hrjd->hrid", right_grad, right_keys, preferred_element_type=jnp.float32)
    )
    band_stats = lax.all_gather(jnp.stack((log_sum, delta)), "hb", axis=2, tiled=True)
    all_query = band_queries.reshape(head_count, -1, head_dim)
    all_cotan = band_cotan.reshape(head_count, -1, head_dim)
    allowed_cols = lax.dynamic_slice_in_dim(allowed_all, own_start, dev_tiles, 2)
    reverse = (
        jnp.einsum(
            "hqd,hkd->hqk",
            all_query,
            key_rows.reshape(head_count, dev_rows, head_dim),
            preferred_element_type=jnp.float32,
        )
        * factor
    )
    rev_shape = (head_count, band_tiles, tile_len, dev_tiles, tile_len)
    row_sums = band_stats[0].reshape(head_count, band_tiles, tile_len, 1, 1)
    rev_probs = jnp.where(
        allowed_cols[:, :, None, :, None], jnp.exp(reverse.reshape(rev_shape) - row_sums), 0.0
    ).reshape(head_count, -1, dev_rows)
    rev_slopes = jnp.einsum(
        "hqd,hkd->hqk",
        all_cotan,
        value_rows.reshape(head_count, dev_rows, head_dim),
        preferred_element_type=jnp.float32,
    )
    rev_grad = (
        rev_probs * (rev_slopes - band_stats[1].reshape(head_count, -1, 1)) * factor
    ).astype(jnp.bfloat16)
    groups = lax.axis_size("hb")
    key_parts = jnp.einsum(
        "hgqk,hgqd->hgkd",
        rev_grad.reshape(head_count, groups, dev_rows, dev_rows),
        all_query.reshape(head_count, groups, dev_rows, head_dim),
        preferred_element_type=jnp.float32,
    )
    value_parts = jnp.einsum(
        "hgqk,hgqd->hgkd",
        rev_probs.astype(jnp.bfloat16).reshape(head_count, groups, dev_rows, dev_rows),
        all_cotan.reshape(head_count, groups, dev_rows, head_dim),
        preferred_element_type=jnp.float32,
    )
    key_band = jnp.sum(settle(key_parts), axis=1)
    value_band = jnp.sum(settle(value_parts), axis=1)
    key_grid = key_band.reshape(grid_shape + (head_dim,))
    value_grid = value_band.reshape(grid_shape + (head_dim,))
    left_key, left_value = edge_terms(
        fringe[2][:, :, 0],
        fringe[3][:, :, 0],
        edge_stats[0][:, :, 0],
        edge_stats[1][:, :, 0],
        key_rows[:, :, 0],
        value_rows[:, :, 0],
        left_open,
        factor,
    )
    right_key, right_value = edge_terms(
        fringe[2][:, :, -1],
        fringe[3][:, :, -1],
        edge_stats[0][:, :, -1],
        edge_stats[1][:, :, -1],
        key_rows[:, :, -1],
        value_rows[:, :, -1],
        right_open,
        factor,
    )
    key_grid = key_grid.at[:, :, 0].add(left_key).at[:, :, -1].add(right_key)
    value_grid = value_grid.at[:, :, 0].add(left_value).at[:, :, -1].add(right_value)
    return (
        grad_query.astype(jnp.bfloat16),
        key_grid.astype(jnp.bfloat16),
        value_grid.astype(jnp.bfloat16),
    )


def solution(mesh):
    return jax.shard_map(
        on_device,
        mesh=mesh,
        in_specs=(
            P("hd", "hb", "wb", None, None),
            P("hd", "hb", "wb", None, None),
            P("hd", "hb", "wb", None, None),
            P("hd", "hb", "wb", None, None),
            P(None, "wb", None),
            P(None, "wb"),
            P("hd"),
        ),
        out_specs=(
            P("hd", "hb", "wb", None, None),
            P("hd", "hb", "wb", None, None),
            P("hd", "hb", "wb", None, None),
        ),
        check_vma=False,
    )
```

profile of v0, /device:TPU:1, one launch (start us, length us, event | category | flops | bytes accessed | tf_op | source)
XLA Modules:
  0.0 137.1 jit_solution(6158767462030387247)
XLA Ops:
  7.2 1.9 %pad_maximum_fusion.1 = bf16[12,1,2,64,128]{4,3,2,1,0:T(8,128)(2,1)} fusion(bf16[3,1,2,64,128]{4,3,2,1,0:T(8,128)(2,1)} %param.34, bf16[3,1,2,64,128]{4,3,2,1,0:T(8,128)(2,1)} %param.31, bf16[3,1,2,64,128]{4,3,2,1,0:T(8,128)(2,1)} %param.33, bf16[3,1,2,64,128]{4,3,2,1,0:T(8,128)(2,1)} %param.32), kind=kLoop, calls=%fused_computation.73 | loop fusion | flops 589824 | bytes 786432 | tf_op jit(solution)/shard_map/concatenate | solution.py:21
  9.1 1.7 %copy_bitcast_fusion = (bf16[1,3,1,2,64,128]{5,4,1,3,2,0:T(8,128)(2,1)S(1)}, bf16[3,1,2,64,128]{4,3,0,2,1:T(8,128)(2,1)}, bf16[1,3,1,2,64,128]{5,4,1,3,2,0:T(8,128)(2,1)S(1)}, bf16[3,1,2,64,128]{4,3,0,2,1:T(8,128)(2,1)}) fusion(bf16[3,1,2,64,128]{4,3,2,1,0:T(8,128)(2,1)} %param.31, bf16[3,1,2,64,128]{4,3,2,1,0:T(8,128)(2,1)} %param.33), kind=kLoop, calls=%fused_computation.165 | loop fusion | bytes 589824 | tf_op jit(solution)/shard_map/stack | solution.py:85
  10.9 0.8 fusion.79
  11.7 0.7 fusion.76
  12.4 1.3 collective-permute-start.1
  13.7 4.8 %collective-permute-start = (bf16[4,3,1,1,64,128]{5,4,1,3,2,0:T(8,128)(2,1)S(1)}, bf16[4,3,1,1,64,128]{5,4,1,3,2,0:T(8,128)(2,1)S(1)}, u32[]{:S(2)}, u32[]{:S(2)}) collective-permute-start(bf16[4,3,1,1,64,128]{5,4,1,3,2,0:T(8,128)(2,1)S(1)} %get-tuple-element.173), channel_id=1, source_target_pairs={{0,8},{8,16},{16,24},{24,32},{32,40},{40,48},{48,56},{1,9},{9,17},... | collective-permute-start | bytes 589832 | tf_op jit(solution)/shard_map/ppermute | solution.py:14
  18.8 0.2 fusion.48
  19.3 0.1 copy.239
  19.4 0.5 broadcast_in_dim.72
  19.9 3.9 %broadcast_in_dim.73 = pred[3,128,2048]{2,1,0:T(32,128)(4,1)S(1)} reshape(pred[3,2,64,32,64]{4,3,2,1,0:T(32,128)(4,1)S(1)} %broadcast_in_dim.72) | data formatting | bytes 1572864 | tf_op jit(solution)/shard_map/jit(_where)/broadcast_in_dim | solution.py:101
  23.8 1.8 %copy.240 = pred[3,128,2048]{1,2,0:T(32,128)(4,1)} copy(pred[3,128,2048]{2,1,0:T(32,128)(4,1)S(1)} %broadcast_in_dim.73) | data formatting | bytes 1572864 | tf_op jit(solution)/shard_map/jit(_where)/broadcast_in_dim | solution.py:101
  25.6 0.5 broadcast_in_dim.78
  26.1 3.9 %broadcast_in_dim.79 = pred[3,2048,128]{1,2,0:T(32,128)(4,1)S(1)} reshape(pred[3,32,64,2,64]{2,1,4,3,0:T(32,128)(4,1)S(1)} %broadcast_in_dim.78) | data formatting | bytes 1572864 | tf_op jit(solution)/shard_map/jit(_where)/broadcast_in_dim | solution.py:177
  30.0 1.8 %copy.272 = pred[3,2048,128]{2,1,0:T(32,128)(4,1)} copy(pred[3,2048,128]{1,2,0:T(32,128)(4,1)S(1)} %broadcast_in_dim.79) | data formatting | bytes 1572864 | tf_op jit(solution)/shard_map/jit(_where)/broadcast_in_dim | solution.py:177
  31.8 0.1 pad_maximum_fusion
  32.0 0.9 slice_bitcast_fusion
  32.9 0.2 fusion.81
  33.1 0.4 copy-done.13
  33.5 0.2 fusion.83
  33.7 40.7 %all-gather.2.cloned.1.call-done = bf16[12,16,2,64,128]{4,3,2,1,0:T(8,128)(2,1)} async-done(((bf16[12,1,2,64,128]{4,3,2,1,0:T(8,128)(2,1)}), bf16[12,16,2,64,128]{4,3,2,1,0:T(8,128)(2,1)}) %all-gather.2.cloned.1.call-update) | async-done | bytes 6291472 | tf_op jit(solution)/shard_map/all_gather | solution.py:22
  74.4 6.5 %fusion.75 = (bf16[3,16,2,64,128]{4,3,2,1,0:T(8,128)(2,1)}, bf16[3,16,2,64,128]{4,3,2,1,0:T(8,128)(2,1)}, bf16[3,16,2,64,128]{4,3,2,1,0:T(8,128)(2,1)}, bf16[3,16,2,64,128]{4,3,2,1,0:T(8,128)(2,1)S(1)}) fusion(bf16[12,16,2,64,128]{4,3,2,1,0:T(8,128)(2,1)} %all-gather.2.cloned.1.call-done), kind=kLoop, calls=%fused_computation.169 | loop fusion | bytes 12582912 | tf_op jit(solution)/shard_map/slice | solution.py:24
  80.9 0.7 fusion.82
  81.6 0.5 copy-done.2
  82.2 0.6 fusion.69
  82.8 0.6 slice_bitcast_fusion.62
  83.4 0.4 exponential_reduce_fusion
  84.0 0.7 exponential_reduce_fusion.2
  84.7 0.9 exponential_reduce_fusion.1
  85.6 0.6 sub.226
  86.2 2.2 %fusion.3 = f32[3,128,128]{2,1,0:T(8,128)S(1)} fusion(bf16[3,2048,128]{2,1,0:T(8,128)(2,1)} %bitcast.254, f32[3,128,2048]{1,2,0:T(8,128)S(1)} %get-tuple-element.204, f32[3,128]{1,0:T(4,128)} %sub.226), kind=kOutput, calls=%fused_computation.13 | convolution fusion | flops 202899456 | bytes 4916736 | tf_op jit(solution)/shard_map/hqk,hkd->hqd/dot_general | solution.py:126
  88.5 0.2 fusion.28
  88.8 0.2 fusion.30
  89.0 0.1 multiply_reduce_fusion
  89.1 0.6 copy.262
  89.7 0.6 fusion.67
  90.3 1.3 sub.235
  91.6 3.8 %fusion.6 = f32[3,128,128]{2,1,0:T(8,128)} fusion(bf16[3,2048,128]{2,1,0:T(8,128)(2,1)} %bitcast.257, bf16[3,2048,128]{2,1,0:T(8,128)(2,1)} %bitcast.255, bf16[3,128,128]{2,1,0:T(8,128)(2,1)S(1)} %bitcast.261, f32[3,128,2048]{1,2,0:T(8,128)S(1)} %get-tuple-element.204, f32[3,128]{1,0:T(4,128)} %sub.235, f32[3,128]{1,0:T(4,128)} %sub.226), kind=kOutput, calls=%fused_computation.15 | convolution fusion | flops 406585344 | bytes 6589440 | tf_op jit(solution)/shard_map/hqk,hkd->hqd/dot_general | solution.py:153
  95.4 1.0 copy.267
  96.5 16.7 %all_gather.7 = f32[2,3,16,2,64]{4,1,3,2,0:T(4,128)S(1)} all-gather(f32[2,3,1,2,64]{4,1,3,2,0:T(4,128)S(1)} %pad_maximum_fusion.4), channel_id=1, replica_groups=mesh['hb'=16,'wb'=8,'hd'=8] {'hb'}, dimensions={2}, use_global_device_ids=true | all-gather | bytes 52224 | tf_op jit(solution)/shard_map/all_gather | solution.py:162
  113.2 0.1 sub.247
  113.4 0.1 sub.250
  113.5 3.2 %fusion.84 = (bf16[3,2048,128]{2,1,0:T(8,128)(2,1)S(1)}, f32[3,2048,128]{2,1,0:T(8,128)S(1)}) fusion(pred[3,2048,128]{2,1,0:T(32,128)(4,1)S(1)} %copy-done.3, f32[3,2048]{1,0:T(4,128)S(1)} %sub.247, bf16[3,2048,128]{2,1,0:T(8,128)(2,1)} %bitcast.250, bf16[3,128,128]{2,1,0:T(8,128)(2,1)S(1)} %bitcast.260), kind=kOutput, calls=%fused_computation.178 | convolution fusion | flops 204472320 | bytes 7200768 | tf_op jit(solution)/shard_map/hqd,hkd->hqk/dot_general | solution.py:167
  116.7 1.1 multiply_convert_fusion
  117.8 0.3 copy-done
  118.1 0.7 convolution_convert_fusion.1
  118.8 0.2 convert_reduce_fusion.1
  119.1 0.4 copy-done.25
  119.5 1.3 collective-permute-start.3
  120.8 4.0 %collective-permute-start.2 = (f32[2,3,1,1,64]{4,1,3,2,0:T(4,128)S(1)}, f32[2,3,1,1,64]{4,1,3,2,0:T(4,128)S(1)}, u32[]{:S(2)}, u32[]{:S(2)}) collective-permute-start(f32[2,3,1,1,64]{4,1,3,2,0:T(4,128)S(1)} %copy-done.24), channel_id=1, source_target_pairs={{0,8},{8,16},{16,24},{24,32},{32,40},{40,48},{48,56},{1,9},{9,17},... | collective-permute-start | bytes 4616 | tf_op jit(solution)/shard_map/ppermute | solution.py:14
  124.8 0.7 convolution_convert_fusion
  125.5 0.2 copy-done.11
  125.7 0.1 copy-done.14
  125.9 0.4 fusion.32
  126.3 0.3 fusion.34
  126.6 0.2 convert_reduce_fusion
  126.9 0.6 copy.288
  127.7 0.2 fusion.23
  127.8 0.2 fusion.25
  128.0 0.3 fusion.36
  128.3 0.3 fusion.38
  128.6 0.6 copy.289
  129.3 0.1 fusion.40
  129.4 0.1 fusion.42
  129.6 0.6 copy.290
  (103 shorter events, 1.5 us)
Async XLA Ops:
  7.2 3.7 %copy-start.6 = (bf16[3,1,2,64,128]{4,3,2,1,0:T(8,128)(2,1)S(1)}, bf16[3,1,2,64,128]{4,3,2,1,0:T(8,128)(2,1)}, u32[]{:S(2)}) copy-start(bf16[3,1,2,64,128]{4,3,2,1,0:T(8,128)(2,1)} %param.34) | copy-start | bytes 294916
  7.2 3.7 %copy-start.5 = (bf16[3,1,2,64,128]{4,3,2,1,0:T(8,128)(2,1)S(1)}, bf16[3,1,2,64,128]{4,3,2,1,0:T(8,128)(2,1)}, u32[]{:S(2)}) copy-start(bf16[3,1,2,64,128]{4,3,2,1,0:T(8,128)(2,1)} %param.32) | copy-start | bytes 294916
  7.2 67.2 %all-gather.2.cloned.1.call-start = ((), (), s32[]{:S(2)}) async-start(), calls=%async_computation | async-start | bytes 6684672 | tf_op jit(solution)/shard_map/all_gather | solution.py:22
  9.1 9.4 %copy-start.23 = (s32[16,2,8]{0,2,1:T(8,128)S(1)}, s32[16,2,8]{0,2,1:T(8,128)}, u32[]{:S(2)}) copy-start(s32[16,2,8]{0,2,1:T(8,128)} %param.35) | copy-start | bytes 3076
  9.1 9.4 %copy-start.27 = (s32[16,2]{0,1:T(2,128)S(1)}, s32[16,2]{0,1:T(2,128)}, u32[]{:S(2)}) copy-start(s32[16,2]{0,1:T(2,128)} %param.36) | copy-start | bytes 388
  9.1 10.0 %copy-start.26 = (s32[3]{0:T(128)S(1)}, s32[3]{0:T(128)}, u32[]{:S(2)}) copy-start(s32[3]{0:T(128)} %param.37) | copy-start | bytes 40
  12.4 19.4 %collective-permute-start.1 = (bf16[4,3,1,1,64,128]{5,4,1,3,2,0:T(8,128)(2,1)}, bf16[4,3,1,1,64,128]{5,4,1,3,2,0:T(8,128)(2,1)S(1)}, u32[]{:S(2)}, u32[]{:S(2)}) collective-permute-start(bf16[4,3,1,1,64,128]{5,4,1,3,2,0:T(8,128)(2,1)} %get-tuple-element.174), channel_id=1, source_target_pairs={{8,0},{16,8},{24,16},{32,24},{40,32},{48,40},{56,48},{9,1},{17,9},... | collective-permute-start | bytes 589832 | tf_op jit(solution)/shard_map/ppermute | solution.py:15
  13.7 18.2 %collective-permute-start = (bf16[4,3,1,1,64,128]{5,4,1,3,2,0:T(8,128)(2,1)S(1)}, bf16[4,3,1,1,64,128]{5,4,1,3,2,0:T(8,128)(2,1)S(1)}, u32[]{:S(2)}, u32[]{:S(2)}) collective-permute-start(bf16[4,3,1,1,64,128]{5,4,1,3,2,0:T(8,128)(2,1)S(1)} %get-tuple-element.173), channel_id=1, source_target_pairs={{0,8},{8,16},{16,24},{24,32},{32,40},{40,48},{48,56},{1,9},{9,17},... | collective-permute-start | bytes 589832 | tf_op jit(solution)/shard_map/ppermute | solution.py:14
  31.8 1.1 copy-start.28
  31.8 1.3 copy-start.30
  31.8 1.1 copy-start.18
  32.9 0.7 copy-start.13
  74.4 6.5 %copy-start.4 = (pred[3,128,2048]{1,2,0:T(32,128)(4,1)S(1)}, pred[3,128,2048]{1,2,0:T(32,128)(4,1)}, u32[]{:S(2)}) copy-start(pred[3,128,2048]{1,2,0:T(32,128)(4,1)} %copy.240) | copy-start | bytes 2359300
  74.4 6.5 %copy-start.7 = (bf16[3,1,2,64,128]{4,3,2,1,0:T(8,128)(2,1)S(1)}, bf16[3,1,2,64,128]{4,3,2,1,0:T(8,128)(2,1)}, u32[]{:S(2)}) copy-start(bf16[3,1,2,64,128]{4,3,2,1,0:T(8,128)(2,1)} %param.31) | copy-start | bytes 294916
  80.9 1.2 copy-start.2
  85.6 2.9 %copy-start.21 = (f32[3,64]{1,0:T(4,128)}, f32[3,64]{1,0:T(4,128)S(1)}, u32[]{:S(2)}) copy-start(f32[3,64]{1,0:T(4,128)S(1)} %get-tuple-element.198) | copy-start | bytes 2308
  85.6 3.1 %copy-start.19 = (f32[3,64]{1,0:T(4,128)}, f32[3,64]{1,0:T(4,128)S(1)}, u32[]{:S(2)}) copy-start(f32[3,64]{1,0:T(4,128)S(1)} %get-tuple-element.197) | copy-start | bytes 2308
  86.2 2.3 %copy-start.10 = (bf16[3,1,4,64,128]{4,3,0,2,1:T(8,128)(2,1)S(1)}, bf16[3,1,4,64,128]{4,3,0,2,1:T(8,128)(2,1)}, u32[]{:S(2)}) copy-start(bf16[3,1,4,64,128]{4,3,0,2,1:T(8,128)(2,1)} %get-tuple-element.171) | copy-start | bytes 589828
  95.4 18.0 %copy-start.3 = (pred[3,2048,128]{2,1,0:T(32,128)(4,1)S(1)}, pred[3,2048,128]{2,1,0:T(32,128)(4,1)}, u32[]{:S(2)}) copy-start(pred[3,2048,128]{2,1,0:T(32,128)(4,1)} %copy.272) | copy-start | bytes 2359300
  113.5 3.2 %copy-start.1 = (bf16[3,16,2,64,128]{4,3,2,1,0:T(8,128)(2,1)S(1)}, bf16[3,16,2,64,128]{4,3,2,1,0:T(8,128)(2,1)}, u32[]{:S(2)}) copy-start(bf16[3,16,2,64,128]{4,3,2,1,0:T(8,128)(2,1)} %get-tuple-element.165) | copy-start | bytes 4718596
  113.5 3.2 %copy-start.8 = (bf16[3,1,2,64,128]{4,3,2,1,0:T(8,128)(2,1)S(1)}, bf16[3,1,2,64,128]{4,3,2,1,0:T(8,128)(2,1)}, u32[]{:S(2)}) copy-start(bf16[3,1,2,64,128]{4,3,2,1,0:T(8,128)(2,1)} %param.33) | copy-start | bytes 294916
  116.7 1.4 %copy-start = (bf16[3,16,2,64,128]{4,3,2,1,0:T(8,128)(2,1)S(1)}, bf16[3,16,2,64,128]{4,3,2,1,0:T(8,128)(2,1)}, u32[]{:S(2)}) copy-start(bf16[3,16,2,64,128]{4,3,2,1,0:T(8,128)(2,1)} %get-tuple-element.166) | copy-start | bytes 4718596
  118.8 0.7 copy-start.25
  118.8 2.0 %copy-start.24 = (f32[2,3,1,1,64]{4,1,3,2,0:T(4,128)S(1)}, f32[2,3,1,1,64]{4,1,3,2,0:T(4,128)}, u32[]{:S(2)}) copy-start(f32[2,3,1,1,64]{4,1,3,2,0:T(4,128)} %get-tuple-element.191) | copy-start | bytes 4612
  119.5 8.1 %collective-permute-start.3 = (f32[2,3,1,1,64]{4,1,3,2,0:T(4,128)S(1)}, f32[2,3,1,1,64]{4,1,3,2,0:T(4,128)S(1)}, u32[]{:S(2)}, u32[]{:S(2)}) collective-permute-start(f32[2,3,1,1,64]{4,1,3,2,0:T(4,128)S(1)} %copy-done.25), channel_id=1, source_target_pairs={{8,0},{16,8},{24,16},{32,24},{40,32},{48,40},{56,48},{9,1},{17,9},... | collective-permute-start | bytes 4616 | tf_op jit(solution)/shard_map/ppermute | solution.py:15
  120.8 6.8 %collective-permute-start.2 = (f32[2,3,1,1,64]{4,1,3,2,0:T(4,128)S(1)}, f32[2,3,1,1,64]{4,1,3,2,0:T(4,128)S(1)}, u32[]{:S(2)}, u32[]{:S(2)}) collective-permute-start(f32[2,3,1,1,64]{4,1,3,2,0:T(4,128)S(1)} %copy-done.24), channel_id=1, source_target_pairs={{0,8},{8,16},{16,24},{24,32},{32,40},{40,48},{48,56},{1,9},{9,17},... | collective-permute-start | bytes 4616 | tf_op jit(solution)/shard_map/ppermute | solution.py:14
  124.8 0.9 copy-start.11
  124.8 1.0 copy-start.14
  124.8 1.1 copy-start.16
  124.8 1.1 copy-start.22
  124.8 1.4 %copy-start.20 = (f32[3,64]{1,0:T(4,128)S(1)}, f32[3,64]{1,0:T(4,128)}, u32[]{:S(2)}) copy-start(f32[3,64]{1,0:T(4,128)} %copy-done.19) | copy-start | bytes 2308
  126.6 1.1 copy-start.12
  126.6 1.1 copy-start.17
  126.6 1.1 copy-start.31
  126.6 1.2 copy-start.29
  126.6 1.4 %copy-start.9 = (bf16[3,1,4,64,128]{4,3,0,2,1:T(8,128)(2,1)S(1)}, bf16[3,1,4,64,128]{4,3,0,2,1:T(8,128)(2,1)}, u32[]{:S(2)}) copy-start(bf16[3,1,4,64,128]{4,3,0,2,1:T(8,128)(2,1)} %get-tuple-element.169) | copy-start | bytes 589828
  126.6 1.4 %copy-start.15 = (bf16[3,1,2,64,128]{4,3,0,2,1:T(8,128)(2,1)S(1)}, bf16[3,1,2,64,128]{4,3,0,2,1:T(8,128)(2,1)}, u32[]{:S(2)}) copy-start(bf16[3,1,2,64,128]{4,3,0,2,1:T(8,128)(2,1)} %get-tuple-element.212) | copy-start | bytes 294916
Sparse Core Ops, SparseCore 0:
  10.7 63.6 all-gather.1
where the time goes:
time: 138 us; the launch traced here: 137 us
  waiting for transfers between devices  40.7 us (29%)
  local copies, waits for them, and re-layouts  32.2 us (23%)
  blocking collectives  16.7 us (12%)
  matrix products  15.1 us (11%)
  between operations  14.8 us (11%)
  starting transfers between devices  11.4 us (8%)
  other arithmetic  6.3 us (5%)
    all_gather x1, waiting for transfers between devices, in_one_piece(): result, at, outs = (lax.all_gather(both, axis, axis=dim, tiled=True), 0, [])  40.7 us
    all_gather x1, blocking collectives, on_device(): lax.all_gather(jnp.stack((log_sum, delta)), 'hb', axis=2, tiled=True)  16.7 us
    ppermute x2, starting transfers between devices, with_halo(): before = lax.ppermute(last, axis, up)  8.76 us
    slice x1, local copies, waits for them, and re-layouts, in_one_piece(): outs.append(lax.slice_in_dim(result, at, at + a.shape[along], axis=along))  6.5 us
    broadcast_in_dim x3, local copies, waits for them, and re-layouts, on_device(): jnp.where(allowed_own[:, :, None, :, None], scores.reshape(shaped), -jnp....  6.18 us
    broadcast_in_dim x3, local copies, waits for them, and re-layouts, on_device(): jnp.where(allowed_cols[:, :, None, :, None], jnp.exp(reverse.reshape(rev_...  6.15 us
    unnamed x70, local copies, waits for them, and re-layouts  4.94 us
    dot_general x1, matrix products, on_device(): jnp.einsum('hqk,hkd->hqd', score_grad, key_flat, preferred_element_type=j...  3.8 us
  transfers between devices with their start and end apart: 5, of which 1 were waited for; matrix products, arithmetic and copies ran while one was open for 15% of the time, Pallas kernels for 0%

commit v1 on v0

v1 whole, which is shorter than its diff:
```python
import functools

import jax
import jax.numpy as jnp
from jax import lax
from jax.experimental import pallas as pl
from jax.experimental.pallas import tpu as pltpu
from jax.sharding import PartitionSpec as P

CLOSED = -1e30
STAT_ROWS = 16
NT = (((1,), (1,)), ((), ()))
NN = (((1,), (0,)), ((), ()))


def dot(a, b, dims):
    return lax.dot_general(a, b, dims, preferred_element_type=jnp.float32)


def three_terms(x):
    high = x.astype(jnp.bfloat16).astype(jnp.float32)
    rest = x - high
    mid = rest.astype(jnp.bfloat16).astype(jnp.float32)
    return [high, mid, rest - mid]


def as_row(col):
    n = col.shape[0]
    return jnp.transpose(jnp.broadcast_to(col, (n, n)))[0:1]


def query_side(
    edge_ref, keys_ref, values_ref, q_ref, g_ref, left_ref, right_ref, bias_ref,
    dq_ref, sent_ref, stats_ref, *, factor, tile
):
    head = pl.program_id(0)
    rows, dim = q_ref.shape[1:]
    keys = keys_ref[:, 0, 0].reshape(-1, dim)
    values = values_ref[:, 0, 0].reshape(-1, dim)
    q = q_ref[0]
    g = g_ref[0]
    shaped = (rows // tile, tile, keys.shape[0])
    scores = dot(q, keys, NT) * factor
    scores = (scores.reshape(shaped) + bias_ref[0][:, None, :]).reshape(rows, -1)
    edge_keys = (left_ref[0, 0], right_ref[0, 0])
    edge_values = (left_ref[1, 0], right_ref[1, 0])
    edge_q = (q[:tile], q[rows - tile:])
    edge_g = (g[:tile], g[rows - tile:])
    edge_scores = [
        dot(edge_q[i], edge_keys[i], NT) * factor + edge_ref[head, i] for i in range(2)
    ]
    inner = rows - 2 * tile

    def spread(parts, fill):
        mid = [jnp.full((inner, 1), fill, jnp.float32)] if inner else []
        return jnp.concatenate([parts[0]] + mid + [parts[1]], axis=0)

    def own(x, i):
        return x[:tile] if i == 0 else x[rows - tile:]

    edge_top = spread([jnp.max(e, axis=1, keepdims=True) for e in edge_scores], CLOSED)
    top = jnp.maximum(jnp.max(scores, axis=1, keepdims=True), edge_top)
    powers = jnp.exp(scores - top)
    edge_powers = [jnp.exp(edge_scores[i] - own(top, i)) for i in range(2)]
    total = jnp.sum(powers, axis=1, keepdims=True) + spread(
        [jnp.sum(e, axis=1, keepdims=True) for e in edge_powers], 0.0
    )
    scale = 1.0 / total
    probs = powers * scale
    edge_probs = [edge_powers[i] * own(scale, i) for i in range(2)]
    slopes = dot(g, values, NT)
    edge_slopes = [dot(edge_g[i], edge_values[i], NT) for i in range(2)]

    def half(x):
        return x.astype(jnp.bfloat16).astype(jnp.float32)

    delta = jnp.sum(half(probs) * slopes, axis=1, keepdims=True) + spread(
        [
            jnp.sum(half(edge_probs[i]) * edge_slopes[i], axis=1, keepdims=True)
            for i in range(2)
        ],
        0.0,
    )
    grad = (probs * (slopes - delta) * factor).astype(jnp.bfloat16)
    dq = dot(grad, keys, NN)
    edge_dq = []
    for i in range(2):
        part = edge_probs[i] * (edge_slopes[i] - own(delta, i)) * factor
        edge_dq.append(dot(part.astype(jnp.bfloat16), edge_keys[i], NN))
    dq_ref[0, :tile] = (dq[:tile] + edge_dq[0]).astype(jnp.bfloat16)
    if inner:
        dq_ref[0, tile:rows - tile] = dq[tile:rows - tile].astype(jnp.bfloat16)
    dq_ref[0, rows - tile:] = (dq[rows - tile:] + edge_dq[1]).astype(jnp.bfloat16)
    log_row = as_row(top + jnp.log(total))
    delta_row = as_row(delta)
    pieces = three_terms(log_row) + three_terms(delta_row)
    blank = jnp.zeros((STAT_ROWS - len(pieces), rows), jnp.float32)
    sent_ref[0, :rows] = g
    sent_ref[0, rows:] = jnp.concatenate(pieces + [blank], axis=0).astype(jnp.bfloat16)
    stats_ref[0] = jnp.concatenate(
        [log_row, delta_row, jnp.zeros((6, rows), jnp.float32)], axis=0
    )


def key_side(
    edge_ref, queries_ref, sent_ref, k_ref, v_ref, left_ref, right_ref,
    left_stats_ref, right_stats_ref, bias_ref, dk_ref, dv_ref, *, factor, tile
):
    head = pl.program_id(0)
    rows, dim = k_ref.shape[1:]
    bands = queries_ref.shape[0]
    queries = queries_ref[:, 0, 0].reshape(-1, dim)
    cotan = sent_ref[:, 0, :rows].reshape(-1, dim)
    k = k_ref[0]
    v = v_ref[0]
    terms = sent_ref[:, 0, rows:].astype(jnp.float32)
    log_sum = terms[:, 0] + terms[:, 1] + terms[:, 2]
    delta = terms[:, 3] + terms[:, 4] + terms[:, 5]
    scores = dot(k, queries, NT)
    slopes = dot(v, cotan, NT)
    grads, probs = [], []
    tiles = rows // tile
    for r in range(bands):
        at = slice(r * rows, (r + 1) * rows)
        offset = bias_ref[0][:, at] - log_sum[r:r + 1]
        part = (scores[:, at] * factor).reshape(tiles, tile, rows) + offset[:, None, :]
        prob = jnp.exp(part).reshape(rows, rows)
        probs.append(prob.astype(jnp.bfloat16))
        grads.append((prob * (slopes[:, at] - delta[r:r + 1]) * factor).astype(jnp.bfloat16))
    dk = dot(jnp.concatenate(grads, axis=1), queries, NN)
    dv = dot(jnp.concatenate(probs, axis=1), cotan, NN)
    edge_k = (k[:tile], k[rows - tile:])
    edge_v = (v[:tile], v[rows - tile:])
    edge_stats = (left_stats_ref[0][:, rows - tile:], right_stats_ref[0][:, :tile])
    halos = (left_ref, right_ref)
    edge_dk, edge_dv = [], []
    for i in range(2):
        q_edge = halos[i][2, 0]
        g_edge = halos[i][3, 0]
        stats = edge_stats[i]
        part = dot(edge_k[i], q_edge, NT) * factor + (edge_ref[head, i] - stats[0:1])
        prob = jnp.exp(part)
        grad = prob * (dot(edge_v[i], g_edge, NT) - stats[1:2]) * factor
        edge_dk.append(dot(grad.astype(jnp.bfloat16), q_edge, NN))
        edge_dv.append(dot(prob.astype(jnp.bfloat16), g_edge, NN))
    for ref, whole, edge in ((dk_ref, dk, edge_dk), (dv_ref, dv, edge_dv)):
        ref[0, :tile] = (whole[:tile] + edge[0]).astype(jnp.bfloat16)
        if rows > 2 * tile:
            ref[0, tile:rows - tile] = whole[tile:rows - tile].astype(jnp.bfloat16)
        ref[0, rows - tile:] = (whole[rows - tile:] + edge[1]).astype(jnp.bfloat16)


def tile_masks(tile_radius, sel_tiles, sel_count):
    band_rows, band_cols, picks = sel_tiles.shape
    tile_total = band_rows * band_cols
    tile_index = jnp.arange(tile_total, dtype=jnp.int32)
    row_of = tile_index // band_cols
    col_of = tile_index % band_cols
    spread = jnp.abs(row_of[:, None] - row_of[None, :]) + jnp.abs(col_of[:, None] - col_of[None, :])
    nearby = spread[None] <= tile_radius[:, None, None]
    live_pick = jnp.arange(picks, dtype=jnp.int32)[None, :] < sel_count.reshape(tile_total, 1)
    matches = (sel_tiles.reshape(tile_total, picks, 1) == tile_index[None, None, :]) & live_pick[
        :, :, None
    ]
    return nearby | jnp.any(matches, axis=1)[None]


def neighbours(first, last, axis):
    size = lax.axis_size(axis)
    up = [(i, i + 1) for i in range(size - 1)]
    down = [(i + 1, i) for i in range(size - 1)]
    return lax.ppermute(last, axis, up), lax.ppermute(first, axis, down)


def row_bias(allowed, tile):
    bias = jnp.where(allowed, 0.0, CLOSED).astype(jnp.float32)
    heads, own, others = bias.shape
    wide = jnp.broadcast_to(bias[..., None], (heads, own, others, tile))
    return wide.reshape(heads, own, others * tile)


def on_device(query_rows, key_rows, value_rows, grad_out, sel_tiles, sel_count, tile_radius):
    heads, tile_rows, tile_cols, tile, dim = query_rows.shape
    dev_tiles = tile_rows * tile_cols
    rows = dev_tiles * tile
    factor = dim ** (-0.5)
    hb_index = lax.axis_index("hb")
    wb_index = lax.axis_index("wb")
    bands = lax.axis_size("hb")
    flat = (heads, rows, dim)
    q, k, v, g = (x.reshape(flat) for x in (query_rows, key_rows, value_rows, grad_out))
    kv = lax.all_gather(jnp.stack((k, v)), "hb")
    all_q = lax.all_gather(q[None], "hb")
    four = (k, v, q, g)
    left, right = neighbours(
        jnp.stack([x[:, :tile] for x in four]), jnp.stack([x[:, rows - tile:] for x in four]), "wb"
    )
    allowed = tile_masks(tile_radius, sel_tiles, sel_count)
    start = hb_index * dev_tiles
    own_bias = row_bias(lax.dynamic_slice_in_dim(allowed, start, dev_tiles, 1), tile)
    col_bias = row_bias(
        jnp.swapaxes(lax.dynamic_slice_in_dim(allowed, start, dev_tiles, 2), 1, 2), tile
    )
    reach = tile_radius >= 1
    edge_open = jnp.stack(
        (reach & (wb_index >= 1), reach & (wb_index < lax.axis_size("wb") - 1)), axis=1
    )
    edge_bias = jnp.where(edge_open, 0.0, CLOSED).astype(jnp.float32)

    def per_head(shape):
        return pl.BlockSpec((1,) + shape, lambda h: (h,) + (0,) * len(shape))

    smem = pl.BlockSpec(memory_space=pltpu.SMEM)
    own = per_head((rows, dim))
    halo = pl.BlockSpec((4, 1, tile, dim), lambda h: (0, h, 0, 0))
    bias = per_head((dev_tiles, bands * rows))
    stat = per_head((8, rows))
    sent_shape = (rows + STAT_ROWS, dim)
    half = functools.partial(jax.ShapeDtypeStruct, dtype=jnp.bfloat16)
    dq, sent, stats = pl.pallas_call(
        functools.partial(query_side, factor=factor, tile=tile),
        grid=(heads,),
        in_specs=[
            smem,
            pl.BlockSpec((bands, 1, 1, rows, dim), lambda h: (0, 0, h, 0, 0)),
            pl.BlockSpec((bands, 1, 1, rows, dim), lambda h: (0, 1, h, 0, 0)),
            own, own, halo, halo, bias,
        ],
        out_specs=[own, per_head(sent_shape), stat],
        out_shape=[
            half(flat), half((heads,) + sent_shape),
            jax.ShapeDtypeStruct((heads, 8, rows), jnp.float32),
        ],
        name="query_side",
    )(edge_bias, kv, kv, q, g, left, right, own_bias)
    all_sent = lax.all_gather(sent, "hb")
    left_stats, right_stats = neighbours(stats, stats, "wb")
    dk, dv = pl.pallas_call(
        functools.partial(key_side, factor=factor, tile=tile),
        grid=(heads,),
        in_specs=[
            smem,
            pl.BlockSpec((bands, 1, 1, rows, dim), lambda h: (0, 0, h, 0, 0)),
            pl.BlockSpec((bands, 1) + sent_shape, lambda h: (0, h, 0, 0)),
            own, own, halo, halo, stat, stat, bias,
        ],
        out_specs=[own, own],
        out_shape=[half(flat), half(flat)],
        name="key_side",
    )(edge_bias, all_q, all_sent, k, v, left, right, left_stats, right_stats, col_bias)
    return tuple(x.reshape(query_rows.shape) for x in (dq, dk, dv))


def solution(mesh):
    banded = P("hd", "hb", "wb", None, None)
    return jax.shard_map(
        on_device,
        mesh=mesh,
        in_specs=(banded,) * 4 + (P(None, "wb", None), P(None, "wb"), P("hd")),
        out_specs=(banded,) * 3,
        check_vma=False,
    )
```

time: 138 us -> 174 us (1.26)
  waiting for transfers between devices: 40.7 us -> 130 us
  local copies, waits for them, and re-layouts: 32.2 us -> 4.84 us
  blocking collectives: 16.7 us -> 0 us
  matrix products: 15.1 us -> 0 us
  Pallas kernels: 0 us -> 11.3 us
  other arithmetic: 6.3 us -> 2.88 us
    all_gather x1 -> x3, waiting for transfers between devices: 40.7 us -> 127 us  [the longest x1 46.6 us: on_device(): all_sent = lax.all_gather(sent, 'hb')]
    all_gather x1 -> x0, blocking collectives: 16.7 us -> none  [on_device(): lax.all_gather(jnp.stack((log_sum, delta)), 'hb', axis=2, tiled=True)]
    dot_general x19 -> x0, matrix products: 15.1 us -> none  [the longest x1 3.8 us: on_device(): jnp.einsum('hqk,hkd->hqd', score_grad, key_flat, preferred_element_type=j...]
    broadcast_in_dim x6 -> x2, local copies, waits for them, and re-layouts: 12.3 us -> 0.17 us  [row_bias(): wide = jnp.broadcast_to(bias[..., None], (heads, own, others, tile))]
    pallas_call x0 -> x2, Pallas kernels: none -> 11.3 us  [the longest x1 6 us: on_device(): pl.pallas_call(functools.partial(query_side, factor=factor, tile=tile), g...]
    slice x5 -> x0, local copies, waits for them, and re-layouts: 7.29 us -> none  [the longest x1 6.5 us: in_one_piece(): outs.append(lax.slice_in_dim(result, at, at + a.shape[along], axis=along))]
    unnamed x70 -> x16, local copies, waits for them, and re-layouts: 4.94 us -> 0.19 us
    sub x10 -> x0, local copies, waits for them, and re-layouts: 2.81 us -> none  [the longest x1 1.29 us: on_device(): slopes - delta.reshape(head_count, dev_rows, 1)]
  transfers between devices with their start and end apart: 5 -> 7, of which waited for: 1 -> 4; matrix products, arithmetic and copies ran while one was open for 15% -> 3% of each run, Pallas kernels for 0% -> 3%
where the time goes in v1:
time: 174 us; the launch traced here: 173 us
  waiting for transfers between devices  130 us (75%)
  between operations  13.9 us (8%)
  Pallas kernels  11.3 us (6%)
  starting transfers between devices  9.97 us (6%)
  local copies, waits for them, and re-layouts  4.84 us (3%)
  other arithmetic  2.88 us (2%)
    all_gather x1, waiting for transfers between devices, on_device(): all_sent = lax.all_gather(sent, 'hb')  46.6 us
    all_gather x1, waiting for transfers between devices, on_device(): kv = lax.all_gather(jnp.stack((k, v)), 'hb')  45.9 us
    all_gather x1, waiting for transfers between devices, on_device(): all_q = lax.all_gather(q[None], 'hb')  34.8 us
    ppermute x4, starting transfers between devices, neighbours(): return (lax.ppermute(last, axis, up), lax.ppermute(first, axis, down))  9.85 us
    pallas_call x1, Pallas kernels, on_device(): pl.pallas_call(functools.partial(query_side, factor=factor, tile=tile), g...  6 us
    pallas_call x1, Pallas kernels, on_device(): pl.pallas_call(functools.partial(key_side, factor=factor, tile=tile), gri...  5.27 us
  transfers between devices with their start and end apart: 7, of which 4 were waited for; matrix products, arithmetic and copies ran while one was open for 3% of the time, Pallas kernels for 3%

profile of v1, /device:TPU:1, one launch (start us, length us, event | category | flops | bytes accessed | tf_op | source)
XLA Modules:
  0.0 173.4 jit_solution(11209078349610058235)
XLA Ops:
  7.2 0.0 copy-start.5
  7.2 0.0 copy-start.4
  7.2 0.0 copy-start.6
  7.2 0.0 all-gather.8.cloned.1.call-start
  7.2 1.7 pad_maximum_fusion
  8.9 0.0 all-gather.8.cloned.1.call-update
  8.9 0.0 all-gather.6.cloned.1.call-start
  9.0 0.7 all-gather.6.cloned.1.call-update
  9.7 0.0 all-gather.10.cloned.1.call-start
  9.7 0.8 slice_bitcast_fusion
  10.6 0.8 slice_bitcast_fusion.1
  11.4 0.9 slice_bitcast_fusion.2
  12.3 4.1 %collective-permute-start = (bf16[4,3,64,128]{3,2,1,0:T(8,128)(2,1)S(1)}, bf16[4,3,64,128]{3,2,1,0:T(8,128)(2,1)S(1)}, u32[]{:S(2)}, u32[]{:S(2)}) collective-permute-start(bf16[4,3,64,128]{3,2,1,0:T(8,128)(2,1)S(1)} %pad_maximum_fusion.1), channel_id=1, source_target_pairs={{0,8},{8,16},{16,24},{24,32},{32,40},{40,48},{48,56},{1,9},{9,17},... | collective-permute-start | bytes 589832 | tf_op jit(solution)/shard_map/ppermute | solution.py:172
  16.5 1.3 collective-permute-start.1
  17.8 0.0 copy-done.5
  17.8 0.1 copy.34
  17.9 0.1 copy.33
  18.1 0.0 copy-done.4
  18.1 0.1 copy.35
  18.1 0.0 copy-done.6
  18.1 0.1 copy.36
  18.2 0.1 lt.35
  18.3 0.1 iota_compare_fusion.1
  18.4 0.2 fusion.1
  18.6 0.1 copy.37
  18.6 0.1 abs_add_fusion
  18.7 0.1 compare_or_fusion
  18.8 0.1 dynamic-slice_select_fusion
  18.9 0.1 copy.38
  19.0 0.1 broadcast_in_dim.48
  19.1 0.7 reshape.169.bias_ref
  19.8 0.7 add_select_fusion.edge_ref
  20.5 0.0 collective-permute-done.left_ref
  20.5 0.0 copy-start
  20.5 2.4 %collective-permute-done.1.right_ref = bf16[4,3,64,128]{3,2,1,0:T(8,128)(2,1)S(1)} collective-permute-done((bf16[4,3,64,128]{3,2,1,0:T(8,128)(2,1)S(1)}, bf16[4,3,64,128]{3,2,1,0:T(8,128)(2,1)S(1)}, u32[]{:S(2)}, u32[]{:S(2)}) %collective-permute-start.1) | collective-permute-done | bytes 196640 | tf_op jit(solution)/shard_map/ppermute | solution.py:172
  22.9 0.0 copy-start.1
  22.9 45.9 %all-gather.8.cloned.1.call-done = bf16[32,3,128,128]{3,2,1,0:T(8,128)(2,1)} async-done(((bf16[2,3,128,128]{3,2,1,0:T(8,128)(2,1)}), bf16[32,3,128,128]{3,2,1,0:T(8,128)(2,1)}) %all-gather.8.cloned.1.call-update) | async-done | bytes 3145744 | tf_op jit(solution)/shard_map/all_gather | solution.py:192
  68.8 0.0 copy-done
  68.8 0.0 copy-done.1
  68.8 6.0 %query_side.1 = (bf16[3,128,128]{2,1,0:T(8,128)(2,1)}, bf16[3,144,128]{2,1,0:T(8,128)(2,1)}, f32[3,8,128]{2,1,0:T(8,128)}) custom-call(f32[3,2]{1,0:T(4,128)} %add_select_fusion.edge_ref, bf16[16,2,3,128,128]{4,3,2,1,0:T(8,128)(2,1)} %bitcast.45, bf16[16,2,3,128,128]{4,3,2,1,0:T(8,128)(2,1)} %bitcast.46, bf16[3,128,128]{2,1,0:T(8,128)(2,1)} %bitcast.50, ...), custom_call_target="tpu_custom_call" | custom-call | tf_op jit(solution)/shard_map/query_side/pallas_call | solution.py:220
  74.8 0.0 all-gather.10.cloned.1.call-update
  74.9 3.1 %collective-permute-start.2 = (f32[3,8,128]{2,1,0:T(8,128)}, f32[3,8,128]{2,1,0:T(8,128)S(1)}, u32[]{:S(2)}, u32[]{:S(2)}) collective-permute-start(f32[3,8,128]{2,1,0:T(8,128)} %get-tuple-element.10), channel_id=1, source_target_pairs={{0,8},{8,16},{16,24},{24,32},{32,40},{40,48},{48,56},{1,9},{9,17},... | collective-permute-start | bytes 36872 | tf_op jit(solution)/shard_map/ppermute | solution.py:172
  78.0 1.3 collective-permute-start.3
  79.3 0.1 broadcast_in_dim.51
  79.4 0.7 reshape.171.bias_ref
  80.1 34.8 %all-gather.6.cloned.1.call-done.queries_ref = bf16[16,1,3,128,128]{4,3,2,1,0:T(8,128)(2,1)} async-done(((bf16[1,1,3,128,128]{4,3,2,1,0:T(8,128)(2,1)}), bf16[16,1,3,128,128]{4,3,2,1,0:T(8,128)(2,1)}) %all-gather.6.cloned.1.call-update) | async-done | bytes 1572880 | tf_op jit(solution)/shard_map/all_gather | solution.py:193
  115.0 0.0 collective-permute-done.2.left_stats_ref
  115.0 0.0 copy-start.2
  115.0 0.0 collective-permute-done.3.right_stats_ref
  115.0 0.0 copy-start.3
  115.0 46.6 %all-gather.10.cloned.1.call-done = bf16[48,144,128]{2,1,0:T(8,128)(2,1)} async-done(((bf16[3,144,128]{2,1,0:T(8,128)(2,1)}), bf16[48,144,128]{2,1,0:T(8,128)(2,1)}) %all-gather.10.cloned.1.call-update) | async-done | bytes 1769488 | tf_op jit(solution)/shard_map/all_gather | solution.py:236
  161.6 0.0 copy-done.2
  161.6 0.0 copy-done.3
  161.6 5.3 %key_side.1 = (bf16[3,128,128]{2,1,0:T(8,128)(2,1)}, bf16[3,128,128]{2,1,0:T(8,128)(2,1)}) custom-call(f32[3,2]{1,0:T(4,128)} %add_select_fusion.edge_ref, bf16[16,1,3,128,128]{4,3,2,1,0:T(8,128)(2,1)} %all-gather.6.cloned.1.call-done.queries_ref, bf16[16,3,144,128]{3,2,1,0:T(8,128)(2,1)} %bitcast.47, bf16[3,128,128]{2,1,0:T(8,128)(2,1)} %bitcast.56, ...), custom_call_target="tpu_custom_call" | custom-call | tf_op jit(solution)/shard_map/key_side/pallas_call | solution.py:238
  (5 shorter events, 0.1 us)
Async XLA Ops:
  7.2 10.6 %copy-start.5 = (s32[3]{0:T(128)S(1)}, s32[3]{0:T(128)}, u32[]{:S(2)}) copy-start(s32[3]{0:T(128)} %param.13) | copy-start | bytes 40
  7.2 10.9 %copy-start.4 = (s32[16,2,8]{0,2,1:T(8,128)S(1)}, s32[16,2,8]{0,2,1:T(8,128)}, u32[]{:S(2)}) copy-start(s32[16,2,8]{0,2,1:T(8,128)} %param.11) | copy-start | bytes 3076
  7.2 10.9 %copy-start.6 = (s32[16,2]{0,1:T(2,128)S(1)}, s32[16,2]{0,1:T(2,128)}, u32[]{:S(2)}) copy-start(s32[16,2]{0,1:T(2,128)} %param.12) | copy-start | bytes 388
  7.2 61.6 %all-gather.8.cloned.1.call-start = ((), (), s32[]{:S(2)}) async-start(), calls=%async_computation.1 | async-start | bytes 3342336 | tf_op jit(solution)/shard_map/all_gather | solution.py:192
  8.9 106.0 %all-gather.6.cloned.1.call-start = ((), (), s32[]{:S(2)}) async-start(), calls=%async_computation | async-start | bytes 1671168 | tf_op jit(solution)/shard_map/all_gather | solution.py:193
  9.7 151.9 %all-gather.10.cloned.1.call-start = ((), (), s32[]{:S(2)}) async-start(), calls=%async_computation.2 | async-start | bytes 1880064 | tf_op jit(solution)/shard_map/all_gather | solution.py:236
  12.3 8.2 %collective-permute-start = (bf16[4,3,64,128]{3,2,1,0:T(8,128)(2,1)S(1)}, bf16[4,3,64,128]{3,2,1,0:T(8,128)(2,1)S(1)}, u32[]{:S(2)}, u32[]{:S(2)}) collective-permute-start(bf16[4,3,64,128]{3,2,1,0:T(8,128)(2,1)S(1)} %pad_maximum_fusion.1), channel_id=1, source_target_pairs={{0,8},{8,16},{16,24},{24,32},{32,40},{40,48},{48,56},{1,9},{9,17},... | collective-permute-start | bytes 589832 | tf_op jit(solution)/shard_map/ppermute | solution.py:172
  16.5 6.4 %collective-permute-start.1 = (bf16[4,3,64,128]{3,2,1,0:T(8,128)(2,1)S(1)}, bf16[4,3,64,128]{3,2,1,0:T(8,128)(2,1)S(1)}, u32[]{:S(2)}, u32[]{:S(2)}) collective-permute-start(bf16[4,3,64,128]{3,2,1,0:T(8,128)(2,1)S(1)} %pad_maximum_fusion.2), channel_id=1, source_target_pairs={{8,0},{16,8},{24,16},{32,24},{40,32},{48,40},{56,48},{9,1},{17,9},... | collective-permute-start | bytes 589832 | tf_op jit(solution)/shard_map/ppermute | solution.py:172
  20.5 48.3 %copy-start = (bf16[4,3,64,128]{3,2,1,0:T(8,128)(2,1)}, bf16[4,3,64,128]{3,2,1,0:T(8,128)(2,1)S(1)}, u32[]{:S(2)}) copy-start(bf16[4,3,64,128]{3,2,1,0:T(8,128)(2,1)S(1)} %collective-permute-done.left_ref) | copy-start | bytes 589828
  22.9 45.9 %copy-start.1 = (bf16[4,3,64,128]{3,2,1,0:T(8,128)(2,1)}, bf16[4,3,64,128]{3,2,1,0:T(8,128)(2,1)S(1)}, u32[]{:S(2)}) copy-start(bf16[4,3,64,128]{3,2,1,0:T(8,128)(2,1)S(1)} %collective-permute-done.1.right_ref) | copy-start | bytes 589828
  74.9 40.1 %collective-permute-start.2 = (f32[3,8,128]{2,1,0:T(8,128)}, f32[3,8,128]{2,1,0:T(8,128)S(1)}, u32[]{:S(2)}, u32[]{:S(2)}) collective-permute-start(f32[3,8,128]{2,1,0:T(8,128)} %get-tuple-element.10), channel_id=1, source_target_pairs={{0,8},{8,16},{16,24},{24,32},{32,40},{40,48},{48,56},{1,9},{9,17},... | collective-permute-start | bytes 36872 | tf_op jit(solution)/shard_map/ppermute | solution.py:172
  78.0 37.0 %collective-permute-start.3 = (f32[3,8,128]{2,1,0:T(8,128)}, f32[3,8,128]{2,1,0:T(8,128)S(1)}, u32[]{:S(2)}, u32[]{:S(2)}) collective-permute-start(f32[3,8,128]{2,1,0:T(8,128)} %get-tuple-element.10), channel_id=1, source_target_pairs={{8,0},{16,8},{24,16},{32,24},{40,32},{48,40},{56,48},{9,1},{17,9},... | collective-permute-start | bytes 36872 | tf_op jit(solution)/shard_map/ppermute | solution.py:172
  115.0 46.6 %copy-start.2 = (f32[3,8,128]{2,1,0:T(8,128)}, f32[3,8,128]{2,1,0:T(8,128)S(1)}, u32[]{:S(2)}) copy-start(f32[3,8,128]{2,1,0:T(8,128)S(1)} %collective-permute-done.2.left_stats_ref) | copy-start | bytes 36868
  115.0 46.6 %copy-start.3 = (f32[3,8,128]{2,1,0:T(8,128)}, f32[3,8,128]{2,1,0:T(8,128)S(1)}, u32[]{:S(2)}) copy-start(f32[3,8,128]{2,1,0:T(8,128)S(1)} %collective-permute-done.3.right_stats_ref) | copy-start | bytes 36868
Sparse Core Ops, SparseCore 0:
  10.7 58.0 all-gather.7
  71.5 43.3 all-gather.5
  117.7 43.8 all-gather.9

commit v2 on v1

--- a/solution.py
+++ b/solution.py
@@ -8,20 +8,12 @@
 from jax.sharding import PartitionSpec as P
 
 CLOSED = -1e30
-STAT_ROWS = 16
 NT = (((1,), (1,)), ((), ()))
 NN = (((1,), (0,)), ((), ()))
 
 
 def dot(a, b, dims):
     return lax.dot_general(a, b, dims, preferred_element_type=jnp.float32)
-
-
-def three_terms(x):
-    high = x.astype(jnp.bfloat16).astype(jnp.float32)
-    rest = x - high
-    mid = rest.astype(jnp.bfloat16).astype(jnp.float32)
-    return [high, mid, rest - mid]
 
 
 def as_row(col):
@@ -31,7 +23,7 @@
 
 def query_side(
     edge_ref, keys_ref, values_ref, q_ref, g_ref, left_ref, right_ref, bias_ref,
-    dq_ref, sent_ref, stats_ref, *, factor, tile
+    dq_ref, stats_ref, *, factor, tile
 ):
     head = pl.program_id(0)
     rows, dim = q_ref.shape[1:]
@@ -91,42 +83,32 @@
     if inner:
         dq_ref[0, tile:rows - tile] = dq[tile:rows - tile].astype(jnp.bfloat16)
     dq_ref[0, rows - tile:] = (dq[rows - tile:] + edge_dq[1]).astype(jnp.bfloat16)
-    log_row = as_row(top + jnp.log(total))
-    delta_row = as_row(delta)
-    pieces = three_terms(log_row) + three_terms(delta_row)
-    blank = jnp.zeros((STAT_ROWS - len(pieces), rows), jnp.float32)
-    sent_ref[0, :rows] = g
-    sent_ref[0, rows:] = jnp.concatenate(pieces + [blank], axis=0).astype(jnp.bfloat16)
-    stats_ref[0] = jnp.concatenate(
-        [log_row, delta_row, jnp.zeros((6, rows), jnp.float32)], axis=0
-    )
+    stats_ref[0, 0:1] = as_row(top + jnp.log(total))
+    stats_ref[0, 1:2] = as_row(delta)
 
 
 def key_side(
-    edge_ref, queries_ref, sent_ref, k_ref, v_ref, left_ref, right_ref,
+    edge_ref, queries_ref, cotan_ref, all_stats_ref, k_ref, v_ref, left_ref, right_ref,
     left_stats_ref, right_stats_ref, bias_ref, dk_ref, dv_ref, *, factor, tile
 ):
     head = pl.program_id(0)
     rows, dim = k_ref.shape[1:]
     bands = queries_ref.shape[0]
     queries = queries_ref[:, 0, 0].reshape(-1, dim)
-    cotan = sent_ref[:, 0, :rows].reshape(-1, dim)
+    cotan = cotan_ref[:, 0, 0].reshape(-1, dim)
     k = k_ref[0]
     v = v_ref[0]
-    terms = sent_ref[:, 0, rows:].astype(jnp.float32)
-    log_sum = terms[:, 0] + terms[:, 1] + terms[:, 2]
-    delta = terms[:, 3] + terms[:, 4] + terms[:, 5]
     scores = dot(k, queries, NT)
     slopes = dot(v, cotan, NT)
     grads, probs = [], []
     tiles = rows // tile
     for r in range(bands):
         at = slice(r * rows, (r + 1) * rows)
-        offset = bias_ref[0][:, at] - log_sum[r:r + 1]
+        offset = bias_ref[0][:, at] - all_stats_ref[r, 0, 0:1]
         part = (scores[:, at] * factor).reshape(tiles, tile, rows) + offset[:, None, :]
         prob = jnp.exp(part).reshape(rows, rows)
         probs.append(prob.astype(jnp.bfloat16))
-        grads.append((prob * (slopes[:, at] - delta[r:r + 1]) * factor).astype(jnp.bfloat16))
+        grads.append((prob * (slopes[:, at] - all_stats_ref[r, 0, 1:2]) * factor).astype(jnp.bfloat16))
     dk = dot(jnp.concatenate(grads, axis=1), queries, NN)
     dv = dot(jnp.concatenate(probs, axis=1), cotan, NN)
     edge_k = (k[:tile], k[rows - tile:])
@@ -189,9 +171,8 @@
     bands = lax.axis_size("hb")
     flat = (heads, rows, dim)
     q, k, v, g = (x.reshape(flat) for x in (query_rows, key_rows, value_rows, grad_out))
-    kv = lax.all_gather(jnp.stack((k, v)), "hb")
-    all_q = lax.all_gather(q[None], "hb")
     four = (k, v, q, g)
+    band = lax.all_gather(jnp.stack(four), "hb")
     left, right = neighbours(
         jnp.stack([x[:, :tile] for x in four]), jnp.stack([x[:, rows - tile:] for x in four]), "wb"
     )
@@ -214,40 +195,38 @@
     own = per_head((rows, dim))
     halo = pl.BlockSpec((4, 1, tile, dim), lambda h: (0, h, 0, 0))
     bias = per_head((dev_tiles, bands * rows))
-    stat = per_head((8, rows))
-    sent_shape = (rows + STAT_ROWS, dim)
+    stat = per_head((2, rows))
+
+    def of_band(slot):
+        return pl.BlockSpec((bands, 1, 1, rows, dim), lambda h: (0, slot, h, 0, 0))
+
     half = functools.partial(jax.ShapeDtypeStruct, dtype=jnp.bfloat16)
-    dq, sent, stats = pl.pallas_call(
+    dq, stats = pl.pallas_call(
         functools.partial(query_side, factor=factor, tile=tile),
         grid=(heads,),
         in_specs=[
             smem,
-            pl.BlockSpec((bands, 1, 1, rows, dim), lambda h: (0, 0, h, 0, 0)),
-            pl.BlockSpec((bands, 1, 1, rows, dim), lambda h: (0, 1, h, 0, 0)),
-            own, own, halo, halo, bias,
+            of_band(0), of_band(1), own, own, halo, halo, bias,
         ],
-        out_specs=[own, per_head(sent_shape), stat],
-        out_shape=[
-            half(flat), half((heads,) + sent_shape),
-            jax.ShapeDtypeStruct((heads, 8, rows), jnp.float32),
-        ],
+        out_specs=[own, stat],
+        out_shape=[half(flat), jax.ShapeDtypeStruct((heads, 2, rows), jnp.float32)],
         name="query_side",
-    )(edge_bias, kv, kv, q, g, left, right, own_bias)
-    all_sent = lax.all_gather(sent, "hb")
+    )(edge_bias, band, band, q, g, left, right, own_bias)
+    all_stats = lax.all_gather(stats, "hb")
     left_stats, right_stats = neighbours(stats, stats, "wb")
     dk, dv = pl.pallas_call(
         functools.partial(key_side, factor=factor, tile=tile),
         grid=(heads,),
         in_specs=[
             smem,
-            pl.BlockSpec((bands, 1, 1, rows, dim), lambda h: (0, 0, h, 0, 0)),
-            pl.BlockSpec((bands, 1) + sent_shape, lambda h: (0, h, 0, 0)),
+            of_band(2), of_band(3),
+            pl.BlockSpec((bands, 1, 2, rows), lambda h: (0, h, 0, 0)),
             own, own, halo, halo, stat, stat, bias,
         ],
         out_specs=[own, own],
         out_shape=[half(flat), half(flat)],
         name="key_side",
-    )(edge_bias, all_q, all_sent, k, v, left, right, left_stats, right_stats, col_bias)
+    )(edge_bias, band, band, all_stats, k, v, left, right, left_stats, right_stats, col_bias)
     return tuple(x.reshape(query_rows.shape) for x in (dq, dk, dv))
 
 

time: 174 us -> 117 us (0.67)
  waiting for transfers between devices: 130 us -> 51.8 us
  blocking collectives: 0 us -> 18.2 us
    all_gather x3 -> x1, waiting for transfers between devices: 127 us -> 51.8 us  [on_device(): band = lax.all_gather(jnp.stack(four), 'hb')]
    all_gather x0 -> x1, blocking collectives: none -> 18.2 us  [on_device(): all_stats = lax.all_gather(stats, 'hb')]
    ppermute x4, waiting for transfers between devices: 2.43 us -> 0.01 us  [neighbours(): return (lax.ppermute(last, axis, up), lax.ppermute(first, axis, down))]
    unnamed x16 -> x10, local copies, waits for them, and re-layouts: 0.19 us -> 2.12 us
  transfers between devices with their start and end apart: 7 -> 5, of which waited for: 4 -> 1; matrix products, arithmetic and copies ran while one was open for 3% -> 7% of each run, Pallas kernels for 3% -> 0%
where the time goes in v2:
time: 117 us; the launch traced here: 116 us
  waiting for transfers between devices  51.8 us (44%)
  blocking collectives  18.2 us (16%)
  between operations  14.2 us (12%)
  Pallas kernels  11.2 us (10%)
  starting transfers between devices  9.89 us (8%)
  local copies, waits for them, and re-layouts  6.02 us (5%)
  other arithmetic  4.38 us (4%)
    all_gather x1, waiting for transfers between devices, on_device(): band = lax.all_gather(jnp.stack(four), 'hb')  51.8 us
    all_gather x1, blocking collectives, on_device(): all_stats = lax.all_gather(stats, 'hb')  18.2 us
    ppermute x4, starting transfers between devices, neighbours(): return (lax.ppermute(last, axis, up), lax.ppermute(first, axis, down))  9.85 us
    pallas_call x1, Pallas kernels, on_device(): pl.pallas_call(functools.partial(query_side, factor=factor, tile=tile), g...  5.99 us
    pallas_call x1, Pallas kernels, on_device(): pl.pallas_call(functools.partial(key_side, factor=factor, tile=tile), gri...  5.21 us
  transfers between devices with their start and end apart: 5, of which 1 were waited for; matrix products, arithmetic and copies ran while one was open for 7% of the time, Pallas kernels for 0%

profile of v2, /device:TPU:1, one launch (start us, length us, event | category | flops | bytes accessed | tf_op | source)
XLA Modules:
  0.0 115.7 jit_solution(6549416435131367092)
XLA Ops:
  7.2 0.0 all-gather.4.cloned.1.call-start
  7.2 1.9 %pad_maximum_fusion = bf16[4,3,128,128]{3,2,1,0:T(8,128)(2,1)} fusion(bf16[1,3,128,128]{3,2,1,0:T(8,128)(2,1)} %bitcast.50, bf16[1,3,128,128]{3,2,1,0:T(8,128)(2,1)} %bitcast.53, bf16[1,3,128,128]{3,2,1,0:T(8,128)(2,1)} %bitcast.56, bf16[1,3,128,128]{3,2,1,0:T(8,128)(2,1)} %bitcast.59), kind=kLoop, calls=%fused_computation | loop fusion | flops 589824 | bytes 786432 | tf_op jit(solution)/shard_map/stack | solution.py:175
  9.1 0.0 all-gather.4.cloned.1.call-update
  9.1 0.9 slice_bitcast_fusion
  10.0 0.9 slice_bitcast_fusion.2
  10.9 4.1 %collective-permute-start = (bf16[4,3,64,128]{3,2,1,0:T(8,128)(2,1)S(1)}, bf16[4,3,64,128]{3,2,1,0:T(8,128)(2,1)S(1)}, u32[]{:S(2)}, u32[]{:S(2)}) collective-permute-start(bf16[4,3,64,128]{3,2,1,0:T(8,128)(2,1)S(1)} %pad_maximum_fusion.1), channel_id=1, source_target_pairs={{0,8},{8,16},{16,24},{24,32},{32,40},{40,48},{48,56},{1,9},{9,17},... | collective-permute-start | bytes 589832 | tf_op jit(solution)/shard_map/ppermute | solution.py:154
  15.1 1.3 %collective-permute-start.1 = (bf16[4,3,64,128]{3,2,1,0:T(8,128)(2,1)S(1)}, bf16[4,3,64,128]{3,2,1,0:T(8,128)(2,1)S(1)}, u32[]{:S(2)}, u32[]{:S(2)}) collective-permute-start(bf16[4,3,64,128]{3,2,1,0:T(8,128)(2,1)S(1)} %pad_maximum_fusion.2), channel_id=1, source_target_pairs={{8,0},{16,8},{24,16},{32,24},{40,32},{48,40},{56,48},{9,1},{17,9},... | collective-permute-start | bytes 589832 | tf_op jit(solution)/shard_map/ppermute | solution.py:154
  16.4 0.7 and_bitcast_fusion.1
  17.1 0.1 copy.34
  17.2 0.1 copy.33
  17.3 0.8 copy.35
  18.1 0.8 copy.36
  18.8 0.1 lt.35
  18.9 0.1 iota_compare_fusion.1
  19.0 0.2 fusion.1
  19.2 0.1 copy.37
  19.3 0.1 abs_add_fusion
  19.3 0.7 compare_or_fusion
  20.1 0.1 dynamic-slice_select_fusion
  20.2 0.1 copy.38
  20.3 0.1 broadcast_in_dim.48
  20.4 0.7 reshape.169.bias_ref
  21.1 0.1 broadcast_in_dim.51
  21.2 0.7 reshape.171.bias_ref
  21.9 0.6 add_select_fusion.edge_ref
  22.6 0.0 collective-permute-done.left_ref
  22.6 0.0 copy-start
  22.6 0.0 collective-permute-done.1.right_ref
  22.6 0.0 copy-start.1
  22.6 51.8 %all-gather.4.cloned.1.call-done = bf16[64,3,128,128]{3,2,1,0:T(8,128)(2,1)} async-done(((bf16[4,3,128,128]{3,2,1,0:T(8,128)(2,1)}), bf16[64,3,128,128]{3,2,1,0:T(8,128)(2,1)}) %all-gather.4.cloned.1.call-update) | async-done | bytes 6291472 | tf_op jit(solution)/shard_map/all_gather | solution.py:175
  74.4 0.0 copy-done
  74.4 0.0 copy-done.1
  74.4 6.0 %query_side.1 = (bf16[3,128,128]{2,1,0:T(8,128)(2,1)}, f32[3,2,128]{2,1,0:T(2,128)}) custom-call(f32[3,2]{1,0:T(4,128)} %add_select_fusion.edge_ref, bf16[16,4,3,128,128]{4,3,2,1,0:T(8,128)(2,1)} %bitcast.46, bf16[16,4,3,128,128]{4,3,2,1,0:T(8,128)(2,1)} %bitcast.47, bf16[3,128,128]{2,1,0:T(8,128)(2,1)} %bitcast.55, bf16[3,128,128]{2,1,0:T(8,128)(2,1)} %bitcast.52, ...), custom_call_target="tpu_custom_call" | custom-call | tf_op jit(solution)/shard_map/query_side/pallas_call | solution.py:204
  80.4 3.1 %collective-permute-start.2 = (f32[3,2,128]{2,1,0:T(2,128)}, f32[3,2,128]{2,1,0:T(2,128)S(1)}, u32[]{:S(2)}, u32[]{:S(2)}) collective-permute-start(f32[3,2,128]{2,1,0:T(2,128)} %get-tuple-element.8), channel_id=1, source_target_pairs={{0,8},{8,16},{16,24},{24,32},{32,40},{40,48},{48,56},{1,9},{9,17},... | collective-permute-start | bytes 9224 | tf_op jit(solution)/shard_map/ppermute | solution.py:154
  83.5 1.3 %collective-permute-start.3 = (f32[3,2,128]{2,1,0:T(2,128)}, f32[3,2,128]{2,1,0:T(2,128)S(1)}, u32[]{:S(2)}, u32[]{:S(2)}) collective-permute-start(f32[3,2,128]{2,1,0:T(2,128)} %get-tuple-element.8), channel_id=1, source_target_pairs={{8,0},{16,8},{24,16},{32,24},{40,32},{48,40},{56,48},{9,1},{17,9},... | collective-permute-start | bytes 9224 | tf_op jit(solution)/shard_map/ppermute | solution.py:154
  84.8 18.2 %all-gather.1 = f32[48,2,128]{2,1,0:T(2,128)} all-gather(f32[3,2,128]{2,1,0:T(2,128)} %get-tuple-element.8), channel_id=3, replica_groups=mesh['hb'=16,'wb'=8,'hd'=8] {'hb'}, dimensions={0}, use_global_device_ids=true | all-gather | bytes 52224 | tf_op jit(solution)/shard_map/all_gather | solution.py:215
  103.0 0.0 collective-permute-done.2.left_stats_ref
  103.0 0.0 copy-start.2
  103.0 0.0 collective-permute-done.3.right_stats_ref
  103.0 0.0 copy-start.3
  103.0 0.6 copy-done.2
  103.6 0.0 copy-done.3
  103.6 5.2 %key_side.1 = (bf16[3,128,128]{2,1,0:T(8,128)(2,1)}, bf16[3,128,128]{2,1,0:T(8,128)(2,1)}) custom-call(f32[3,2]{1,0:T(4,128)} %add_select_fusion.edge_ref, bf16[16,4,3,128,128]{4,3,2,1,0:T(8,128)(2,1)} %bitcast.48, bf16[16,4,3,128,128]{4,3,2,1,0:T(8,128)(2,1)} %bitcast.49, f32[16,3,2,128]{3,2,1,0:T(2,128)} %bitcast.62, bf16[3,128,128]{2,1,0:T(8,128)(2,1)} %bitcast.61, ...), custom_call_target="tpu_custom_call" | custom-call | tf_op jit(solution)/shard_map/key_side/pallas_call | solution.py:217
  (4 shorter events, 0.1 us)
Async XLA Ops:
  7.2 67.2 %all-gather.4.cloned.1.call-start = ((), (), s32[]{:S(2)}) async-start(), calls=%async_computation | async-start | bytes 6684672 | tf_op jit(solution)/shard_map/all_gather | solution.py:175
  10.9 11.6 %collective-permute-start = (bf16[4,3,64,128]{3,2,1,0:T(8,128)(2,1)S(1)}, bf16[4,3,64,128]{3,2,1,0:T(8,128)(2,1)S(1)}, u32[]{:S(2)}, u32[]{:S(2)}) collective-permute-start(bf16[4,3,64,128]{3,2,1,0:T(8,128)(2,1)S(1)} %pad_maximum_fusion.1), channel_id=1, source_target_pairs={{0,8},{8,16},{16,24},{24,32},{32,40},{40,48},{48,56},{1,9},{9,17},... | collective-permute-start | bytes 589832 | tf_op jit(solution)/shard_map/ppermute | solution.py:154
  15.1 7.5 %collective-permute-start.1 = (bf16[4,3,64,128]{3,2,1,0:T(8,128)(2,1)S(1)}, bf16[4,3,64,128]{3,2,1,0:T(8,128)(2,1)S(1)}, u32[]{:S(2)}, u32[]{:S(2)}) collective-permute-start(bf16[4,3,64,128]{3,2,1,0:T(8,128)(2,1)S(1)} %pad_maximum_fusion.2), channel_id=1, source_target_pairs={{8,0},{16,8},{24,16},{32,24},{40,32},{48,40},{56,48},{9,1},{17,9},... | collective-permute-start | bytes 589832 | tf_op jit(solution)/shard_map/ppermute | solution.py:154
  22.6 51.8 %copy-start = (bf16[4,3,64,128]{3,2,1,0:T(8,128)(2,1)}, bf16[4,3,64,128]{3,2,1,0:T(8,128)(2,1)S(1)}, u32[]{:S(2)}) copy-start(bf16[4,3,64,128]{3,2,1,0:T(8,128)(2,1)S(1)} %collective-permute-done.left_ref) | copy-start | bytes 589828
  22.6 51.8 %copy-start.1 = (bf16[4,3,64,128]{3,2,1,0:T(8,128)(2,1)}, bf16[4,3,64,128]{3,2,1,0:T(8,128)(2,1)S(1)}, u32[]{:S(2)}) copy-start(bf16[4,3,64,128]{3,2,1,0:T(8,128)(2,1)S(1)} %collective-permute-done.1.right_ref) | copy-start | bytes 589828
  80.4 22.6 %collective-permute-start.2 = (f32[3,2,128]{2,1,0:T(2,128)}, f32[3,2,128]{2,1,0:T(2,128)S(1)}, u32[]{:S(2)}, u32[]{:S(2)}) collective-permute-start(f32[3,2,128]{2,1,0:T(2,128)} %get-tuple-element.8), channel_id=1, source_target_pairs={{0,8},{8,16},{16,24},{24,32},{32,40},{40,48},{48,56},{1,9},{9,17},... | collective-permute-start | bytes 9224 | tf_op jit(solution)/shard_map/ppermute | solution.py:154
  83.5 19.5 %collective-permute-start.3 = (f32[3,2,128]{2,1,0:T(2,128)}, f32[3,2,128]{2,1,0:T(2,128)S(1)}, u32[]{:S(2)}, u32[]{:S(2)}) collective-permute-start(f32[3,2,128]{2,1,0:T(2,128)} %get-tuple-element.8), channel_id=1, source_target_pairs={{8,0},{16,8},{24,16},{32,24},{40,32},{48,40},{56,48},{9,1},{17,9},... | collective-permute-start | bytes 9224 | tf_op jit(solution)/shard_map/ppermute | solution.py:154
  103.0 0.6 copy-start.2
  103.0 0.6 copy-start.3
Sparse Core Ops, SparseCore 0:
  10.7 63.6 all-gather.3

commit v3 on v2

--- a/solution.py
+++ b/solution.py
@@ -21,19 +21,28 @@
     return jnp.transpose(jnp.broadcast_to(col, (n, n)))[0:1]
 
 
-def query_side(
-    edge_ref, keys_ref, values_ref, q_ref, g_ref, left_ref, right_ref, bias_ref,
-    dq_ref, stats_ref, *, factor, tile
-):
+def joined(units, slot):
+    return jnp.concatenate([u[i, slot, 0] for u in units for i in range(u.shape[0])], axis=0)
+
+
+def bias_of(bias_ref, row, rows):
+    return bias_ref[0, :, pl.ds(pl.multiple_of(row * rows, rows), rows)]
+
+
+def query_side(order_ref, edge_ref, *refs, factor, tile):
+    bands = order_ref.shape[0]
+    units = refs[:-6]
+    own_ref, left_ref, right_ref, bias_ref, dq_ref, stats_ref = refs[-6:]
     head = pl.program_id(0)
-    rows, dim = q_ref.shape[1:]
-    keys = keys_ref[:, 0, 0].reshape(-1, dim)
-    values = values_ref[:, 0, 0].reshape(-1, dim)
-    q = q_ref[0]
-    g = g_ref[0]
+    rows, dim = dq_ref.shape[1:]
+    keys = joined(units, 0)
+    values = joined(units, 1)
+    q = own_ref[0, 0]
+    g = own_ref[1, 0]
     shaped = (rows // tile, tile, keys.shape[0])
     scores = dot(q, keys, NT) * factor
-    scores = (scores.reshape(shaped) + bias_ref[0][:, None, :]).reshape(rows, -1)
+    bias = jnp.concatenate([bias_of(bias_ref, order_ref[u], rows) for u in range(bands)], axis=1)
+    scores = (scores.reshape(shaped) + bias[:, None, :]).reshape(rows, -1)
     edge_keys = (left_ref[0, 0], right_ref[0, 0])
     edge_values = (left_ref[1, 0], right_ref[1, 0])
     edge_q = (q[:tile], q[rows - tile:])
@@ -88,16 +97,16 @@
 
 
 def key_side(
-    edge_ref, queries_ref, cotan_ref, all_stats_ref, k_ref, v_ref, left_ref, right_ref,
-    left_stats_ref, right_stats_ref, bias_ref, dk_ref, dv_ref, *, factor, tile
+    edge_ref, asked_ref, all_stats_ref, own_ref, left_ref, right_ref, left_stats_ref,
+    right_stats_ref, bias_ref, dk_ref, dv_ref, *, factor, tile
 ):
+    bands = asked_ref.shape[0]
     head = pl.program_id(0)
-    rows, dim = k_ref.shape[1:]
-    bands = queries_ref.shape[0]
-    queries = queries_ref[:, 0, 0].reshape(-1, dim)
-    cotan = cotan_ref[:, 0, 0].reshape(-1, dim)
-    k = k_ref[0]
-    v = v_ref[0]
+    rows, dim = dk_ref.shape[1:]
+    queries = joined([asked_ref], 0)
+    cotan = joined([asked_ref], 1)
+    k = own_ref[0, 0]
+    v = own_ref[1, 0]
     scores = dot(k, queries, NT)
     slopes = dot(v, cotan, NT)
     grads, probs = [], []
@@ -154,6 +163,36 @@
     return lax.ppermute(last, axis, up), lax.ppermute(first, axis, down)
 
 
+def band_units(own, axis, aside):
+    size = lax.axis_size(axis)
+    index = lax.axis_index(axis)
+    pairs = size // 2
+    side = index % 2
+    swap = [(i, i ^ 1) for i in range(size)]
+    step = [(i, (i + (2 if i % 2 == 0 else -2)) % size) for i in range(size)]
+
+    def handed(x):
+        return lax.ppermute(x, axis, swap)
+
+    def passed(x):
+        return lax.ppermute(x, axis, step)
+
+    held = jnp.stack((own, handed(own)))
+    units, order = [held], [index, index ^ 1]
+    for s in range(1, pairs // 2 + 1):
+        if s == 3:
+            held, aside = lax.optimization_barrier((held, aside))
+        near = (index // 2 - (1 - 2 * side) * s) % pairs
+        far = (index // 2 + (1 - 2 * side) * s) % pairs
+        sides = [side, 1 - side]
+        if 2 * s == pairs:
+            held, sides = held[:1], sides[:1]
+        held = passed(held)
+        units += [held, handed(held)]
+        order += [2 * near + i for i in sides] + [2 * far + 1 - i for i in sides]
+    return units, jnp.stack(order).astype(jnp.int32), aside
+
+
 def row_bias(allowed, tile):
     bias = jnp.where(allowed, 0.0, CLOSED).astype(jnp.float32)
     heads, own, others = bias.shape
@@ -171,8 +210,10 @@
     bands = lax.axis_size("hb")
     flat = (heads, rows, dim)
     q, k, v, g = (x.reshape(flat) for x in (query_rows, key_rows, value_rows, grad_out))
+    asking = jnp.stack((q, g))
+    keyed = jnp.stack((k, v))
+    all_asking = lax.all_gather(asking, "hb")
     four = (k, v, q, g)
-    band = lax.all_gather(jnp.stack(four), "hb")
     left, right = neighbours(
         jnp.stack([x[:, :tile] for x in four]), jnp.stack([x[:, rows - tile:] for x in four]), "wb"
     )
@@ -188,45 +229,48 @@
     )
     edge_bias = jnp.where(edge_open, 0.0, CLOSED).astype(jnp.float32)
 
+    units, order, (own_bias, col_bias, edge_bias) = band_units(
+        keyed, "hb", (own_bias, col_bias, edge_bias)
+    )
+
     def per_head(shape):
         return pl.BlockSpec((1,) + shape, lambda h: (h,) + (0,) * len(shape))
 
     smem = pl.BlockSpec(memory_space=pltpu.SMEM)
-    own = per_head((rows, dim))
+    result = per_head((rows, dim))
+    pair = pl.BlockSpec((2, 1, rows, dim), lambda h: (0, h, 0, 0))
+
+    def units_of(count):
+        return pl.BlockSpec((count, 2, 1, rows, dim), lambda h: (0, 0, h, 0, 0))
+
     halo = pl.BlockSpec((4, 1, tile, dim), lambda h: (0, h, 0, 0))
     bias = per_head((dev_tiles, bands * rows))
     stat = per_head((2, rows))
-
-    def of_band(slot):
-        return pl.BlockSpec((bands, 1, 1, rows, dim), lambda h: (0, slot, h, 0, 0))
-
-    half = functools.partial(jax.ShapeDtypeStruct, dtype=jnp.bfloat16)
+    half = jax.ShapeDtypeStruct(flat, jnp.bfloat16)
     dq, stats = pl.pallas_call(
         functools.partial(query_side, factor=factor, tile=tile),
         grid=(heads,),
-        in_specs=[
-            smem,
-            of_band(0), of_band(1), own, own, halo, halo, bias,
-        ],
-        out_specs=[own, stat],
-        out_shape=[half(flat), jax.ShapeDtypeStruct((heads, 2, rows), jnp.float32)],
+        in_specs=[smem, smem] + [units_of(u.shape[0]) for u in units] + [pair, halo, halo, bias],
+        out_specs=[result, stat],
+        out_shape=[half, jax.ShapeDtypeStruct((heads, 2, rows), jnp.float32)],
         name="query_side",
-    )(edge_bias, band, band, q, g, left, right, own_bias)
+    )(order, edge_bias, *units, asking, left, right, own_bias)
+    left_stats, right_stats = neighbours(stats, stats, "wb")
     all_stats = lax.all_gather(stats, "hb")
-    left_stats, right_stats = neighbours(stats, stats, "wb")
     dk, dv = pl.pallas_call(
         functools.partial(key_side, factor=factor, tile=tile),
         grid=(heads,),
         in_specs=[
-            smem,
-            of_band(2), of_band(3),
+            smem, units_of(bands),
             pl.BlockSpec((bands, 1, 2, rows), lambda h: (0, h, 0, 0)),
-            own, own, halo, halo, stat, stat, bias,
+            pair, halo, halo, stat, stat, bias,
         ],
-        out_specs=[own, own],
-        out_shape=[half(flat), half(flat)],
+        out_specs=[result, result],
+        out_shape=[half, half],
         name="key_side",
-    )(edge_bias, band, band, all_stats, k, v, left, right, left_stats, right_stats, col_bias)
+    )(
+        edge_bias, all_asking, all_stats, keyed, left, right, left_stats, right_stats, col_bias
+    )
     return tuple(x.reshape(query_rows.shape) for x in (dq, dk, dv))
 
 

time: 117 us -> 126 us (1.077)
  starting transfers between devices: 9.89 us -> 48.9 us
  waiting for transfers between devices: 51.8 us -> 17.3 us
  blocking collectives: 18.2 us -> 19.8 us
  other arithmetic: 4.38 us -> 5.88 us
    all_gather x1, waiting for transfers between devices: 51.8 us -> 0.02 us  [on_device(): all_asking = lax.all_gather(asking, 'hb')]
    ppermute x0 -> x9, starting transfers between devices: none -> 41.9 us  [the longest x5 29.5 us: handed(): return lax.ppermute(x, axis, swap)]
    ppermute x0 -> x9, waiting for transfers between devices: none -> 17.2 us  [the longest x4 16.9 us: passed(): return lax.ppermute(x, axis, step)]
    ppermute x4, starting transfers between devices: 9.85 us -> 6.99 us  [neighbours(): return (lax.ppermute(last, axis, up), lax.ppermute(first, axis, down))]
    all_gather x1, blocking collectives: 18.2 us -> 19.8 us  [on_device(): all_stats = lax.all_gather(stats, 'hb')]
    unnamed x10 -> x32, local copies, waits for them, and re-layouts: 2.12 us -> 3.5 us
    another operation x1 -> x3, other arithmetic: 1.86 us -> 2.67 us  [the longest x1 1.66 us: on_device(): asking = jnp.stack((q, g))]
  transfers between devices with their start and end apart: 5 -> 14, of which waited for: 1 -> 4; matrix products, arithmetic and copies ran while one was open for 7% -> 8% of each run, Pallas kernels for 0% -> 5%
where the time goes in v3:
time: 126 us; the launch traced here: 125 us
  starting transfers between devices  48.9 us (39%)
  blocking collectives  19.8 us (16%)
  waiting for transfers between devices  17.3 us (14%)
  between operations  14.6 us (12%)
  Pallas kernels  11.4 us (9%)
  local copies, waits for them, and re-layouts  7.24 us (6%)
  other arithmetic  5.88 us (5%)
    ppermute x5, starting transfers between devices, handed(): return lax.ppermute(x, axis, swap)  29.5 us
    all_gather x1, blocking collectives, on_device(): all_stats = lax.all_gather(stats, 'hb')  19.8 us
    ppermute x4, waiting for transfers between devices, passed(): return lax.ppermute(x, axis, step)  16.9 us
    ppermute x4, starting transfers between devices, passed(): return lax.ppermute(x, axis, step)  12.4 us
    ppermute x4, starting transfers between devices, neighbours(): return (lax.ppermute(last, axis, up), lax.ppermute(first, axis, down))  6.99 us
    pallas_call x1, Pallas kernels, on_device(): pl.pallas_call(functools.partial(query_side, factor=factor, tile=tile), g...  6.18 us
    pallas_call x1, Pallas kernels, on_device(): pl.pallas_call(functools.partial(key_side, factor=factor, tile=tile), gri...  5.22 us
    unnamed x32, local copies, waits for them, and re-layouts  3.5 us
  transfers between devices with their start and end apart: 14, of which 4 were waited for; matrix products, arithmetic and copies ran while one was open for 8% of the time, Pallas kernels for 5%

profile of v3, /device:TPU:1, one launch (start us, length us, event | category | flops | bytes accessed | tf_op | source)
XLA Modules:
  0.0 125.0 jit_solution(13704636119368839817)
XLA Ops:
  7.2 0.0 all-gather.4.cloned.1.call-start
  7.2 1.7 %pad_maximum_fusion.2.refs_9_ = bf16[2,3,128,128]{3,2,1,0:T(8,128)(2,1)} fusion(bf16[1,3,128,128]{3,2,1,0:T(8,128)(2,1)} %bitcast.70, bf16[1,3,128,128]{3,2,1,0:T(8,128)(2,1)} %bitcast.72), kind=kLoop, calls=%fused_computation.2 | loop fusion | flops 98304 | bytes 393216 | tf_op jit(solution)/shard_map/stack | solution.py:213
  8.9 0.0 all-gather.4.cloned.1.call-update
  8.9 1.0 fusion.3
  9.9 16.0 %collective-permute-start = (bf16[2,3,128,128]{3,2,1,0:T(8,128)(2,1)S(1)}, bf16[2,3,128,128]{3,2,1,0:T(8,128)(2,1)S(1)}, u32[]{:S(2)}, u32[]{:S(2)}) collective-permute-start(bf16[2,3,128,128]{3,2,1,0:T(8,128)(2,1)S(1)} %get-tuple-element.32.own_ref), channel_id=1, source_target_pairs={{0,64},{64,0},{128,192},{192,128},{256,320},{320,256},{384,448},{4... | collective-permute-start | bytes 589832 | tf_op jit(solution)/shard_map/ppermute | solution.py:175
  25.9 0.8 copy.33
  26.7 0.8 copy.34
  27.5 0.1 lt.81
  27.6 0.1 abs_add_fusion
  27.6 0.1 iota_compare_fusion.1
  27.7 0.0 collective-permute-done
  27.8 1.9 %collective-permute-start.1 = (bf16[2,2,3,128,128]{4,3,2,1,0:T(8,128)(2,1)S(1)}, bf16[2,2,3,128,128]{4,3,2,1,0:T(8,128)(2,1)S(1)}, u32[]{:S(2)}, u32[]{:S(2)}) collective-permute-start(bf16[2,2,3,128,128]{4,3,2,1,0:T(8,128)(2,1)S(1)} %pad_maximum_fusion.refs_0_), channel_id=1, source_target_pairs={{0,128},{64,960},{128,256},{192,64},{256,384},{320,192},{384,512},... | collective-permute-start | bytes 1179656 | tf_op jit(solution)/shard_map/ppermute | solution.py:178
  29.7 0.2 fusion.1
  29.9 0.1 copy.35
  30.0 0.7 compare_or_fusion
  30.7 0.1 dynamic-slice_select_fusion
  30.8 0.1 copy.36
  30.9 0.1 broadcast_in_dim.46
  31.0 0.7 reshape.165.refs_12_
  31.7 4.9 %collective-permute-done.1.refs_1_ = bf16[2,2,3,128,128]{4,3,2,1,0:T(8,128)(2,1)S(1)} collective-permute-done((bf16[2,2,3,128,128]{4,3,2,1,0:T(8,128)(2,1)S(1)}, bf16[2,2,3,128,128]{4,3,2,1,0:T(8,128)(2,1)S(1)}, u32[]{:S(2)}, u32[]{:S(2)}) %collective-permute-start.1) | collective-permute-done | bytes 393248 | tf_op jit(solution)/shard_map/ppermute | solution.py:178
  36.6 2.8 %collective-permute-start.2 = (bf16[2,2,3,128,128]{4,3,2,1,0:T(8,128)(2,1)S(1)}, bf16[2,2,3,128,128]{4,3,2,1,0:T(8,128)(2,1)S(1)}, u32[]{:S(2)}, u32[]{:S(2)}) collective-permute-start(bf16[2,2,3,128,128]{4,3,2,1,0:T(8,128)(2,1)S(1)} %collective-permute-done.1.refs_1_), channel_id=1, source_target_pairs={{0,128},{64,960},{128,256},{192,64},{256,384},{320,192},{384,512},... | collective-permute-start | bytes 1179656 | tf_op jit(solution)/shard_map/ppermute | solution.py:178
  39.5 0.1 broadcast_in_dim.49
  39.5 0.7 reshape.166.bias_ref
  40.3 0.7 and_bitcast_fusion.1
  40.9 0.1 copy.37
  41.0 0.1 copy.38
  41.1 0.7 add_select_fusion.edge_ref
  41.8 8.5 %collective-permute-done.2.refs_3_ = bf16[2,2,3,128,128]{4,3,2,1,0:T(8,128)(2,1)S(1)} collective-permute-done((bf16[2,2,3,128,128]{4,3,2,1,0:T(8,128)(2,1)S(1)}, bf16[2,2,3,128,128]{4,3,2,1,0:T(8,128)(2,1)S(1)}, u32[]{:S(2)}, u32[]{:S(2)}) %collective-permute-start.2) | collective-permute-done | bytes 393248 | tf_op jit(solution)/shard_map/ppermute | solution.py:178
  50.3 3.1 %collective-permute-start.5 = (bf16[2,2,3,128,128]{4,3,2,1,0:T(8,128)(2,1)S(1)}, bf16[2,2,3,128,128]{4,3,2,1,0:T(8,128)(2,1)S(1)}, u32[]{:S(2)}, u32[]{:S(2)}) collective-permute-start(bf16[2,2,3,128,128]{4,3,2,1,0:T(8,128)(2,1)S(1)} %collective-permute-done.2.refs_3_), channel_id=1, source_target_pairs={{0,128},{64,960},{128,256},{192,64},{256,384},{320,192},{384,512},... | collective-permute-start | bytes 1179656 | tf_op jit(solution)/shard_map/ppermute | solution.py:178
  53.5 0.9 slice_bitcast_fusion.2
  54.5 1.3 %collective-permute-start.10 = (bf16[4,3,64,128]{3,2,1,0:T(8,128)(2,1)S(1)}, bf16[4,3,64,128]{3,2,1,0:T(8,128)(2,1)S(1)}, u32[]{:S(2)}, u32[]{:S(2)}) collective-permute-start(bf16[4,3,64,128]{3,2,1,0:T(8,128)(2,1)S(1)} %pad_maximum_fusion.4), channel_id=1, source_target_pairs={{8,0},{16,8},{24,16},{32,24},{40,32},{48,40},{56,48},{9,1},{17,9},... | collective-permute-start | bytes 589832 | tf_op jit(solution)/shard_map/ppermute | solution.py:163
  55.8 4.1 %collective-permute-start.3 = (bf16[2,2,3,128,128]{4,3,2,1,0:T(8,128)(2,1)S(1)}, bf16[2,2,3,128,128]{4,3,2,1,0:T(8,128)(2,1)S(1)}, u32[]{:S(2)}, u32[]{:S(2)}) collective-permute-start(bf16[2,2,3,128,128]{4,3,2,1,0:T(8,128)(2,1)S(1)} %collective-permute-done.1.refs_1_), channel_id=1, source_target_pairs={{0,64},{64,0},{128,192},{192,128},{256,320},{320,256},{384,448},{4... | collective-permute-start | bytes 1179656 | tf_op jit(solution)/shard_map/ppermute | solution.py:175
  59.9 1.9 %collective-permute-start.4 = (bf16[2,2,3,128,128]{4,3,2,1,0:T(8,128)(2,1)S(1)}, bf16[2,2,3,128,128]{4,3,2,1,0:T(8,128)(2,1)S(1)}, u32[]{:S(2)}, u32[]{:S(2)}) collective-permute-start(bf16[2,2,3,128,128]{4,3,2,1,0:T(8,128)(2,1)S(1)} %collective-permute-done.2.refs_3_), channel_id=1, source_target_pairs={{0,64},{64,0},{128,192},{192,128},{256,320},{320,256},{384,448},{4... | collective-permute-start | bytes 1179656 | tf_op jit(solution)/shard_map/ppermute | solution.py:175
  61.9 3.5 %collective-permute-done.5.refs_5_ = bf16[2,2,3,128,128]{4,3,2,1,0:T(8,128)(2,1)S(1)} collective-permute-done((bf16[2,2,3,128,128]{4,3,2,1,0:T(8,128)(2,1)S(1)}, bf16[2,2,3,128,128]{4,3,2,1,0:T(8,128)(2,1)S(1)}, u32[]{:S(2)}, u32[]{:S(2)}) %collective-permute-start.5) | collective-permute-done | bytes 393248 | tf_op jit(solution)/shard_map/ppermute | solution.py:178
  65.4 4.5 %collective-permute-start.7 = (bf16[1,2,3,128,128]{4,3,2,1,0:T(8,128)(2,1)S(1)}, bf16[1,2,3,128,128]{4,3,2,1,0:T(8,128)(2,1)S(1)}, u32[]{:S(2)}, u32[]{:S(2)}) collective-permute-start(bf16[1,2,3,128,128]{4,3,2,1,0:T(8,128)(2,1)S(1)} %slice.36), channel_id=1, source_target_pairs={{0,128},{64,960},{128,256},{192,64},{256,384},{320,192},{384,512},... | collective-permute-start | bytes 589832 | tf_op jit(solution)/shard_map/ppermute | solution.py:178
  69.9 2.6 %collective-permute-start.6 = (bf16[2,2,3,128,128]{4,3,2,1,0:T(8,128)(2,1)S(1)}, bf16[2,2,3,128,128]{4,3,2,1,0:T(8,128)(2,1)S(1)}, u32[]{:S(2)}, u32[]{:S(2)}) collective-permute-start(bf16[2,2,3,128,128]{4,3,2,1,0:T(8,128)(2,1)S(1)} %collective-permute-done.5.refs_5_), channel_id=1, source_target_pairs={{0,64},{64,0},{128,192},{192,128},{256,320},{320,256},{384,448},{4... | collective-permute-start | bytes 1179656 | tf_op jit(solution)/shard_map/ppermute | solution.py:175
  72.5 0.7 pad_maximum_fusion.3
  73.2 0.0 collective-permute-done.10.refs_11_.right_ref
  73.2 1.3 %collective-permute-start.9 = (bf16[4,3,64,128]{3,2,1,0:T(8,128)(2,1)}, bf16[4,3,64,128]{3,2,1,0:T(8,128)(2,1)S(1)}, u32[]{:S(2)}, u32[]{:S(2)}) collective-permute-start(bf16[4,3,64,128]{3,2,1,0:T(8,128)(2,1)} %pad_maximum_fusion.3), channel_id=1, source_target_pairs={{0,8},{8,16},{16,24},{24,32},{32,40},{40,48},{48,56},{1,9},{9,17},... | collective-permute-start | bytes 589832 | tf_op jit(solution)/shard_map/ppermute | solution.py:163
  74.5 0.0 collective-permute-done.7.refs_7_
  74.5 4.8 %collective-permute-start.8 = (bf16[1,2,3,128,128]{4,3,2,1,0:T(8,128)(2,1)S(1)}, bf16[1,2,3,128,128]{4,3,2,1,0:T(8,128)(2,1)}, u32[]{:S(2)}, u32[]{:S(2)}) collective-permute-start(bf16[1,2,3,128,128]{4,3,2,1,0:T(8,128)(2,1)S(1)} %collective-permute-done.7.refs_7_), channel_id=1, source_target_pairs={{0,64},{64,0},{128,192},{192,128},{256,320},{320,256},{384,448},{4... | collective-permute-start | bytes 589832 | tf_op jit(solution)/shard_map/ppermute | solution.py:175
  79.5 0.7 stack.121.order_ref
  80.2 0.0 collective-permute-done.9.refs_10_.left_ref
  80.2 0.0 collective-permute-done.3.refs_2_
  80.2 0.0 collective-permute-done.4.refs_4_
  80.2 0.0 copy-start.8
  80.2 0.3 collective-permute-done.8.refs_8_
  80.5 0.0 collective-permute-done.6.refs_6_
  80.5 0.0 copy-done.6
  80.6 0.3 copy-done.3
  80.9 0.1 copy-done.7
  81.0 0.2 copy-done.8
  81.2 0.7 copy-done.9
  81.9 6.2 %query_side.1 = (bf16[3,128,128]{2,1,0:T(8,128)(2,1)}, f32[3,2,128]{2,1,0:T(2,128)}) custom-call(s32[16]{0:T(128)} %stack.121.order_ref, f32[3,2]{1,0:T(4,128)} %add_select_fusion.edge_ref, bf16[2,2,3,128,128]{4,3,2,1,0:T(8,128)(2,1)} %copy-done, bf16[2,2,3,128,128]{4,3,2,1,0:T(8,128)(2,1)} %copy-done.5, bf16[2,2,3,128,128]{4,3,2,1,0:T(8,128)(2,1)} %copy-done.7, ...), custom_call_target="tpu_custom_call" | custom-call | tf_op jit(solution)/shard_map/query_side/pallas_call | solution.py:250
  88.1 0.0 copy-done.4
  88.1 3.1 %collective-permute-start.11 = (f32[3,2,128]{2,1,0:T(2,128)}, f32[3,2,128]{2,1,0:T(2,128)S(1)}, u32[]{:S(2)}, u32[]{:S(2)}) collective-permute-start(f32[3,2,128]{2,1,0:T(2,128)} %get-tuple-element.15), channel_id=1, source_target_pairs={{0,8},{8,16},{16,24},{24,32},{32,40},{40,48},{48,56},{1,9},{9,17},... | collective-permute-start | bytes 9224 | tf_op jit(solution)/shard_map/ppermute | solution.py:163
  91.2 1.3 %collective-permute-start.12 = (f32[3,2,128]{2,1,0:T(2,128)}, f32[3,2,128]{2,1,0:T(2,128)S(1)}, u32[]{:S(2)}, u32[]{:S(2)}) collective-permute-start(f32[3,2,128]{2,1,0:T(2,128)} %get-tuple-element.15), channel_id=1, source_target_pairs={{8,0},{16,8},{24,16},{32,24},{40,32},{48,40},{56,48},{9,1},{17,9},... | collective-permute-start | bytes 9224 | tf_op jit(solution)/shard_map/ppermute | solution.py:163
  92.5 19.8 %all-gather.1 = f32[48,2,128]{2,1,0:T(2,128)} all-gather(f32[3,2,128]{2,1,0:T(2,128)} %get-tuple-element.15), channel_id=3, replica_groups=mesh['hb'=16,'wb'=8,'hd'=8] {'hb'}, dimensions={0}, use_global_device_ids=true | all-gather | bytes 52224 | tf_op jit(solution)/shard_map/all_gather | solution.py:259
  112.3 0.0 collective-permute-done.11.left_stats_ref
  112.4 0.0 collective-permute-done.12.right_stats_ref
  112.4 0.0 all-gather.4.cloned.1.call-done
  112.4 0.5 copy-done.13
  112.9 0.0 copy-done.14
  113.0 5.2 %key_side.1 = (bf16[3,128,128]{2,1,0:T(8,128)(2,1)}, bf16[3,128,128]{2,1,0:T(8,128)(2,1)}) custom-call(f32[3,2]{1,0:T(4,128)} %add_select_fusion.edge_ref, bf16[16,2,3,128,128]{4,3,2,1,0:T(8,128)(2,1)} %bitcast.65, f32[16,3,2,128]{3,2,1,0:T(2,128)} %bitcast.74, bf16[2,3,128,128]{3,2,1,0:T(8,128)(2,1)} %copy-done.4, bf16[4,3,64,128]{3,2,1,0:T(8,128)(2,1)} %copy-done.3, ...), custom_call_target="tpu_custom_call" | custom-call | tf_op jit(solution)/shard_map/key_side/pallas_call | solution.py:260
  (27 shorter events, 0.2 us)
Async XLA Ops:
  7.2 47.2 %copy-start.11 = (bf16[3,1,2,64,128]{4,3,2,1,0:T(8,128)(2,1)S(1)}, bf16[3,1,2,64,128]{4,3,2,1,0:T(8,128)(2,1)}, u32[]{:S(2)}) copy-start(bf16[3,1,2,64,128]{4,3,2,1,0:T(8,128)(2,1)} %param.7) | copy-start | bytes 294916
  7.2 47.2 %copy-start.10 = (bf16[3,1,2,64,128]{4,3,2,1,0:T(8,128)(2,1)S(1)}, bf16[3,1,2,64,128]{4,3,2,1,0:T(8,128)(2,1)}, u32[]{:S(2)}) copy-start(bf16[3,1,2,64,128]{4,3,2,1,0:T(8,128)(2,1)} %param.10) | copy-start | bytes 294916
  7.2 105.2 %all-gather.4.cloned.1.call-start = ((), (), s32[]{:S(2)}) async-start(), calls=%async_computation | async-start | bytes 3342336 | tf_op jit(solution)/shard_map/all_gather | solution.py:215
  9.9 78.2 %copy-start.4 = (bf16[2,3,128,128]{3,2,1,0:T(8,128)(2,1)}, bf16[2,3,128,128]{3,2,1,0:T(8,128)(2,1)S(1)}, u32[]{:S(2)}) copy-start(bf16[2,3,128,128]{3,2,1,0:T(8,128)(2,1)S(1)} %get-tuple-element.32.own_ref) | copy-start | bytes 589828
  9.9 17.8 %collective-permute-start = (bf16[2,3,128,128]{3,2,1,0:T(8,128)(2,1)S(1)}, bf16[2,3,128,128]{3,2,1,0:T(8,128)(2,1)S(1)}, u32[]{:S(2)}, u32[]{:S(2)}) collective-permute-start(bf16[2,3,128,128]{3,2,1,0:T(8,128)(2,1)S(1)} %get-tuple-element.32.own_ref), channel_id=1, source_target_pairs={{0,64},{64,0},{128,192},{192,128},{256,320},{320,256},{384,448},{4... | collective-permute-start | bytes 589832 | tf_op jit(solution)/shard_map/ppermute | solution.py:175
  27.8 52.7 %copy-start = (bf16[2,2,3,128,128]{4,3,2,1,0:T(8,128)(2,1)}, bf16[2,2,3,128,128]{4,3,2,1,0:T(8,128)(2,1)S(1)}, u32[]{:S(2)}) copy-start(bf16[2,2,3,128,128]{4,3,2,1,0:T(8,128)(2,1)S(1)} %pad_maximum_fusion.refs_0_) | copy-start | bytes 1179652
  27.8 8.8 %collective-permute-start.1 = (bf16[2,2,3,128,128]{4,3,2,1,0:T(8,128)(2,1)S(1)}, bf16[2,2,3,128,128]{4,3,2,1,0:T(8,128)(2,1)S(1)}, u32[]{:S(2)}, u32[]{:S(2)}) collective-permute-start(bf16[2,2,3,128,128]{4,3,2,1,0:T(8,128)(2,1)S(1)} %pad_maximum_fusion.refs_0_), channel_id=1, source_target_pairs={{0,128},{64,960},{128,256},{192,64},{256,384},{320,192},{384,512},... | collective-permute-start | bytes 1179656 | tf_op jit(solution)/shard_map/ppermute | solution.py:178
  36.6 43.9 %copy-start.5 = (bf16[2,2,3,128,128]{4,3,2,1,0:T(8,128)(2,1)}, bf16[2,2,3,128,128]{4,3,2,1,0:T(8,128)(2,1)S(1)}, u32[]{:S(2)}) copy-start(bf16[2,2,3,128,128]{4,3,2,1,0:T(8,128)(2,1)S(1)} %collective-permute-done.1.refs_1_) | copy-start | bytes 1179652
  36.6 13.7 %collective-permute-start.2 = (bf16[2,2,3,128,128]{4,3,2,1,0:T(8,128)(2,1)S(1)}, bf16[2,2,3,128,128]{4,3,2,1,0:T(8,128)(2,1)S(1)}, u32[]{:S(2)}, u32[]{:S(2)}) collective-permute-start(bf16[2,2,3,128,128]{4,3,2,1,0:T(8,128)(2,1)S(1)} %collective-permute-done.1.refs_1_), channel_id=1, source_target_pairs={{0,128},{64,960},{128,256},{192,64},{256,384},{320,192},{384,512},... | collective-permute-start | bytes 1179656 | tf_op jit(solution)/shard_map/ppermute | solution.py:178
  50.3 30.2 %copy-start.6 = (bf16[2,2,3,128,128]{4,3,2,1,0:T(8,128)(2,1)}, bf16[2,2,3,128,128]{4,3,2,1,0:T(8,128)(2,1)S(1)}, u32[]{:S(2)}) copy-start(bf16[2,2,3,128,128]{4,3,2,1,0:T(8,128)(2,1)S(1)} %collective-permute-done.2.refs_3_) | copy-start | bytes 1179652
  50.3 15.0 %collective-permute-start.5 = (bf16[2,2,3,128,128]{4,3,2,1,0:T(8,128)(2,1)S(1)}, bf16[2,2,3,128,128]{4,3,2,1,0:T(8,128)(2,1)S(1)}, u32[]{:S(2)}, u32[]{:S(2)}) collective-permute-start(bf16[2,2,3,128,128]{4,3,2,1,0:T(8,128)(2,1)S(1)} %collective-permute-done.2.refs_3_), channel_id=1, source_target_pairs={{0,128},{64,960},{128,256},{192,64},{256,384},{320,192},{384,512},... | collective-permute-start | bytes 1179656 | tf_op jit(solution)/shard_map/ppermute | solution.py:178
  54.5 18.7 %collective-permute-start.10 = (bf16[4,3,64,128]{3,2,1,0:T(8,128)(2,1)S(1)}, bf16[4,3,64,128]{3,2,1,0:T(8,128)(2,1)S(1)}, u32[]{:S(2)}, u32[]{:S(2)}) collective-permute-start(bf16[4,3,64,128]{3,2,1,0:T(8,128)(2,1)S(1)} %pad_maximum_fusion.4), channel_id=1, source_target_pairs={{8,0},{16,8},{24,16},{32,24},{40,32},{48,40},{56,48},{9,1},{17,9},... | collective-permute-start | bytes 589832 | tf_op jit(solution)/shard_map/ppermute | solution.py:163
  55.8 24.4 %collective-permute-start.3 = (bf16[2,2,3,128,128]{4,3,2,1,0:T(8,128)(2,1)S(1)}, bf16[2,2,3,128,128]{4,3,2,1,0:T(8,128)(2,1)S(1)}, u32[]{:S(2)}, u32[]{:S(2)}) collective-permute-start(bf16[2,2,3,128,128]{4,3,2,1,0:T(8,128)(2,1)S(1)} %collective-permute-done.1.refs_1_), channel_id=1, source_target_pairs={{0,64},{64,0},{128,192},{192,128},{256,320},{320,256},{384,448},{4... | collective-permute-start | bytes 1179656 | tf_op jit(solution)/shard_map/ppermute | solution.py:175
  59.9 20.3 %collective-permute-start.4 = (bf16[2,2,3,128,128]{4,3,2,1,0:T(8,128)(2,1)S(1)}, bf16[2,2,3,128,128]{4,3,2,1,0:T(8,128)(2,1)S(1)}, u32[]{:S(2)}, u32[]{:S(2)}) collective-permute-start(bf16[2,2,3,128,128]{4,3,2,1,0:T(8,128)(2,1)S(1)} %collective-permute-done.2.refs_3_), channel_id=1, source_target_pairs={{0,64},{64,0},{128,192},{192,128},{256,320},{320,256},{384,448},{4... | collective-permute-start | bytes 1179656 | tf_op jit(solution)/shard_map/ppermute | solution.py:175
  65.4 15.2 %copy-start.1 = (bf16[2,2,3,128,128]{4,3,2,1,0:T(8,128)(2,1)}, bf16[2,2,3,128,128]{4,3,2,1,0:T(8,128)(2,1)S(1)}, u32[]{:S(2)}) copy-start(bf16[2,2,3,128,128]{4,3,2,1,0:T(8,128)(2,1)S(1)} %collective-permute-done.5.refs_5_) | copy-start | bytes 1179652
  65.4 9.1 %collective-permute-start.7 = (bf16[1,2,3,128,128]{4,3,2,1,0:T(8,128)(2,1)S(1)}, bf16[1,2,3,128,128]{4,3,2,1,0:T(8,128)(2,1)S(1)}, u32[]{:S(2)}, u32[]{:S(2)}) collective-permute-start(bf16[1,2,3,128,128]{4,3,2,1,0:T(8,128)(2,1)S(1)} %slice.36), channel_id=1, source_target_pairs={{0,128},{64,960},{128,256},{192,64},{256,384},{320,192},{384,512},... | collective-permute-start | bytes 589832 | tf_op jit(solution)/shard_map/ppermute | solution.py:178
  69.9 10.6 %collective-permute-start.6 = (bf16[2,2,3,128,128]{4,3,2,1,0:T(8,128)(2,1)S(1)}, bf16[2,2,3,128,128]{4,3,2,1,0:T(8,128)(2,1)S(1)}, u32[]{:S(2)}, u32[]{:S(2)}) collective-permute-start(bf16[2,2,3,128,128]{4,3,2,1,0:T(8,128)(2,1)S(1)} %collective-permute-done.5.refs_5_), channel_id=1, source_target_pairs={{0,64},{64,0},{128,192},{192,128},{256,320},{320,256},{384,448},{4... | collective-permute-start | bytes 1179656 | tf_op jit(solution)/shard_map/ppermute | solution.py:175
  73.2 7.3 %copy-start.2 = (bf16[4,3,64,128]{3,2,1,0:T(8,128)(2,1)}, bf16[4,3,64,128]{3,2,1,0:T(8,128)(2,1)S(1)}, u32[]{:S(2)}) copy-start(bf16[4,3,64,128]{3,2,1,0:T(8,128)(2,1)S(1)} %collective-permute-done.10.refs_11_.right_ref) | copy-start | bytes 589828
  73.2 7.0 %collective-permute-start.9 = (bf16[4,3,64,128]{3,2,1,0:T(8,128)(2,1)}, bf16[4,3,64,128]{3,2,1,0:T(8,128)(2,1)S(1)}, u32[]{:S(2)}, u32[]{:S(2)}) collective-permute-start(bf16[4,3,64,128]{3,2,1,0:T(8,128)(2,1)} %pad_maximum_fusion.3), channel_id=1, source_target_pairs={{0,8},{8,16},{16,24},{24,32},{32,40},{40,48},{48,56},{1,9},{9,17},... | collective-permute-start | bytes 589832 | tf_op jit(solution)/shard_map/ppermute | solution.py:163
  74.5 6.0 %copy-start.12 = (bf16[1,2,3,128,128]{4,3,2,1,0:T(8,128)(2,1)}, bf16[1,2,3,128,128]{4,3,2,1,0:T(8,128)(2,1)S(1)}, u32[]{:S(2)}) copy-start(bf16[1,2,3,128,128]{4,3,2,1,0:T(8,128)(2,1)S(1)} %collective-permute-done.7.refs_7_) | copy-start | bytes 589828
  74.5 6.0 %collective-permute-start.8 = (bf16[1,2,3,128,128]{4,3,2,1,0:T(8,128)(2,1)S(1)}, bf16[1,2,3,128,128]{4,3,2,1,0:T(8,128)(2,1)}, u32[]{:S(2)}, u32[]{:S(2)}) collective-permute-start(bf16[1,2,3,128,128]{4,3,2,1,0:T(8,128)(2,1)S(1)} %collective-permute-done.7.refs_7_), channel_id=1, source_target_pairs={{0,64},{64,0},{128,192},{192,128},{256,320},{320,256},{384,448},{4... | collective-permute-start | bytes 589832 | tf_op jit(solution)/shard_map/ppermute | solution.py:175
  80.2 0.7 copy-start.3
  80.2 0.8 copy-start.7
  80.2 1.0 copy-start.8
  81.2 0.7 copy-start.9
  88.1 24.2 %collective-permute-start.11 = (f32[3,2,128]{2,1,0:T(2,128)}, f32[3,2,128]{2,1,0:T(2,128)S(1)}, u32[]{:S(2)}, u32[]{:S(2)}) collective-permute-start(f32[3,2,128]{2,1,0:T(2,128)} %get-tuple-element.15), channel_id=1, source_target_pairs={{0,8},{8,16},{16,24},{24,32},{32,40},{40,48},{48,56},{1,9},{9,17},... | collective-permute-start | bytes 9224 | tf_op jit(solution)/shard_map/ppermute | solution.py:163
  91.2 21.1 %collective-permute-start.12 = (f32[3,2,128]{2,1,0:T(2,128)}, f32[3,2,128]{2,1,0:T(2,128)S(1)}, u32[]{:S(2)}, u32[]{:S(2)}) collective-permute-start(f32[3,2,128]{2,1,0:T(2,128)} %get-tuple-element.15), channel_id=1, source_target_pairs={{8,0},{16,8},{24,16},{32,24},{40,32},{48,40},{56,48},{9,1},{17,9},... | collective-permute-start | bytes 9224 | tf_op jit(solution)/shard_map/ppermute | solution.py:163
  112.4 0.6 copy-start.13
  112.4 0.6 copy-start.14
Sparse Core Ops, SparseCore 0:
  10.7 59.9 all-gather.3

commit v4 on v3

--- a/solution.py
+++ b/solution.py
@@ -163,7 +163,7 @@
     return lax.ppermute(last, axis, up), lax.ppermute(first, axis, down)
 
 
-def band_units(own, axis, aside):
+def band_units(own, axis, work, state, later):
     size = lax.axis_size(axis)
     index = lax.axis_index(axis)
     pairs = size // 2
@@ -180,8 +180,12 @@
     held = jnp.stack((own, handed(own)))
     units, order = [held], [index, index ^ 1]
     for s in range(1, pairs // 2 + 1):
-        if s == 3:
-            held, aside = lax.optimization_barrier((held, aside))
+        if s > 1:
+            for fill in work[s - 2:s - 1]:
+                state = fill(state)
+            held, state = lax.optimization_barrier((held, state))
+        if s == 2:
+            held, later = lax.optimization_barrier((held, later))
         near = (index // 2 - (1 - 2 * side) * s) % pairs
         far = (index // 2 + (1 - 2 * side) * s) % pairs
         sides = [side, 1 - side]
@@ -190,7 +194,7 @@
         held = passed(held)
         units += [held, handed(held)]
         order += [2 * near + i for i in sides] + [2 * far + 1 - i for i in sides]
-    return units, jnp.stack(order).astype(jnp.int32), aside
+    return units, jnp.stack(order).astype(jnp.int32), state, later
 
 
 def row_bias(allowed, tile):
@@ -212,26 +216,37 @@
     q, k, v, g = (x.reshape(flat) for x in (query_rows, key_rows, value_rows, grad_out))
     asking = jnp.stack((q, g))
     keyed = jnp.stack((k, v))
-    all_asking = lax.all_gather(asking, "hb")
     four = (k, v, q, g)
     left, right = neighbours(
         jnp.stack([x[:, :tile] for x in four]), jnp.stack([x[:, rows - tile:] for x in four]), "wb"
     )
-    allowed = tile_masks(tile_radius, sel_tiles, sel_count)
+
     start = hb_index * dev_tiles
-    own_bias = row_bias(lax.dynamic_slice_in_dim(allowed, start, dev_tiles, 1), tile)
-    col_bias = row_bias(
-        jnp.swapaxes(lax.dynamic_slice_in_dim(allowed, start, dev_tiles, 2), 1, 2), tile
-    )
-    reach = tile_radius >= 1
-    edge_open = jnp.stack(
-        (reach & (wb_index >= 1), reach & (wb_index < lax.axis_size("wb") - 1)), axis=1
-    )
-    edge_bias = jnp.where(edge_open, 0.0, CLOSED).astype(jnp.float32)
-
-    units, order, (own_bias, col_bias, edge_bias) = band_units(
-        keyed, "hb", (own_bias, col_bias, edge_bias)
-    )
+
+    def masks(state):
+        reach = tile_radius >= 1
+        edge_open = jnp.stack(
+            (reach & (wb_index >= 1), reach & (wb_index < lax.axis_size("wb") - 1)), axis=1
+        )
+        edge_bias = jnp.where(edge_open, 0.0, CLOSED).astype(jnp.float32)
+        return {"allowed": tile_masks(tile_radius, sel_tiles, sel_count), "edge": edge_bias}
+
+    def own_rows(state):
+        own = lax.dynamic_slice_in_dim(state["allowed"], start, dev_tiles, 1)
+        return state | {"own": row_bias(own, tile)}
+
+    def own_cols(state):
+        own = lax.dynamic_slice_in_dim(state["allowed"], start, dev_tiles, 2)
+        return {
+            "edge": state["edge"], "own": state["own"],
+            "col": row_bias(jnp.swapaxes(own, 1, 2), tile),
+        }
+
+    units, order, state, late_asking = band_units(
+        keyed, "hb", (masks, own_rows, own_cols), {}, asking
+    )
+    own_bias, col_bias, edge_bias = state["own"], state["col"], state["edge"]
+    all_asking = lax.all_gather(late_asking, "hb")
 
     def per_head(shape):
         return pl.BlockSpec((1,) + shape, lambda h: (h,) + (0,) * len(shape))

time: 126 us -> 123 us (0.976)
  waiting for transfers between devices: 17.3 us -> 8.23 us
  starting transfers between devices: 48.9 us -> 53.1 us
  other arithmetic: 5.88 us -> 7.37 us
  local copies, waits for them, and re-layouts: 7.24 us -> 8.59 us
    ppermute x4, waiting for transfers between devices: 16.9 us -> 7.83 us  [passed(): return lax.ppermute(x, axis, step)]
    ppermute x5, starting transfers between devices: 29.5 us -> 34.5 us  [handed(): return lax.ppermute(x, axis, swap)]
    ppermute x4, starting transfers between devices: 6.99 us -> 5.18 us  [neighbours(): return (lax.ppermute(last, axis, up), lax.ppermute(first, axis, down))]
    another operation x2, local copies, waits for them, and re-layouts: 0.93 us -> 2.42 us  [on_device(): jnp.stack([x[:, :tile] for x in four])]
    unnamed x32 -> x28, local copies, waits for them, and re-layouts: 3.5 us -> 3.42 us
  transfers between devices with their start and end apart: 14 -> 14, of which waited for: 4 -> 3; matrix products, arithmetic and copies ran while one was open for 8% -> 11% of each run, Pallas kernels for 5% -> 5%
where the time goes in v4:
time: 123 us; the launch traced here: 122 us
  starting transfers between devices  53.1 us (43%)
  blocking collectives  19 us (15%)
  between operations  14.5 us (12%)
  Pallas kernels  11.4 us (9%)
  local copies, waits for them, and re-layouts  8.59 us (7%)
  waiting for transfers between devices  8.23 us (7%)
  other arithmetic  7.37 us (6%)
    ppermute x5, starting transfers between devices, handed(): return lax.ppermute(x, axis, swap)  34.5 us
    all_gather x1, blocking collectives, on_device(): all_stats = lax.all_gather(stats, 'hb')  19 us
    ppermute x4, starting transfers between devices, passed(): return lax.ppermute(x, axis, step)  13.4 us
    ppermute x4, waiting for transfers between devices, passed(): return lax.ppermute(x, axis, step)  7.83 us
    pallas_call x1, Pallas kernels, on_device(): pl.pallas_call(functools.partial(query_side, factor=factor, tile=tile), g...  6.18 us
    pallas_call x1, Pallas kernels, on_device(): pl.pallas_call(functools.partial(key_side, factor=factor, tile=tile), gri...  5.22 us
    ppermute x4, starting transfers between devices, neighbours(): return (lax.ppermute(last, axis, up), lax.ppermute(first, axis, down))  5.18 us
    unnamed x28, local copies, waits for them, and re-layouts  3.42 us
  transfers between devices with their start and end apart: 14, of which 3 were waited for; matrix products, arithmetic and copies ran while one was open for 11% of the time, Pallas kernels for 5%

profile of v4, /device:TPU:1, one launch (start us, length us, event | category | flops | bytes accessed | tf_op | source)
XLA Modules:
  0.0 122.2 jit_solution(10310651409819648838)
XLA Ops:
  7.2 0.0 all-gather.4.cloned.1.call-start
  7.2 1.0 fusion.3
  8.2 0.0 copy-start.4
  8.2 16.0 %collective-permute-start = (bf16[2,3,128,128]{3,2,1,0:T(8,128)(2,1)S(1)}, bf16[2,3,128,128]{3,2,1,0:T(8,128)(2,1)S(1)}, u32[]{:S(2)}, u32[]{:S(2)}) collective-permute-start(bf16[2,3,128,128]{3,2,1,0:T(8,128)(2,1)S(1)} %get-tuple-element.50.own_ref), channel_id=1, source_target_pairs={{0,64},{64,0},{128,192},{192,128},{256,320},{320,256},{384,448},{4... | collective-permute-start | bytes 589832 | tf_op jit(solution)/shard_map/ppermute | solution.py:175
  24.2 0.7 and_bitcast_fusion.1
  24.9 0.1 copy.36
  25.0 0.1 copy.37
  25.1 0.8 copy.33
  25.9 0.8 copy.34
  26.7 0.1 lt.81
  26.7 0.1 iota_compare_fusion.1
  26.8 0.2 fusion.1
  27.0 0.1 abs_add_fusion
  27.1 0.0 collective-permute-done
  27.1 1.9 %collective-permute-start.1 = (bf16[2,2,3,128,128]{4,3,2,1,0:T(8,128)(2,1)S(1)}, bf16[2,2,3,128,128]{4,3,2,1,0:T(8,128)(2,1)S(1)}, u32[]{:S(2)}, u32[]{:S(2)}) collective-permute-start(bf16[2,2,3,128,128]{4,3,2,1,0:T(8,128)(2,1)S(1)} %pad_maximum_fusion.refs_0_), channel_id=1, source_target_pairs={{0,128},{64,960},{128,256},{192,64},{256,384},{320,192},{384,512},... | collective-permute-start | bytes 1179656 | tf_op jit(solution)/shard_map/ppermute | solution.py:178
  29.1 0.7 add_select_fusion.edge_ref
  29.7 0.1 copy.35
  29.8 1.6 %pad_maximum_fusion.2.refs_9_ = bf16[2,3,128,128]{3,2,1,0:T(8,128)(2,1)} fusion(bf16[1,3,128,128]{3,2,1,0:T(8,128)(2,1)} %bitcast.70, bf16[1,3,128,128]{3,2,1,0:T(8,128)(2,1)} %bitcast.72), kind=kLoop, calls=%fused_computation.2 | loop fusion | flops 98304 | bytes 393216 | tf_op jit(solution)/shard_map/stack | solution.py:217
  31.5 0.7 compare_or_fusion
  32.2 3.8 %collective-permute-done.1.refs_1_ = bf16[2,2,3,128,128]{4,3,2,1,0:T(8,128)(2,1)S(1)} collective-permute-done((bf16[2,2,3,128,128]{4,3,2,1,0:T(8,128)(2,1)S(1)}, bf16[2,2,3,128,128]{4,3,2,1,0:T(8,128)(2,1)S(1)}, u32[]{:S(2)}, u32[]{:S(2)}) %collective-permute-start.1) | collective-permute-done | bytes 393248 | tf_op jit(solution)/shard_map/ppermute | solution.py:178
  36.0 0.0 all-gather.4.cloned.1.call-update
  36.0 2.8 %collective-permute-start.2 = (bf16[2,2,3,128,128]{4,3,2,1,0:T(8,128)(2,1)S(1)}, bf16[2,2,3,128,128]{4,3,2,1,0:T(8,128)(2,1)S(1)}, u32[]{:S(2)}, u32[]{:S(2)}) collective-permute-start(bf16[2,2,3,128,128]{4,3,2,1,0:T(8,128)(2,1)S(1)} %collective-permute-done.1.refs_1_), channel_id=1, source_target_pairs={{0,128},{64,960},{128,256},{192,64},{256,384},{320,192},{384,512},... | collective-permute-start | bytes 1179656 | tf_op jit(solution)/shard_map/ppermute | solution.py:178
  38.8 0.9 slice_bitcast_fusion.2
  39.7 0.1 dynamic-slice_select_fusion
  39.8 0.1 copy.38
  39.9 0.1 broadcast_in_dim.48
  40.0 0.7 reshape.165.refs_12_
  40.7 4.1 %collective-permute-done.2.refs_3_ = bf16[2,2,3,128,128]{4,3,2,1,0:T(8,128)(2,1)S(1)} collective-permute-done((bf16[2,2,3,128,128]{4,3,2,1,0:T(8,128)(2,1)S(1)}, bf16[2,2,3,128,128]{4,3,2,1,0:T(8,128)(2,1)S(1)}, u32[]{:S(2)}, u32[]{:S(2)}) %collective-permute-start.2) | collective-permute-done | bytes 393248 | tf_op jit(solution)/shard_map/ppermute | solution.py:178
  44.8 3.7 %collective-permute-start.3 = (bf16[2,2,3,128,128]{4,3,2,1,0:T(8,128)(2,1)S(1)}, bf16[2,2,3,128,128]{4,3,2,1,0:T(8,128)(2,1)S(1)}, u32[]{:S(2)}, u32[]{:S(2)}) collective-permute-start(bf16[2,2,3,128,128]{4,3,2,1,0:T(8,128)(2,1)S(1)} %collective-permute-done.2.refs_3_), channel_id=1, source_target_pairs={{0,128},{64,960},{128,256},{192,64},{256,384},{320,192},{384,512},... | collective-permute-start | bytes 1179656 | tf_op jit(solution)/shard_map/ppermute | solution.py:178
  48.5 1.5 %slice_bitcast_fusion = (bf16[1,3,64,128]{3,2,1,0:T(8,128)(2,1)S(1)}, bf16[1,3,64,128]{3,2,1,0:T(8,128)(2,1)}, bf16[1,3,64,128]{3,2,1,0:T(8,128)(2,1)}, bf16[1,3,64,128]{3,2,1,0:T(8,128)(2,1)S(1)}) fusion(bf16[3,128,128]{2,1,0:T(8,128)(2,1)} %bitcast.71, bf16[3,128,128]{2,1,0:T(8,128)(2,1)} %bitcast.73), kind=kLoop, calls=%fused_computation.8 | loop fusion | bytes 393216 | tf_op jit(solution)/shard_map/stack | solution.py:221
  50.1 0.7 pad_maximum_fusion.4
  50.8 1.3 %collective-permute-start.10 = (bf16[4,3,64,128]{3,2,1,0:T(8,128)(2,1)}, bf16[4,3,64,128]{3,2,1,0:T(8,128)(2,1)S(1)}, u32[]{:S(2)}, u32[]{:S(2)}) collective-permute-start(bf16[4,3,64,128]{3,2,1,0:T(8,128)(2,1)} %pad_maximum_fusion.4), channel_id=1, source_target_pairs={{8,0},{16,8},{24,16},{32,24},{40,32},{48,40},{56,48},{9,1},{17,9},... | collective-permute-start | bytes 589832 | tf_op jit(solution)/shard_map/ppermute | solution.py:163
  52.1 4.2 %collective-permute-start.4 = (bf16[2,2,3,128,128]{4,3,2,1,0:T(8,128)(2,1)S(1)}, bf16[2,2,3,128,128]{4,3,2,1,0:T(8,128)(2,1)S(1)}, u32[]{:S(2)}, u32[]{:S(2)}) collective-permute-start(bf16[2,2,3,128,128]{4,3,2,1,0:T(8,128)(2,1)S(1)} %collective-permute-done.1.refs_1_), channel_id=1, source_target_pairs={{0,64},{64,0},{128,192},{192,128},{256,320},{320,256},{384,448},{4... | collective-permute-start | bytes 1179656 | tf_op jit(solution)/shard_map/ppermute | solution.py:175
  56.3 0.1 broadcast_in_dim.51
  56.4 0.7 reshape.166.bias_ref
  57.1 1.9 %collective-permute-start.5 = (bf16[2,2,3,128,128]{4,3,2,1,0:T(8,128)(2,1)S(1)}, bf16[2,2,3,128,128]{4,3,2,1,0:T(8,128)(2,1)S(1)}, u32[]{:S(2)}, u32[]{:S(2)}) collective-permute-start(bf16[2,2,3,128,128]{4,3,2,1,0:T(8,128)(2,1)S(1)} %collective-permute-done.2.refs_3_), channel_id=1, source_target_pairs={{0,64},{64,0},{128,192},{192,128},{256,320},{320,256},{384,448},{4... | collective-permute-start | bytes 1179656 | tf_op jit(solution)/shard_map/ppermute | solution.py:175
  59.1 0.0 collective-permute-done.3.refs_5_
  59.1 4.9 %collective-permute-start.7 = (bf16[1,2,3,128,128]{4,3,2,1,0:T(8,128)(2,1)S(1)}, bf16[1,2,3,128,128]{4,3,2,1,0:T(8,128)(2,1)S(1)}, u32[]{:S(2)}, u32[]{:S(2)}) collective-permute-start(bf16[1,2,3,128,128]{4,3,2,1,0:T(8,128)(2,1)S(1)} %slice.27), channel_id=1, source_target_pairs={{0,128},{64,960},{128,256},{192,64},{256,384},{320,192},{384,512},... | collective-permute-start | bytes 589832 | tf_op jit(solution)/shard_map/ppermute | solution.py:178
  64.0 4.9 %collective-permute-start.6 = (bf16[2,2,3,128,128]{4,3,2,1,0:T(8,128)(2,1)S(1)}, bf16[2,2,3,128,128]{4,3,2,1,0:T(8,128)(2,1)S(1)}, u32[]{:S(2)}, u32[]{:S(2)}) collective-permute-start(bf16[2,2,3,128,128]{4,3,2,1,0:T(8,128)(2,1)S(1)} %collective-permute-done.3.refs_5_), channel_id=1, source_target_pairs={{0,64},{64,0},{128,192},{192,128},{256,320},{320,256},{384,448},{4... | collective-permute-start | bytes 1179656 | tf_op jit(solution)/shard_map/ppermute | solution.py:175
  68.8 1.5 %pad_maximum_fusion.3 = bf16[4,3,64,128]{3,2,1,0:T(8,128)(2,1)} fusion(bf16[1,3,64,128]{3,2,1,0:T(8,128)(2,1)} %get-tuple-element.58, bf16[1,3,64,128]{3,2,1,0:T(8,128)(2,1)} %get-tuple-element.63, bf16[1,3,64,128]{3,2,1,0:T(8,128)(2,1)S(1)} %get-tuple-element.54, bf16[1,3,64,128]{3,2,1,0:T(8,128)(2,1)S(1)} %get-tuple-element.65), kind=kLoop, calls=%fused_computation.3 | loop fusion | flops 294912 | bytes 393216 | tf_op jit(solution)/shard_map/stack | solution.py:221
  70.4 0.0 collective-permute-done.10.refs_11_.right_ref
  70.4 1.3 %collective-permute-start.9 = (bf16[4,3,64,128]{3,2,1,0:T(8,128)(2,1)}, bf16[4,3,64,128]{3,2,1,0:T(8,128)(2,1)S(1)}, u32[]{:S(2)}, u32[]{:S(2)}) collective-permute-start(bf16[4,3,64,128]{3,2,1,0:T(8,128)(2,1)} %pad_maximum_fusion.3), channel_id=1, source_target_pairs={{0,8},{8,16},{16,24},{24,32},{32,40},{40,48},{48,56},{1,9},{9,17},... | collective-permute-start | bytes 589832 | tf_op jit(solution)/shard_map/ppermute | solution.py:163
  71.7 0.0 collective-permute-done.7.refs_7_
  71.7 7.5 %collective-permute-start.8 = (bf16[1,2,3,128,128]{4,3,2,1,0:T(8,128)(2,1)S(1)}, bf16[1,2,3,128,128]{4,3,2,1,0:T(8,128)(2,1)}, u32[]{:S(2)}, u32[]{:S(2)}) collective-permute-start(bf16[1,2,3,128,128]{4,3,2,1,0:T(8,128)(2,1)S(1)} %collective-permute-done.7.refs_7_), channel_id=1, source_target_pairs={{0,64},{64,0},{128,192},{192,128},{256,320},{320,256},{384,448},{4... | collective-permute-start | bytes 589832 | tf_op jit(solution)/shard_map/ppermute | solution.py:175
  79.3 0.6 stack.121.order_ref
  80.0 0.0 collective-permute-done.9.refs_10_.left_ref
  80.0 0.0 collective-permute-done.4.refs_2_
  80.0 0.0 collective-permute-done.5.refs_4_
  80.0 0.3 collective-permute-done.8.refs_8_
  80.4 0.0 collective-permute-done.6.refs_6_
  80.4 0.2 copy-done.3
  80.7 0.2 copy-done.7
  80.8 0.2 copy-done.8
  81.0 0.7 copy-done.9
  81.7 6.2 %query_side.1 = (bf16[3,128,128]{2,1,0:T(8,128)(2,1)}, f32[3,2,128]{2,1,0:T(2,128)}) custom-call(s32[16]{0:T(128)} %stack.121.order_ref, f32[3,2]{1,0:T(4,128)} %add_select_fusion.edge_ref, bf16[2,2,3,128,128]{4,3,2,1,0:T(8,128)(2,1)} %copy-done, bf16[2,2,3,128,128]{4,3,2,1,0:T(8,128)(2,1)} %copy-done.5, bf16[2,2,3,128,128]{4,3,2,1,0:T(8,128)(2,1)} %copy-done.7, ...), custom_call_target="tpu_custom_call" | custom-call | tf_op jit(solution)/shard_map/query_side/pallas_call | solution.py:265
  87.9 1.3 %collective-permute-start.11 = (f32[3,2,128]{2,1,0:T(2,128)}, f32[3,2,128]{2,1,0:T(2,128)S(1)}, u32[]{:S(2)}, u32[]{:S(2)}) collective-permute-start(f32[3,2,128]{2,1,0:T(2,128)} %get-tuple-element.33), channel_id=1, source_target_pairs={{0,8},{8,16},{16,24},{24,32},{32,40},{40,48},{48,56},{1,9},{9,17},... | collective-permute-start | bytes 9224 | tf_op jit(solution)/shard_map/ppermute | solution.py:163
  89.2 1.3 %collective-permute-start.12 = (f32[3,2,128]{2,1,0:T(2,128)}, f32[3,2,128]{2,1,0:T(2,128)S(1)}, u32[]{:S(2)}, u32[]{:S(2)}) collective-permute-start(f32[3,2,128]{2,1,0:T(2,128)} %get-tuple-element.33), channel_id=1, source_target_pairs={{8,0},{16,8},{24,16},{32,24},{40,32},{48,40},{56,48},{9,1},{17,9},... | collective-permute-start | bytes 9224 | tf_op jit(solution)/shard_map/ppermute | solution.py:163
  90.5 19.0 %all-gather.1 = f32[48,2,128]{2,1,0:T(2,128)} all-gather(f32[3,2,128]{2,1,0:T(2,128)} %get-tuple-element.33), channel_id=3, replica_groups=mesh['hb'=16,'wb'=8,'hd'=8] {'hb'}, dimensions={0}, use_global_device_ids=true | all-gather | bytes 52224 | tf_op jit(solution)/shard_map/all_gather | solution.py:274
  109.5 0.0 collective-permute-done.11.left_stats_ref
  109.5 0.0 collective-permute-done.12.right_stats_ref
  109.5 0.0 all-gather.4.cloned.1.call-done
  109.6 0.5 copy-done.11
  110.1 0.0 copy-done.12
  110.1 5.2 %key_side.1 = (bf16[3,128,128]{2,1,0:T(8,128)(2,1)}, bf16[3,128,128]{2,1,0:T(8,128)(2,1)}) custom-call(f32[3,2]{1,0:T(4,128)} %add_select_fusion.edge_ref, bf16[16,2,3,128,128]{4,3,2,1,0:T(8,128)(2,1)} %bitcast.65, f32[16,3,2,128]{3,2,1,0:T(2,128)} %bitcast.74, bf16[2,3,128,128]{3,2,1,0:T(8,128)(2,1)} %copy-done.4, bf16[4,3,64,128]{3,2,1,0:T(8,128)(2,1)} %copy-done.3, ...), custom_call_target="tpu_custom_call" | custom-call | tf_op jit(solution)/shard_map/key_side/pallas_call | solution.py:275
  (23 shorter events, 0.1 us)
Async XLA Ops:
  7.2 102.4 %all-gather.4.cloned.1.call-start = ((), (), s32[]{:S(2)}) async-start(), calls=%async_computation | async-start | bytes 3342336 | tf_op jit(solution)/shard_map/all_gather | solution.py:249
  8.2 79.7 %copy-start.4 = (bf16[2,3,128,128]{3,2,1,0:T(8,128)(2,1)}, bf16[2,3,128,128]{3,2,1,0:T(8,128)(2,1)S(1)}, u32[]{:S(2)}) copy-start(bf16[2,3,128,128]{3,2,1,0:T(8,128)(2,1)S(1)} %get-tuple-element.50.own_ref) | copy-start | bytes 589828
  8.2 18.9 %collective-permute-start = (bf16[2,3,128,128]{3,2,1,0:T(8,128)(2,1)S(1)}, bf16[2,3,128,128]{3,2,1,0:T(8,128)(2,1)S(1)}, u32[]{:S(2)}, u32[]{:S(2)}) collective-permute-start(bf16[2,3,128,128]{3,2,1,0:T(8,128)(2,1)S(1)} %get-tuple-element.50.own_ref), channel_id=1, source_target_pairs={{0,64},{64,0},{128,192},{192,128},{256,320},{320,256},{384,448},{4... | collective-permute-start | bytes 589832 | tf_op jit(solution)/shard_map/ppermute | solution.py:175
  27.1 53.3 %copy-start = (bf16[2,2,3,128,128]{4,3,2,1,0:T(8,128)(2,1)}, bf16[2,2,3,128,128]{4,3,2,1,0:T(8,128)(2,1)S(1)}, u32[]{:S(2)}) copy-start(bf16[2,2,3,128,128]{4,3,2,1,0:T(8,128)(2,1)S(1)} %pad_maximum_fusion.refs_0_) | copy-start | bytes 1179652
  27.1 8.8 %collective-permute-start.1 = (bf16[2,2,3,128,128]{4,3,2,1,0:T(8,128)(2,1)S(1)}, bf16[2,2,3,128,128]{4,3,2,1,0:T(8,128)(2,1)S(1)}, u32[]{:S(2)}, u32[]{:S(2)}) collective-permute-start(bf16[2,2,3,128,128]{4,3,2,1,0:T(8,128)(2,1)S(1)} %pad_maximum_fusion.refs_0_), channel_id=1, source_target_pairs={{0,128},{64,960},{128,256},{192,64},{256,384},{320,192},{384,512},... | collective-permute-start | bytes 1179656 | tf_op jit(solution)/shard_map/ppermute | solution.py:178
  36.0 44.4 %copy-start.5 = (bf16[2,2,3,128,128]{4,3,2,1,0:T(8,128)(2,1)}, bf16[2,2,3,128,128]{4,3,2,1,0:T(8,128)(2,1)S(1)}, u32[]{:S(2)}) copy-start(bf16[2,2,3,128,128]{4,3,2,1,0:T(8,128)(2,1)S(1)} %collective-permute-done.1.refs_1_) | copy-start | bytes 1179652
  36.0 8.8 %collective-permute-start.2 = (bf16[2,2,3,128,128]{4,3,2,1,0:T(8,128)(2,1)S(1)}, bf16[2,2,3,128,128]{4,3,2,1,0:T(8,128)(2,1)S(1)}, u32[]{:S(2)}, u32[]{:S(2)}) collective-permute-start(bf16[2,2,3,128,128]{4,3,2,1,0:T(8,128)(2,1)S(1)} %collective-permute-done.1.refs_1_), channel_id=1, source_target_pairs={{0,128},{64,960},{128,256},{192,64},{256,384},{320,192},{384,512},... | collective-permute-start | bytes 1179656 | tf_op jit(solution)/shard_map/ppermute | solution.py:178
  44.8 35.6 %copy-start.6 = (bf16[2,2,3,128,128]{4,3,2,1,0:T(8,128)(2,1)}, bf16[2,2,3,128,128]{4,3,2,1,0:T(8,128)(2,1)S(1)}, u32[]{:S(2)}) copy-start(bf16[2,2,3,128,128]{4,3,2,1,0:T(8,128)(2,1)S(1)} %collective-permute-done.2.refs_3_) | copy-start | bytes 1179652
  44.8 14.3 %collective-permute-start.3 = (bf16[2,2,3,128,128]{4,3,2,1,0:T(8,128)(2,1)S(1)}, bf16[2,2,3,128,128]{4,3,2,1,0:T(8,128)(2,1)S(1)}, u32[]{:S(2)}, u32[]{:S(2)}) collective-permute-start(bf16[2,2,3,128,128]{4,3,2,1,0:T(8,128)(2,1)S(1)} %collective-permute-done.2.refs_3_), channel_id=1, source_target_pairs={{0,128},{64,960},{128,256},{192,64},{256,384},{320,192},{384,512},... | collective-permute-start | bytes 1179656 | tf_op jit(solution)/shard_map/ppermute | solution.py:178
  50.8 19.6 %collective-permute-start.10 = (bf16[4,3,64,128]{3,2,1,0:T(8,128)(2,1)}, bf16[4,3,64,128]{3,2,1,0:T(8,128)(2,1)S(1)}, u32[]{:S(2)}, u32[]{:S(2)}) collective-permute-start(bf16[4,3,64,128]{3,2,1,0:T(8,128)(2,1)} %pad_maximum_fusion.4), channel_id=1, source_target_pairs={{8,0},{16,8},{24,16},{32,24},{40,32},{48,40},{56,48},{9,1},{17,9},... | collective-permute-start | bytes 589832 | tf_op jit(solution)/shard_map/ppermute | solution.py:163
  52.1 27.9 %collective-permute-start.4 = (bf16[2,2,3,128,128]{4,3,2,1,0:T(8,128)(2,1)S(1)}, bf16[2,2,3,128,128]{4,3,2,1,0:T(8,128)(2,1)S(1)}, u32[]{:S(2)}, u32[]{:S(2)}) collective-permute-start(bf16[2,2,3,128,128]{4,3,2,1,0:T(8,128)(2,1)S(1)} %collective-permute-done.1.refs_1_), channel_id=1, source_target_pairs={{0,64},{64,0},{128,192},{192,128},{256,320},{320,256},{384,448},{4... | collective-permute-start | bytes 1179656 | tf_op jit(solution)/shard_map/ppermute | solution.py:175
  57.1 22.9 %collective-permute-start.5 = (bf16[2,2,3,128,128]{4,3,2,1,0:T(8,128)(2,1)S(1)}, bf16[2,2,3,128,128]{4,3,2,1,0:T(8,128)(2,1)S(1)}, u32[]{:S(2)}, u32[]{:S(2)}) collective-permute-start(bf16[2,2,3,128,128]{4,3,2,1,0:T(8,128)(2,1)S(1)} %collective-permute-done.2.refs_3_), channel_id=1, source_target_pairs={{0,64},{64,0},{128,192},{192,128},{256,320},{320,256},{384,448},{4... | collective-permute-start | bytes 1179656 | tf_op jit(solution)/shard_map/ppermute | solution.py:175
  59.1 21.3 %copy-start.1 = (bf16[2,2,3,128,128]{4,3,2,1,0:T(8,128)(2,1)}, bf16[2,2,3,128,128]{4,3,2,1,0:T(8,128)(2,1)S(1)}, u32[]{:S(2)}) copy-start(bf16[2,2,3,128,128]{4,3,2,1,0:T(8,128)(2,1)S(1)} %collective-permute-done.3.refs_5_) | copy-start | bytes 1179652
  59.1 12.6 %collective-permute-start.7 = (bf16[1,2,3,128,128]{4,3,2,1,0:T(8,128)(2,1)S(1)}, bf16[1,2,3,128,128]{4,3,2,1,0:T(8,128)(2,1)S(1)}, u32[]{:S(2)}, u32[]{:S(2)}) collective-permute-start(bf16[1,2,3,128,128]{4,3,2,1,0:T(8,128)(2,1)S(1)} %slice.27), channel_id=1, source_target_pairs={{0,128},{64,960},{128,256},{192,64},{256,384},{320,192},{384,512},... | collective-permute-start | bytes 589832 | tf_op jit(solution)/shard_map/ppermute | solution.py:178
  64.0 16.4 %collective-permute-start.6 = (bf16[2,2,3,128,128]{4,3,2,1,0:T(8,128)(2,1)S(1)}, bf16[2,2,3,128,128]{4,3,2,1,0:T(8,128)(2,1)S(1)}, u32[]{:S(2)}, u32[]{:S(2)}) collective-permute-start(bf16[2,2,3,128,128]{4,3,2,1,0:T(8,128)(2,1)S(1)} %collective-permute-done.3.refs_5_), channel_id=1, source_target_pairs={{0,64},{64,0},{128,192},{192,128},{256,320},{320,256},{384,448},{4... | collective-permute-start | bytes 1179656 | tf_op jit(solution)/shard_map/ppermute | solution.py:175
  70.4 10.0 %copy-start.2 = (bf16[4,3,64,128]{3,2,1,0:T(8,128)(2,1)}, bf16[4,3,64,128]{3,2,1,0:T(8,128)(2,1)S(1)}, u32[]{:S(2)}) copy-start(bf16[4,3,64,128]{3,2,1,0:T(8,128)(2,1)S(1)} %collective-permute-done.10.refs_11_.right_ref) | copy-start | bytes 589828
  70.4 9.6 %collective-permute-start.9 = (bf16[4,3,64,128]{3,2,1,0:T(8,128)(2,1)}, bf16[4,3,64,128]{3,2,1,0:T(8,128)(2,1)S(1)}, u32[]{:S(2)}, u32[]{:S(2)}) collective-permute-start(bf16[4,3,64,128]{3,2,1,0:T(8,128)(2,1)} %pad_maximum_fusion.3), channel_id=1, source_target_pairs={{0,8},{8,16},{16,24},{24,32},{32,40},{40,48},{48,56},{1,9},{9,17},... | collective-permute-start | bytes 589832 | tf_op jit(solution)/shard_map/ppermute | solution.py:163
  71.7 8.7 %copy-start.10 = (bf16[1,2,3,128,128]{4,3,2,1,0:T(8,128)(2,1)}, bf16[1,2,3,128,128]{4,3,2,1,0:T(8,128)(2,1)S(1)}, u32[]{:S(2)}) copy-start(bf16[1,2,3,128,128]{4,3,2,1,0:T(8,128)(2,1)S(1)} %collective-permute-done.7.refs_7_) | copy-start | bytes 589828
  71.7 8.7 %collective-permute-start.8 = (bf16[1,2,3,128,128]{4,3,2,1,0:T(8,128)(2,1)S(1)}, bf16[1,2,3,128,128]{4,3,2,1,0:T(8,128)(2,1)}, u32[]{:S(2)}, u32[]{:S(2)}) collective-permute-start(bf16[1,2,3,128,128]{4,3,2,1,0:T(8,128)(2,1)S(1)} %collective-permute-done.7.refs_7_), channel_id=1, source_target_pairs={{0,64},{64,0},{128,192},{192,128},{256,320},{320,256},{384,448},{4... | collective-permute-start | bytes 589832 | tf_op jit(solution)/shard_map/ppermute | solution.py:175
  80.0 0.7 copy-start.3
  80.0 0.8 copy-start.7
  80.0 1.0 copy-start.8
  81.0 0.7 copy-start.9
  87.9 21.6 %collective-permute-start.11 = (f32[3,2,128]{2,1,0:T(2,128)}, f32[3,2,128]{2,1,0:T(2,128)S(1)}, u32[]{:S(2)}, u32[]{:S(2)}) collective-permute-start(f32[3,2,128]{2,1,0:T(2,128)} %get-tuple-element.33), channel_id=1, source_target_pairs={{0,8},{8,16},{16,24},{24,32},{32,40},{40,48},{48,56},{1,9},{9,17},... | collective-permute-start | bytes 9224 | tf_op jit(solution)/shard_map/ppermute | solution.py:163
  89.2 20.3 %collective-permute-start.12 = (f32[3,2,128]{2,1,0:T(2,128)}, f32[3,2,128]{2,1,0:T(2,128)S(1)}, u32[]{:S(2)}, u32[]{:S(2)}) collective-permute-start(f32[3,2,128]{2,1,0:T(2,128)} %get-tuple-element.33), channel_id=1, source_target_pairs={{8,0},{16,8},{24,16},{32,24},{40,32},{48,40},{56,48},{9,1},{17,9},... | collective-permute-start | bytes 9224 | tf_op jit(solution)/shard_map/ppermute | solution.py:163
  109.5 0.6 copy-start.11
  109.5 0.6 copy-start.12
Sparse Core Ops, SparseCore 0:
  36.1 46.8 all-gather.3

commit v5 on v2

v5 whole, which is shorter than its diff:
```python
import functools

import jax
import jax.numpy as jnp
from jax import lax
from jax.experimental import pallas as pl
from jax.experimental.pallas import tpu as pltpu
from jax.sharding import PartitionSpec as P

CLOSED = -1e30
VMEM_BYTES = 32 * 2**20
LOG2_E = 1.4426950408889634
NT = (((1,), (1,)), ((), ()))
NN = (((1,), (0,)), ((), ()))


def dot(a, b, dims):
    return lax.dot_general(a, b, dims, preferred_element_type=jnp.float32)


def as_row(col):
    n = col.shape[0]
    return jnp.transpose(jnp.broadcast_to(col, (n, n)))[0:1]


def query_side(
    edge_ref, band_ref, q_ref, g_ref, left_ref, right_ref, bias_ref, dq_ref, stats_ref, *,
    factor, tile
):
    for h in range(q_ref.shape[0]):
        query_head(
            h, edge_ref, band_ref, q_ref, g_ref, left_ref, right_ref, bias_ref, dq_ref,
            stats_ref, factor=factor, tile=tile
        )


def query_head(
    head, edge_ref, band_ref, q_ref, g_ref, left_ref, right_ref, bias_ref, dq_ref, stats_ref, *,
    factor, tile
):
    rows, dim = q_ref.shape[1:]
    keys = band_ref[:, 0, head].reshape(-1, dim)
    values = band_ref[:, 1, head].reshape(-1, dim)
    q = q_ref[head]
    g = g_ref[head]
    shaped = (rows // tile, tile, keys.shape[0])
    scores = dot(q, keys, NT) * (factor * LOG2_E)
    scores = (scores.reshape(shaped) + bias_ref[head][:, None, :]).reshape(rows, -1)
    edge_keys = (left_ref[0, head], right_ref[0, head])
    edge_values = (left_ref[1, head], right_ref[1, head])
    edge_q = (q[:tile], q[rows - tile:])
    edge_g = (g[:tile], g[rows - tile:])
    edge_scores = [
        dot(edge_q[i], edge_keys[i], NT) * (factor * LOG2_E) + edge_ref[head, i]
        for i in range(2)
    ]
    inner = rows - 2 * tile

    def spread(parts, fill):
        mid = [jnp.full((inner, 1), fill, jnp.float32)] if inner else []
        return jnp.concatenate([parts[0]] + mid + [parts[1]], axis=0)

    def own(x, i):
        return x[:tile] if i == 0 else x[rows - tile:]

    def row_sums(x):
        return jnp.sum(x, axis=1, keepdims=True)

    edge_top = spread([jnp.max(e, axis=1, keepdims=True) for e in edge_scores], CLOSED)
    top = jnp.maximum(jnp.max(scores, axis=1, keepdims=True), edge_top)
    powers = jnp.exp2(scores - top)
    edge_powers = [jnp.exp2(edge_scores[i] - own(top, i)) for i in range(2)]
    total = row_sums(powers) + spread([row_sums(e) for e in edge_powers], 0.0)
    slopes = dot(g, values, NT)
    edge_slopes = [dot(edge_g[i], edge_values[i], NT) for i in range(2)]
    scale = 1.0 / total
    weighted = row_sums(powers * slopes) + spread(
        [row_sums(edge_powers[i] * edge_slopes[i]) for i in range(2)], 0.0
    )
    delta = weighted * scale
    grad = (powers * (slopes - delta)).astype(jnp.bfloat16)
    dq = dot(grad, keys, NN)
    edge_dq = []
    for i in range(2):
        part = edge_powers[i] * (edge_slopes[i] - own(delta, i))
        edge_dq.append(dot(part.astype(jnp.bfloat16), edge_keys[i], NN))
    last = scale * factor
    dq_ref[head, :tile] = ((dq[:tile] + edge_dq[0]) * own(last, 0)).astype(jnp.bfloat16)
    if inner:
        middle = slice(tile, rows - tile)
        dq_ref[head, middle] = (dq[middle] * last[middle]).astype(jnp.bfloat16)
    dq_ref[head, rows - tile:] = ((dq[rows - tile:] + edge_dq[1]) * own(last, 1)).astype(jnp.bfloat16)
    stats_ref[head, 0:1] = as_row(top + jnp.log2(total))
    stats_ref[head, 1:2] = as_row(delta)


def key_side(
    edge_ref, band_ref, all_stats_ref, k_ref, v_ref, left_ref, right_ref, left_stats_ref,
    right_stats_ref, bias_ref, dk_ref, dv_ref, *, factor, tile
):
    for h in range(k_ref.shape[0]):
        key_head(
            h, edge_ref, band_ref, all_stats_ref, k_ref, v_ref, left_ref, right_ref,
            left_stats_ref, right_stats_ref, bias_ref, dk_ref, dv_ref, factor=factor, tile=tile
        )


def key_head(
    head, edge_ref, band_ref, all_stats_ref, k_ref, v_ref, left_ref, right_ref,
    left_stats_ref, right_stats_ref, bias_ref, dk_ref, dv_ref, *, factor, tile
):
    rows, dim = k_ref.shape[1:]
    bands = band_ref.shape[0]
    k = k_ref[head]
    v = v_ref[head]
    queries = band_ref[:, 2, head].reshape(-1, dim)
    cotan = band_ref[:, 3, head].reshape(-1, dim)
    scores = dot(k, queries, NT)
    slopes = dot(v, cotan, NT)
    grads, probs = [], []
    tiles = rows // tile
    for r in range(bands):
        at = slice(r * rows, (r + 1) * rows)
        offset = bias_ref[head][:, at] - all_stats_ref[r, head, 0:1]
        part = (scores[:, at] * (factor * LOG2_E)).reshape(tiles, tile, rows)
        prob = jnp.exp2(part + offset[:, None, :]).reshape(rows, rows)
        probs.append(prob.astype(jnp.bfloat16))
        grads.append((prob * (slopes[:, at] - all_stats_ref[r, head, 1:2])).astype(jnp.bfloat16))
    dk = dot(jnp.concatenate(grads, axis=1), queries, NN)
    dv = dot(jnp.concatenate(probs, axis=1), cotan, NN)
    edge_k = (k[:tile], k[rows - tile:])
    edge_v = (v[:tile], v[rows - tile:])
    edge_stats = (left_stats_ref[head][:, rows - tile:], right_stats_ref[head][:, :tile])
    halos = (left_ref, right_ref)
    edge_dk, edge_dv = [], []
    for i in range(2):
        q_edge = halos[i][2, head]
        g_edge = halos[i][3, head]
        stats = edge_stats[i]
        part = dot(edge_k[i], q_edge, NT) * (factor * LOG2_E)
        prob = jnp.exp2(part + (edge_ref[head, i] - stats[0:1]))
        grad = prob * (dot(edge_v[i], g_edge, NT) - stats[1:2])
        edge_dk.append(dot(grad.astype(jnp.bfloat16), q_edge, NN))
        edge_dv.append(dot(prob.astype(jnp.bfloat16), g_edge, NN))
    for ref, whole, edge, last in ((dk_ref, dk, edge_dk, factor), (dv_ref, dv, edge_dv, 1.0)):
        ref[head, :tile] = ((whole[:tile] + edge[0]) * last).astype(jnp.bfloat16)
        if rows > 2 * tile:
            ref[head, tile:rows - tile] = (whole[tile:rows - tile] * last).astype(jnp.bfloat16)
        ref[head, rows - tile:] = ((whole[rows - tile:] + edge[1]) * last).astype(jnp.bfloat16)


def tile_masks(tile_radius, sel_tiles, sel_count):
    band_rows, band_cols, picks = sel_tiles.shape
    tile_total = band_rows * band_cols
    tile_index = jnp.arange(tile_total, dtype=jnp.int32)
    row_of = tile_index // band_cols
    col_of = tile_index % band_cols
    spread = jnp.abs(row_of[:, None] - row_of[None, :]) + jnp.abs(col_of[:, None] - col_of[None, :])
    nearby = spread[None] <= tile_radius[:, None, None]
    live_pick = jnp.arange(picks, dtype=jnp.int32)[None, :] < sel_count.reshape(tile_total, 1)
    matches = (sel_tiles.reshape(tile_total, picks, 1) == tile_index[None, None, :]) & live_pick[
        :, :, None
    ]
    return nearby | jnp.any(matches, axis=1)[None]


def neighbours(first, last, axis):
    size = lax.axis_size(axis)
    up = [(i, i + 1) for i in range(size - 1)]
    down = [(i + 1, i) for i in range(size - 1)]
    return lax.ppermute(last, axis, up), lax.ppermute(first, axis, down)


def row_bias(allowed, tile):
    bias = jnp.where(allowed, 0.0, CLOSED).astype(jnp.float32)
    heads, own, others = bias.shape
    wide = jnp.broadcast_to(bias[..., None], (heads, own, others, tile))
    return wide.reshape(heads, own, others * tile)


def on_device(query_rows, key_rows, value_rows, grad_out, sel_tiles, sel_count, tile_radius):
    heads, tile_rows, tile_cols, tile, dim = query_rows.shape
    dev_tiles = tile_rows * tile_cols
    rows = dev_tiles * tile
    factor = dim ** (-0.5)
    hb_index = lax.axis_index("hb")
    wb_index = lax.axis_index("wb")
    bands = lax.axis_size("hb")
    flat = (heads, rows, dim)
    q, k, v, g = (x.reshape(flat) for x in (query_rows, key_rows, value_rows, grad_out))
    four = (k, v, q, g)
    band = lax.all_gather(jnp.stack(four), "hb")
    left, right = neighbours(
        jnp.stack([x[:, :tile] for x in four]), jnp.stack([x[:, rows - tile:] for x in four]), "wb"
    )
    allowed = tile_masks(tile_radius, sel_tiles, sel_count)
    start = hb_index * dev_tiles
    own_bias = row_bias(lax.dynamic_slice_in_dim(allowed, start, dev_tiles, 1), tile)
    col_bias = row_bias(
        jnp.swapaxes(lax.dynamic_slice_in_dim(allowed, start, dev_tiles, 2), 1, 2), tile
    )
    reach = tile_radius >= 1
    edge_open = jnp.stack(
        (reach & (wb_index >= 1), reach & (wb_index < lax.axis_size("wb") - 1)), axis=1
    )
    edge_bias = jnp.where(edge_open, 0.0, CLOSED).astype(jnp.float32)

    smem = pl.BlockSpec(memory_space=pltpu.SMEM)
    near = pl.BlockSpec(memory_space=pltpu.VMEM)
    half = jax.ShapeDtypeStruct(flat, jnp.bfloat16)
    params = pltpu.CompilerParams(vmem_limit_bytes=VMEM_BYTES)
    dq, stats = pl.pallas_call(
        functools.partial(query_side, factor=factor, tile=tile),
        in_specs=[smem] + [near] * 6,
        out_specs=[near, near],
        out_shape=[half, jax.ShapeDtypeStruct((heads, 2, rows), jnp.float32)],
        compiler_params=params,
        name="query_side",
    )(edge_bias, band, q, g, left, right, own_bias)
    all_stats = lax.all_gather(stats, "hb")
    left_stats, right_stats = neighbours(stats, stats, "wb")
    dk, dv = pl.pallas_call(
        functools.partial(key_side, factor=factor, tile=tile),
        in_specs=[smem] + [near] * 9,
        out_specs=[near, near],
        out_shape=[half, half],
        compiler_params=params,
        name="key_side",
    )(edge_bias, band, all_stats, k, v, left, right, left_stats, right_stats, col_bias)
    return tuple(x.reshape(query_rows.shape) for x in (dq, dk, dv))


def solution(mesh):
    banded = P("hd", "hb", "wb", None, None)
    return jax.shard_map(
        on_device,
        mesh=mesh,
        in_specs=(banded,) * 4 + (P(None, "wb", None), P(None, "wb"), P("hd")),
        out_specs=(banded,) * 3,
        check_vma=False,
    )
```

time: 117 us -> 117 us (level)
  local copies, waits for them, and re-layouts: 6.02 us -> 8.76 us
  Pallas kernels: 11.2 us -> 8.76 us
  waiting for transfers between devices: 51.8 us -> 53.6 us
  blocking collectives: 18.2 us -> 16.6 us
    unnamed x10 -> x12, local copies, waits for them, and re-layouts: 2.12 us -> 6.11 us
    pallas_call x2, Pallas kernels: 11.2 us -> 8.76 us  [the longest x1 4.53 us: on_device(): pl.pallas_call(functools.partial(query_side, factor=factor, tile=tile), i...]
    all_gather x1, blocking collectives: 18.2 us -> 16.6 us  [on_device(): all_stats = lax.all_gather(stats, 'hb')]
    reshape x2, local copies, waits for them, and re-layouts: 1.46 us -> 0.21 us  [row_bias(): return wide.reshape(heads, own, others * tile)]
  transfers between devices with their start and end apart: 5 -> 5, of which waited for: 1 -> 2; matrix products, arithmetic and copies ran while one was open for 7% -> 5% of each run, Pallas kernels for 0% -> 0%
where the time goes in v5:
time: 117 us; the launch traced here: 116 us
  waiting for transfers between devices  53.6 us (46%)
  blocking collectives  16.6 us (14%)
  between operations  14.2 us (12%)
  starting transfers between devices  9.89 us (8%)
  local copies, waits for them, and re-layouts  8.76 us (7%)
  Pallas kernels  8.76 us (7%)
  other arithmetic  3.84 us (3%)
    all_gather x1, waiting for transfers between devices, on_device(): band = lax.all_gather(jnp.stack(four), 'hb')  52.8 us
    all_gather x1, blocking collectives, on_device(): all_stats = lax.all_gather(stats, 'hb')  16.6 us
    ppermute x4, starting transfers between devices, neighbours(): return (lax.ppermute(last, axis, up), lax.ppermute(first, axis, down))  9.85 us
    unnamed x12, local copies, waits for them, and re-layouts  6.11 us
    pallas_call x1, Pallas kernels, on_device(): pl.pallas_call(functools.partial(query_side, factor=factor, tile=tile), i...  4.53 us
    pallas_call x1, Pallas kernels, on_device(): pl.pallas_call(functools.partial(key_side, factor=factor, tile=tile), in_...  4.23 us
  transfers between devices with their start and end apart: 5, of which 2 were waited for; matrix products, arithmetic and copies ran while one was open for 5% of the time, Pallas kernels for 0%

profile of v5, /device:TPU:1, one launch (start us, length us, event | category | flops | bytes accessed | tf_op | source)
XLA Modules:
  0.0 115.6 jit_solution(12209408948893296080)
XLA Ops:
  7.2 0.0 copy-start.3
  7.2 0.0 copy-start.4
  7.2 0.0 all-gather.4.cloned.1.call-start
  7.2 1.9 %pad_maximum_fusion = bf16[4,3,128,128]{3,2,1,0:T(8,128)(2,1)} fusion(bf16[1,3,128,128]{3,2,1,0:T(8,128)(2,1)} %bitcast.48, bf16[1,3,128,128]{3,2,1,0:T(8,128)(2,1)} %bitcast.51, bf16[1,3,128,128]{3,2,1,0:T(8,128)(2,1)} %bitcast.54, bf16[1,3,128,128]{3,2,1,0:T(8,128)(2,1)} %bitcast.57), kind=kLoop, calls=%fused_computation | loop fusion | flops 589824 | bytes 786432 | tf_op jit(solution)/shard_map/stack | solution.py:192
  9.1 0.0 all-gather.4.cloned.1.call-update
  9.1 0.9 slice_bitcast_fusion
  10.0 0.9 slice_bitcast_fusion.2
  11.0 4.1 %collective-permute-start = (bf16[4,3,64,128]{3,2,1,0:T(8,128)(2,1)S(1)}, bf16[4,3,64,128]{3,2,1,0:T(8,128)(2,1)S(1)}, u32[]{:S(2)}, u32[]{:S(2)}) collective-permute-start(bf16[4,3,64,128]{3,2,1,0:T(8,128)(2,1)S(1)} %pad_maximum_fusion.1), channel_id=1, source_target_pairs={{0,8},{8,16},{16,24},{24,32},{32,40},{40,48},{48,56},{1,9},{9,17},... | collective-permute-start | bytes 589832 | tf_op jit(solution)/shard_map/ppermute | solution.py:171
  15.2 1.3 %collective-permute-start.1 = (bf16[4,3,64,128]{3,2,1,0:T(8,128)(2,1)S(1)}, bf16[4,3,64,128]{3,2,1,0:T(8,128)(2,1)S(1)}, u32[]{:S(2)}, u32[]{:S(2)}) collective-permute-start(bf16[4,3,64,128]{3,2,1,0:T(8,128)(2,1)S(1)} %pad_maximum_fusion.2), channel_id=1, source_target_pairs={{8,0},{16,8},{24,16},{32,24},{40,32},{48,40},{56,48},{9,1},{17,9},... | collective-permute-start | bytes 589832 | tf_op jit(solution)/shard_map/ppermute | solution.py:171
  16.5 0.7 and_bitcast_fusion.1
  17.1 0.1 copy.34
  17.2 0.1 copy.33
  17.4 0.8 copy.35
  18.1 0.8 copy.36
  18.9 0.1 lt.35
  19.0 0.1 iota_compare_fusion.1
  19.1 0.2 fusion.1
  19.2 0.1 copy.37
  19.3 0.1 abs_add_fusion
  19.4 0.7 compare_or_fusion
  20.1 0.1 dynamic-slice_select_fusion
  20.2 0.1 copy.38
  20.3 0.1 broadcast_in_dim.48
  20.4 0.1 reshape.169.bias_ref
  20.6 0.1 broadcast_in_dim.51
  20.6 0.1 reshape.171.bias_ref
  20.7 0.1 add_select_fusion.edge_ref
  20.8 0.0 collective-permute-done.left_ref
  20.8 0.8 collective-permute-done.1.right_ref
  21.6 52.8 %all-gather.4.cloned.1.call-done = bf16[64,3,128,128]{3,2,1,0:T(8,128)(2,1)} async-done(((bf16[4,3,128,128]{3,2,1,0:T(8,128)(2,1)}), bf16[64,3,128,128]{3,2,1,0:T(8,128)(2,1)}) %all-gather.4.cloned.1.call-update) | async-done | bytes 6291472 | tf_op jit(solution)/shard_map/all_gather | solution.py:192
  74.4 0.0 copy-start
  74.4 2.8 %copy-done = bf16[64,3,128,128]{3,2,1,0:T(8,128)(2,1)S(1)} copy-done((bf16[64,3,128,128]{3,2,1,0:T(8,128)(2,1)S(1)}, bf16[64,3,128,128]{3,2,1,0:T(8,128)(2,1)}, u32[]{:S(2)}) %copy-start) | copy-done | bytes 6291480
  77.2 0.0 copy-start.1
  77.2 0.9 copy-done.1
  78.1 0.0 copy-start.2
  78.1 0.9 copy-done.2
  79.0 4.5 %query_side.1 = (bf16[3,128,128]{2,1,0:T(8,128)(2,1)}, f32[3,2,128]{2,1,0:T(2,128)S(1)}) custom-call(f32[3,2]{1,0:T(4,128)S(1)} %add_select_fusion.edge_ref, bf16[16,4,3,128,128]{4,3,2,1,0:T(8,128)(2,1)S(1)} %bitcast.46, bf16[3,128,128]{2,1,0:T(8,128)(2,1)S(1)} %bitcast.53, bf16[3,128,128]{2,1,0:T(8,128)(2,1)S(1)} %bitcast.50, ...), custom_call_target="tpu_custom_call" | custom-call | tf_op jit(solution)/shard_map/query_side/pallas_call | solution.py:212
  83.5 3.1 %collective-permute-start.2 = (f32[3,2,128]{2,1,0:T(2,128)S(1)}, f32[3,2,128]{2,1,0:T(2,128)S(1)}, u32[]{:S(2)}, u32[]{:S(2)}) collective-permute-start(f32[3,2,128]{2,1,0:T(2,128)S(1)} %get-tuple-element.8), channel_id=1, source_target_pairs={{0,8},{8,16},{16,24},{24,32},{32,40},{40,48},{48,56},{1,9},{9,17},... | collective-permute-start | bytes 9224 | tf_op jit(solution)/shard_map/ppermute | solution.py:171
  86.6 1.3 %collective-permute-start.3 = (f32[3,2,128]{2,1,0:T(2,128)S(1)}, f32[3,2,128]{2,1,0:T(2,128)S(1)}, u32[]{:S(2)}, u32[]{:S(2)}) collective-permute-start(f32[3,2,128]{2,1,0:T(2,128)S(1)} %get-tuple-element.8), channel_id=1, source_target_pairs={{8,0},{16,8},{24,16},{32,24},{40,32},{48,40},{56,48},{9,1},{17,9},... | collective-permute-start | bytes 9224 | tf_op jit(solution)/shard_map/ppermute | solution.py:171
  87.9 16.6 %all-gather.1 = f32[48,2,128]{2,1,0:T(2,128)S(1)} all-gather(f32[3,2,128]{2,1,0:T(2,128)S(1)} %get-tuple-element.8), channel_id=3, replica_groups=mesh['hb'=16,'wb'=8,'hd'=8] {'hb'}, dimensions={0}, use_global_device_ids=true | all-gather | bytes 52224 | tf_op jit(solution)/shard_map/all_gather | solution.py:220
  104.5 0.0 collective-permute-done.2.left_stats_ref
  104.5 0.0 collective-permute-done.3.right_stats_ref
  104.5 0.0 copy-done.3
  104.5 0.0 copy-done.4
  104.5 4.2 %key_side.1 = (bf16[3,128,128]{2,1,0:T(8,128)(2,1)}, bf16[3,128,128]{2,1,0:T(8,128)(2,1)}) custom-call(f32[3,2]{1,0:T(4,128)S(1)} %add_select_fusion.edge_ref, bf16[16,4,3,128,128]{4,3,2,1,0:T(8,128)(2,1)S(1)} %bitcast.47, f32[16,3,2,128]{3,2,1,0:T(2,128)S(1)} %bitcast.60, bf16[3,128,128]{2,1,0:T(8,128)(2,1)S(1)} %bitcast.59, ...), custom_call_target="tpu_custom_call" | custom-call | tf_op jit(solution)/shard_map/key_side/pallas_call | solution.py:222
  (4 shorter events, 0.1 us)
Async XLA Ops:
  7.2 97.3 %copy-start.3 = (bf16[3,1,2,64,128]{4,3,2,1,0:T(8,128)(2,1)S(1)}, bf16[3,1,2,64,128]{4,3,2,1,0:T(8,128)(2,1)}, u32[]{:S(2)}) copy-start(bf16[3,1,2,64,128]{4,3,2,1,0:T(8,128)(2,1)} %param.9) | copy-start | bytes 294916
  7.2 97.3 %copy-start.4 = (bf16[3,1,2,64,128]{4,3,2,1,0:T(8,128)(2,1)S(1)}, bf16[3,1,2,64,128]{4,3,2,1,0:T(8,128)(2,1)}, u32[]{:S(2)}) copy-start(bf16[3,1,2,64,128]{4,3,2,1,0:T(8,128)(2,1)} %param.8) | copy-start | bytes 294916
  7.2 67.2 %all-gather.4.cloned.1.call-start = ((), (), s32[]{:S(2)}) async-start(), calls=%async_computation | async-start | bytes 6684672 | tf_op jit(solution)/shard_map/all_gather | solution.py:192
  11.0 9.9 %collective-permute-start = (bf16[4,3,64,128]{3,2,1,0:T(8,128)(2,1)S(1)}, bf16[4,3,64,128]{3,2,1,0:T(8,128)(2,1)S(1)}, u32[]{:S(2)}, u32[]{:S(2)}) collective-permute-start(bf16[4,3,64,128]{3,2,1,0:T(8,128)(2,1)S(1)} %pad_maximum_fusion.1), channel_id=1, source_target_pairs={{0,8},{8,16},{16,24},{24,32},{32,40},{40,48},{48,56},{1,9},{9,17},... | collective-permute-start | bytes 589832 | tf_op jit(solution)/shard_map/ppermute | solution.py:171
  15.2 6.4 %collective-permute-start.1 = (bf16[4,3,64,128]{3,2,1,0:T(8,128)(2,1)S(1)}, bf16[4,3,64,128]{3,2,1,0:T(8,128)(2,1)S(1)}, u32[]{:S(2)}, u32[]{:S(2)}) collective-permute-start(bf16[4,3,64,128]{3,2,1,0:T(8,128)(2,1)S(1)} %pad_maximum_fusion.2), channel_id=1, source_target_pairs={{8,0},{16,8},{24,16},{32,24},{40,32},{48,40},{56,48},{9,1},{17,9},... | collective-permute-start | bytes 589832 | tf_op jit(solution)/shard_map/ppermute | solution.py:171
  74.4 2.8 %copy-start = (bf16[64,3,128,128]{3,2,1,0:T(8,128)(2,1)S(1)}, bf16[64,3,128,128]{3,2,1,0:T(8,128)(2,1)}, u32[]{:S(2)}) copy-start(bf16[64,3,128,128]{3,2,1,0:T(8,128)(2,1)} %all-gather.4.cloned.1.call-done) | copy-start | bytes 18874372
  77.2 0.9 copy-start.1
  78.1 0.9 copy-start.2
  83.5 21.0 %collective-permute-start.2 = (f32[3,2,128]{2,1,0:T(2,128)S(1)}, f32[3,2,128]{2,1,0:T(2,128)S(1)}, u32[]{:S(2)}, u32[]{:S(2)}) collective-permute-start(f32[3,2,128]{2,1,0:T(2,128)S(1)} %get-tuple-element.8), channel_id=1, source_target_pairs={{0,8},{8,16},{16,24},{24,32},{32,40},{40,48},{48,56},{1,9},{9,17},... | collective-permute-start | bytes 9224 | tf_op jit(solution)/shard_map/ppermute | solution.py:171
  86.6 17.9 %collective-permute-start.3 = (f32[3,2,128]{2,1,0:T(2,128)S(1)}, f32[3,2,128]{2,1,0:T(2,128)S(1)}, u32[]{:S(2)}, u32[]{:S(2)}) collective-permute-start(f32[3,2,128]{2,1,0:T(2,128)S(1)} %get-tuple-element.8), channel_id=1, source_target_pairs={{8,0},{16,8},{24,16},{32,24},{40,32},{48,40},{56,48},{9,1},{17,9},... | collective-permute-start | bytes 9224 | tf_op jit(solution)/shard_map/ppermute | solution.py:171
Sparse Core Ops, SparseCore 0:
  10.7 63.6 all-gather.3

commit v6 on v5

--- a/solution.py
+++ b/solution.py
@@ -24,25 +24,25 @@
 
 
 def query_side(
-    edge_ref, band_ref, q_ref, g_ref, left_ref, right_ref, bias_ref, dq_ref, stats_ref, *,
+    place_ref, edge_ref, band_ref, left_ref, right_ref, bias_ref, dq_ref, stats_ref, *,
     factor, tile
 ):
-    for h in range(q_ref.shape[0]):
+    for h in range(dq_ref.shape[0]):
         query_head(
-            h, edge_ref, band_ref, q_ref, g_ref, left_ref, right_ref, bias_ref, dq_ref,
-            stats_ref, factor=factor, tile=tile
+            h, place_ref, edge_ref, band_ref, left_ref, right_ref, bias_ref, dq_ref, stats_ref,
+            factor=factor, tile=tile
         )
 
 
 def query_head(
-    head, edge_ref, band_ref, q_ref, g_ref, left_ref, right_ref, bias_ref, dq_ref, stats_ref, *,
+    head, place_ref, edge_ref, band_ref, left_ref, right_ref, bias_ref, dq_ref, stats_ref, *,
     factor, tile
 ):
-    rows, dim = q_ref.shape[1:]
+    rows, dim = dq_ref.shape[1:]
     keys = band_ref[:, 0, head].reshape(-1, dim)
     values = band_ref[:, 1, head].reshape(-1, dim)
-    q = q_ref[head]
-    g = g_ref[head]
+    q = band_ref[place_ref[0], 2, head]
+    g = band_ref[place_ref[0], 3, head]
     shaped = (rows // tile, tile, keys.shape[0])
     scores = dot(q, keys, NT) * (factor * LOG2_E)
     scores = (scores.reshape(shaped) + bias_ref[head][:, None, :]).reshape(rows, -1)
@@ -95,24 +95,24 @@
 
 
 def key_side(
-    edge_ref, band_ref, all_stats_ref, k_ref, v_ref, left_ref, right_ref, left_stats_ref,
+    place_ref, edge_ref, band_ref, all_stats_ref, left_ref, right_ref, left_stats_ref,
     right_stats_ref, bias_ref, dk_ref, dv_ref, *, factor, tile
 ):
-    for h in range(k_ref.shape[0]):
+    for h in range(dk_ref.shape[0]):
         key_head(
-            h, edge_ref, band_ref, all_stats_ref, k_ref, v_ref, left_ref, right_ref,
+            h, place_ref, edge_ref, band_ref, all_stats_ref, left_ref, right_ref,
             left_stats_ref, right_stats_ref, bias_ref, dk_ref, dv_ref, factor=factor, tile=tile
         )
 
 
 def key_head(
-    head, edge_ref, band_ref, all_stats_ref, k_ref, v_ref, left_ref, right_ref,
+    head, place_ref, edge_ref, band_ref, all_stats_ref, left_ref, right_ref,
     left_stats_ref, right_stats_ref, bias_ref, dk_ref, dv_ref, *, factor, tile
 ):
-    rows, dim = k_ref.shape[1:]
+    rows, dim = dk_ref.shape[1:]
     bands = band_ref.shape[0]
-    k = k_ref[head]
-    v = v_ref[head]
+    k = band_ref[place_ref[0], 0, head]
+    v = band_ref[place_ref[0], 1, head]
     queries = band_ref[:, 2, head].reshape(-1, dim)
     cotan = band_ref[:, 3, head].reshape(-1, dim)
     scores = dot(k, queries, NT)
@@ -205,28 +205,31 @@
     )
     edge_bias = jnp.where(edge_open, 0.0, CLOSED).astype(jnp.float32)
 
+    place = hb_index.astype(jnp.int32)[None]
     smem = pl.BlockSpec(memory_space=pltpu.SMEM)
     near = pl.BlockSpec(memory_space=pltpu.VMEM)
     half = jax.ShapeDtypeStruct(flat, jnp.bfloat16)
     params = pltpu.CompilerParams(vmem_limit_bytes=VMEM_BYTES)
     dq, stats = pl.pallas_call(
         functools.partial(query_side, factor=factor, tile=tile),
-        in_specs=[smem] + [near] * 6,
+        in_specs=[smem, smem] + [near] * 4,
         out_specs=[near, near],
         out_shape=[half, jax.ShapeDtypeStruct((heads, 2, rows), jnp.float32)],
         compiler_params=params,
         name="query_side",
-    )(edge_bias, band, q, g, left, right, own_bias)
+    )(place, edge_bias, band, left, right, own_bias)
     all_stats = lax.all_gather(stats, "hb")
     left_stats, right_stats = neighbours(stats, stats, "wb")
     dk, dv = pl.pallas_call(
         functools.partial(key_side, factor=factor, tile=tile),
-        in_specs=[smem] + [near] * 9,
+        in_specs=[smem, smem] + [near] * 7,
         out_specs=[near, near],
         out_shape=[half, half],
         compiler_params=params,
         name="key_side",
-    )(edge_bias, band, all_stats, k, v, left, right, left_stats, right_stats, col_bias)
+    )(
+        place, edge_bias, band, all_stats, left, right, left_stats, right_stats, col_bias
+    )
     return tuple(x.reshape(query_rows.shape) for x in (dq, dk, dv))
 
 

time: 117 us -> 115 us (0.983)
  local copies, waits for them, and re-layouts: 8.76 us -> 6.96 us
    unnamed x12 -> x4, local copies, waits for them, and re-layouts: 6.11 us -> 4.32 us
where the time goes in v6:
time: 115 us; the launch traced here: 114 us
  waiting for transfers between devices  53.6 us (47%)
  blocking collectives  16.6 us (14%)
  between operations  14.2 us (12%)
  starting transfers between devices  9.9 us (9%)
  Pallas kernels  8.76 us (8%)
  local copies, waits for them, and re-layouts  6.96 us (6%)
  other arithmetic  3.8 us (3%)
    all_gather x1, waiting for transfers between devices, on_device(): band = lax.all_gather(jnp.stack(four), 'hb')  52.8 us
    all_gather x1, blocking collectives, on_device(): all_stats = lax.all_gather(stats, 'hb')  16.6 us
    ppermute x4, starting transfers between devices, neighbours(): return (lax.ppermute(last, axis, up), lax.ppermute(first, axis, down))  9.86 us
    pallas_call x1, Pallas kernels, on_device(): pl.pallas_call(functools.partial(query_side, factor=factor, tile=tile), i...  4.54 us
    unnamed x4, local copies, waits for them, and re-layouts  4.32 us
    pallas_call x1, Pallas kernels, on_device(): pl.pallas_call(functools.partial(key_side, factor=factor, tile=tile), in_...  4.22 us
  transfers between devices with their start and end apart: 5, of which 2 were waited for; matrix products, arithmetic and copies ran while one was open for 5% of the time, Pallas kernels for 0%

profile of v6, /device:TPU:1, one launch (start us, length us, event | category | flops | bytes accessed | tf_op | source)
XLA Modules:
  0.0 113.8 jit_solution(2091098375016995772)
XLA Ops:
  7.2 0.0 all-gather.4.cloned.1.call-start
  7.2 1.8 %pad_maximum_fusion = bf16[4,3,128,128]{3,2,1,0:T(8,128)(2,1)} fusion(bf16[1,3,128,128]{3,2,1,0:T(8,128)(2,1)} %bitcast.50, bf16[1,3,128,128]{3,2,1,0:T(8,128)(2,1)} %bitcast.52, bf16[1,3,128,128]{3,2,1,0:T(8,128)(2,1)} %bitcast.54, bf16[1,3,128,128]{3,2,1,0:T(8,128)(2,1)} %bitcast.56), kind=kLoop, calls=%fused_computation | loop fusion | flops 589824 | bytes 786432 | tf_op jit(solution)/shard_map/stack | solution.py:192
  9.1 0.0 all-gather.4.cloned.1.call-update
  9.1 0.9 slice_bitcast_fusion
  10.0 0.9 slice_bitcast_fusion.2
  10.9 4.1 %collective-permute-start = (bf16[4,3,64,128]{3,2,1,0:T(8,128)(2,1)S(1)}, bf16[4,3,64,128]{3,2,1,0:T(8,128)(2,1)S(1)}, u32[]{:S(2)}, u32[]{:S(2)}) collective-permute-start(bf16[4,3,64,128]{3,2,1,0:T(8,128)(2,1)S(1)} %pad_maximum_fusion.1), channel_id=1, source_target_pairs={{0,8},{8,16},{16,24},{24,32},{32,40},{40,48},{48,56},{1,9},{9,17},... | collective-permute-start | bytes 589832 | tf_op jit(solution)/shard_map/ppermute | solution.py:171
  15.1 1.3 %collective-permute-start.1 = (bf16[4,3,64,128]{3,2,1,0:T(8,128)(2,1)S(1)}, bf16[4,3,64,128]{3,2,1,0:T(8,128)(2,1)S(1)}, u32[]{:S(2)}, u32[]{:S(2)}) collective-permute-start(bf16[4,3,64,128]{3,2,1,0:T(8,128)(2,1)S(1)} %pad_maximum_fusion.2), channel_id=1, source_target_pairs={{8,0},{16,8},{24,16},{32,24},{40,32},{48,40},{56,48},{9,1},{17,9},... | collective-permute-start | bytes 589832 | tf_op jit(solution)/shard_map/ppermute | solution.py:171
  16.4 0.7 and_bitcast_fusion.1
  17.1 0.1 copy.34
  17.2 0.1 copy.33
  17.3 0.8 copy.35
  18.1 0.8 copy.36
  18.8 0.1 lt.35
  18.9 0.1 iota_compare_fusion.1
  19.0 0.2 fusion.1
  19.2 0.1 copy.37
  19.3 0.1 abs_add_fusion
  19.3 0.7 compare_or_fusion
  20.1 0.1 dynamic-slice_select_fusion
  20.2 0.1 copy.38
  20.3 0.1 broadcast_in_dim.52
  20.4 0.1 reshape.169.bias_ref
  20.5 0.1 broadcast_in_dim.55
  20.6 0.1 reshape.171.bias_ref
  20.7 0.1 add_select_fusion.edge_ref
  20.8 0.0 collective-permute-done.left_ref
  20.8 0.8 collective-permute-done.1.right_ref
  21.5 52.8 %all-gather.4.cloned.1.call-done = bf16[64,3,128,128]{3,2,1,0:T(8,128)(2,1)} async-done(((bf16[4,3,128,128]{3,2,1,0:T(8,128)(2,1)}), bf16[64,3,128,128]{3,2,1,0:T(8,128)(2,1)}) %all-gather.4.cloned.1.call-update) | async-done | bytes 6291472 | tf_op jit(solution)/shard_map/all_gather | solution.py:192
  74.4 0.0 copy-start
  74.4 2.8 %copy-done = bf16[64,3,128,128]{3,2,1,0:T(8,128)(2,1)S(1)} copy-done((bf16[64,3,128,128]{3,2,1,0:T(8,128)(2,1)S(1)}, bf16[64,3,128,128]{3,2,1,0:T(8,128)(2,1)}, u32[]{:S(2)}) %copy-start) | copy-done | bytes 6291480
  77.1 4.5 %query_side.1 = (bf16[3,128,128]{2,1,0:T(8,128)(2,1)}, f32[3,2,128]{2,1,0:T(2,128)S(1)}) custom-call(s32[1]{0:T(128)} %bitcast.place_ref, f32[3,2]{1,0:T(4,128)S(1)} %add_select_fusion.edge_ref, bf16[16,4,3,128,128]{4,3,2,1,0:T(8,128)(2,1)S(1)} %bitcast.47, bf16[4,3,64,128]{3,2,1,0:T(8,128)(2,1)S(1)} %collective-permute-done.left_ref, ...), custom_call_target="tpu_custom_call" | custom-call | tf_op jit(solution)/shard_map/query_side/pallas_call | solution.py:213
  81.7 3.1 %collective-permute-start.2 = (f32[3,2,128]{2,1,0:T(2,128)S(1)}, f32[3,2,128]{2,1,0:T(2,128)S(1)}, u32[]{:S(2)}, u32[]{:S(2)}) collective-permute-start(f32[3,2,128]{2,1,0:T(2,128)S(1)} %get-tuple-element.8), channel_id=1, source_target_pairs={{0,8},{8,16},{16,24},{24,32},{32,40},{40,48},{48,56},{1,9},{9,17},... | collective-permute-start | bytes 9224 | tf_op jit(solution)/shard_map/ppermute | solution.py:171
  84.8 1.3 %collective-permute-start.3 = (f32[3,2,128]{2,1,0:T(2,128)S(1)}, f32[3,2,128]{2,1,0:T(2,128)S(1)}, u32[]{:S(2)}, u32[]{:S(2)}) collective-permute-start(f32[3,2,128]{2,1,0:T(2,128)S(1)} %get-tuple-element.8), channel_id=1, source_target_pairs={{8,0},{16,8},{24,16},{32,24},{40,32},{48,40},{56,48},{9,1},{17,9},... | collective-permute-start | bytes 9224 | tf_op jit(solution)/shard_map/ppermute | solution.py:171
  86.1 16.6 %all-gather.1 = f32[48,2,128]{2,1,0:T(2,128)S(1)} all-gather(f32[3,2,128]{2,1,0:T(2,128)S(1)} %get-tuple-element.8), channel_id=3, replica_groups=mesh['hb'=16,'wb'=8,'hd'=8] {'hb'}, dimensions={0}, use_global_device_ids=true | all-gather | bytes 52224 | tf_op jit(solution)/shard_map/all_gather | solution.py:221
  102.7 0.0 collective-permute-done.2.left_stats_ref
  102.7 0.0 collective-permute-done.3.right_stats_ref
  102.7 4.2 %key_side.1 = (bf16[3,128,128]{2,1,0:T(8,128)(2,1)}, bf16[3,128,128]{2,1,0:T(8,128)(2,1)}) custom-call(s32[1]{0:T(128)} %bitcast.place_ref, f32[3,2]{1,0:T(4,128)S(1)} %add_select_fusion.edge_ref, bf16[16,4,3,128,128]{4,3,2,1,0:T(8,128)(2,1)S(1)} %bitcast.48, f32[16,3,2,128]{3,2,1,0:T(2,128)S(1)} %bitcast.49, ...), custom_call_target="tpu_custom_call" | custom-call | tf_op jit(solution)/shard_map/key_side/pallas_call | solution.py:223
  (4 shorter events, 0.1 us)
Async XLA Ops:
  7.2 67.2 %all-gather.4.cloned.1.call-start = ((), (), s32[]{:S(2)}) async-start(), calls=%async_computation | async-start | bytes 6684672 | tf_op jit(solution)/shard_map/all_gather | solution.py:192
  10.9 9.9 %collective-permute-start = (bf16[4,3,64,128]{3,2,1,0:T(8,128)(2,1)S(1)}, bf16[4,3,64,128]{3,2,1,0:T(8,128)(2,1)S(1)}, u32[]{:S(2)}, u32[]{:S(2)}) collective-permute-start(bf16[4,3,64,128]{3,2,1,0:T(8,128)(2,1)S(1)} %pad_maximum_fusion.1), channel_id=1, source_target_pairs={{0,8},{8,16},{16,24},{24,32},{32,40},{40,48},{48,56},{1,9},{9,17},... | collective-permute-start | bytes 589832 | tf_op jit(solution)/shard_map/ppermute | solution.py:171
  15.1 6.4 %collective-permute-start.1 = (bf16[4,3,64,128]{3,2,1,0:T(8,128)(2,1)S(1)}, bf16[4,3,64,128]{3,2,1,0:T(8,128)(2,1)S(1)}, u32[]{:S(2)}, u32[]{:S(2)}) collective-permute-start(bf16[4,3,64,128]{3,2,1,0:T(8,128)(2,1)S(1)} %pad_maximum_fusion.2), channel_id=1, source_target_pairs={{8,0},{16,8},{24,16},{32,24},{40,32},{48,40},{56,48},{9,1},{17,9},... | collective-permute-start | bytes 589832 | tf_op jit(solution)/shard_map/ppermute | solution.py:171
  74.4 2.8 %copy-start = (bf16[64,3,128,128]{3,2,1,0:T(8,128)(2,1)S(1)}, bf16[64,3,128,128]{3,2,1,0:T(8,128)(2,1)}, u32[]{:S(2)}) copy-start(bf16[64,3,128,128]{3,2,1,0:T(8,128)(2,1)} %all-gather.4.cloned.1.call-done) | copy-start | bytes 18874372
  81.7 21.0 %collective-permute-start.2 = (f32[3,2,128]{2,1,0:T(2,128)S(1)}, f32[3,2,128]{2,1,0:T(2,128)S(1)}, u32[]{:S(2)}, u32[]{:S(2)}) collective-permute-start(f32[3,2,128]{2,1,0:T(2,128)S(1)} %get-tuple-element.8), channel_id=1, source_target_pairs={{0,8},{8,16},{16,24},{24,32},{32,40},{40,48},{48,56},{1,9},{9,17},... | collective-permute-start | bytes 9224 | tf_op jit(solution)/shard_map/ppermute | solution.py:171
  84.8 17.9 %collective-permute-start.3 = (f32[3,2,128]{2,1,0:T(2,128)S(1)}, f32[3,2,128]{2,1,0:T(2,128)S(1)}, u32[]{:S(2)}, u32[]{:S(2)}) collective-permute-start(f32[3,2,128]{2,1,0:T(2,128)S(1)} %get-tuple-element.8), channel_id=1, source_target_pairs={{8,0},{16,8},{24,16},{32,24},{40,32},{48,40},{56,48},{9,1},{17,9},... | collective-permute-start | bytes 9224 | tf_op jit(solution)/shard_map/ppermute | solution.py:171
Sparse Core Ops, SparseCore 0:
  10.7 63.6 all-gather.3

commit v7 on v5

--- a/solution.py
+++ b/solution.py
@@ -8,7 +8,7 @@
 from jax.sharding import PartitionSpec as P
 
 CLOSED = -1e30
-VMEM_BYTES = 32 * 2**20
+VMEM_BYTES = 47 * 2**20
 LOG2_E = 1.4426950408889634
 NT = (((1,), (1,)), ((), ()))
 NN = (((1,), (0,)), ((), ()))
@@ -24,30 +24,31 @@
 
 
 def query_side(
-    edge_ref, band_ref, q_ref, g_ref, left_ref, right_ref, bias_ref, dq_ref, stats_ref, *,
-    factor, tile
+    place_ref, edge_ref, band_ref, keys_ref, values_ref, q_ref, g_ref, left_ref, right_ref, bias_ref,
+    dq_ref, stats_ref, asked_ref, sems, *, factor, tile
 ):
-    for h in range(q_ref.shape[0]):
-        query_head(
-            h, edge_ref, band_ref, q_ref, g_ref, left_ref, right_ref, bias_ref, dq_ref,
-            stats_ref, factor=factor, tile=tile
-        )
-
-
-def query_head(
-    head, edge_ref, band_ref, q_ref, g_ref, left_ref, right_ref, bias_ref, dq_ref, stats_ref, *,
-    factor, tile
-):
-    rows, dim = q_ref.shape[1:]
-    keys = band_ref[:, 0, head].reshape(-1, dim)
-    values = band_ref[:, 1, head].reshape(-1, dim)
-    q = q_ref[head]
-    g = g_ref[head]
+    loads = [
+        pltpu.make_async_copy(band_ref.at[:, 2 + i, h], asked_ref.at[h, i], sems.at[h, i])
+        for h in range(asked_ref.shape[0])
+        for i in range(2)
+    ]
+
+    @pl.when(pl.program_id(0) == 0)
+    def _():
+        for load in loads:
+            load.start()
+
+    head = pl.program_id(0)
+    rows, dim = q_ref.shape[3:]
+    keys = keys_ref[:, 0, 0].reshape(-1, dim)
+    values = values_ref[:, 0, 0].reshape(-1, dim)
+    q = q_ref[0, 0, 0]
+    g = g_ref[0, 0, 0]
     shaped = (rows // tile, tile, keys.shape[0])
     scores = dot(q, keys, NT) * (factor * LOG2_E)
-    scores = (scores.reshape(shaped) + bias_ref[head][:, None, :]).reshape(rows, -1)
-    edge_keys = (left_ref[0, head], right_ref[0, head])
-    edge_values = (left_ref[1, head], right_ref[1, head])
+    scores = (scores.reshape(shaped) + bias_ref[0][:, None, :]).reshape(rows, -1)
+    edge_keys = (left_ref[0, 0], right_ref[0, 0])
+    edge_values = (left_ref[1, 0], right_ref[1, 0])
     edge_q = (q[:tile], q[rows - tile:])
     edge_g = (g[:tile], g[rows - tile:])
     edge_scores = [
@@ -85,36 +86,41 @@
         part = edge_powers[i] * (edge_slopes[i] - own(delta, i))
         edge_dq.append(dot(part.astype(jnp.bfloat16), edge_keys[i], NN))
     last = scale * factor
-    dq_ref[head, :tile] = ((dq[:tile] + edge_dq[0]) * own(last, 0)).astype(jnp.bfloat16)
+    dq_ref[0, :tile] = ((dq[:tile] + edge_dq[0]) * own(last, 0)).astype(jnp.bfloat16)
     if inner:
         middle = slice(tile, rows - tile)
-        dq_ref[head, middle] = (dq[middle] * last[middle]).astype(jnp.bfloat16)
-    dq_ref[head, rows - tile:] = ((dq[rows - tile:] + edge_dq[1]) * own(last, 1)).astype(jnp.bfloat16)
-    stats_ref[head, 0:1] = as_row(top + jnp.log2(total))
-    stats_ref[head, 1:2] = as_row(delta)
+        dq_ref[0, middle] = (dq[middle] * last[middle]).astype(jnp.bfloat16)
+    dq_ref[0, rows - tile:] = ((dq[rows - tile:] + edge_dq[1]) * own(last, 1)).astype(jnp.bfloat16)
+    stats_ref[0, 0:1] = as_row(top + jnp.log2(total))
+    stats_ref[0, 1:2] = as_row(delta)
+
+    @pl.when(head == pl.num_programs(0) - 1)
+    def _():
+        for load in loads:
+            load.wait()
 
 
 def key_side(
-    edge_ref, band_ref, all_stats_ref, k_ref, v_ref, left_ref, right_ref, left_stats_ref,
+    edge_ref, asked_ref, all_stats_ref, k_ref, v_ref, left_ref, right_ref, left_stats_ref,
     right_stats_ref, bias_ref, dk_ref, dv_ref, *, factor, tile
 ):
     for h in range(k_ref.shape[0]):
         key_head(
-            h, edge_ref, band_ref, all_stats_ref, k_ref, v_ref, left_ref, right_ref,
+            h, edge_ref, asked_ref, all_stats_ref, k_ref, v_ref, left_ref, right_ref,
             left_stats_ref, right_stats_ref, bias_ref, dk_ref, dv_ref, factor=factor, tile=tile
         )
 
 
 def key_head(
-    head, edge_ref, band_ref, all_stats_ref, k_ref, v_ref, left_ref, right_ref,
+    head, edge_ref, asked_ref, all_stats_ref, k_ref, v_ref, left_ref, right_ref,
     left_stats_ref, right_stats_ref, bias_ref, dk_ref, dv_ref, *, factor, tile
 ):
     rows, dim = k_ref.shape[1:]
-    bands = band_ref.shape[0]
+    bands = asked_ref.shape[2]
     k = k_ref[head]
     v = v_ref[head]
-    queries = band_ref[:, 2, head].reshape(-1, dim)
-    cotan = band_ref[:, 3, head].reshape(-1, dim)
+    queries = asked_ref[head, 0].reshape(-1, dim)
+    cotan = asked_ref[head, 1].reshape(-1, dim)
     scores = dot(k, queries, NT)
     slopes = dot(v, cotan, NT)
     grads, probs = [], []
@@ -205,28 +211,52 @@
     )
     edge_bias = jnp.where(edge_open, 0.0, CLOSED).astype(jnp.float32)
 
+    def per_head(shape):
+        return pl.BlockSpec((1,) + shape, lambda h, *_: (h,) + (0,) * len(shape))
+
     smem = pl.BlockSpec(memory_space=pltpu.SMEM)
+    own = per_head((rows, dim))
+    halo = pl.BlockSpec((4, 1, tile, dim), lambda h, *_: (0, h, 0, 0))
+    bias = per_head((dev_tiles, bands * rows))
+    stat = per_head((2, rows))
+
+    def of_band(slot):
+        return pl.BlockSpec((bands, 1, 1, rows, dim), lambda h, *_: (0, slot, h, 0, 0))
+
+    half = functools.partial(jax.ShapeDtypeStruct, dtype=jnp.bfloat16)
+    def of_own(slot):
+        return pl.BlockSpec((1, 1, 1, rows, dim), lambda h, at: (at[0], slot, h, 0, 0))
+
+    place = hb_index.astype(jnp.int32)[None]
     near = pl.BlockSpec(memory_space=pltpu.VMEM)
-    half = jax.ShapeDtypeStruct(flat, jnp.bfloat16)
+    far = pl.BlockSpec(memory_space=pltpu.HBM)
     params = pltpu.CompilerParams(vmem_limit_bytes=VMEM_BYTES)
-    dq, stats = pl.pallas_call(
+    dq, stats, asked = pl.pallas_call(
         functools.partial(query_side, factor=factor, tile=tile),
-        in_specs=[smem] + [near] * 6,
-        out_specs=[near, near],
-        out_shape=[half, jax.ShapeDtypeStruct((heads, 2, rows), jnp.float32)],
+        grid_spec=pltpu.PrefetchScalarGridSpec(
+            num_scalar_prefetch=1,
+            grid=(heads,),
+            in_specs=[smem, far, of_band(0), of_band(1), of_own(2), of_own(3), halo, halo, bias],
+            out_specs=[own, stat, near],
+            scratch_shapes=[pltpu.SemaphoreType.DMA((heads, 2))],
+        ),
+        out_shape=[
+            half(flat), jax.ShapeDtypeStruct((heads, 2, rows), jnp.float32),
+            half((heads, 2, bands, rows, dim)),
+        ],
         compiler_params=params,
         name="query_side",
-    )(edge_bias, band, q, g, left, right, own_bias)
+    )(place, edge_bias, band, band, band, band, band, left, right, own_bias)
     all_stats = lax.all_gather(stats, "hb")
     left_stats, right_stats = neighbours(stats, stats, "wb")
     dk, dv = pl.pallas_call(
         functools.partial(key_side, factor=factor, tile=tile),
         in_specs=[smem] + [near] * 9,
         out_specs=[near, near],
-        out_shape=[half, half],
+        out_shape=[half(flat), half(flat)],
         compiler_params=params,
         name="key_side",
-    )(edge_bias, band, all_stats, k, v, left, right, left_stats, right_stats, col_bias)
+    )(edge_bias, asked, all_stats, k, v, left, right, left_stats, right_stats, col_bias)
     return tuple(x.reshape(query_rows.shape) for x in (dq, dk, dv))
 
 

time: 117 us -> 114 us (0.974)
  local copies, waits for them, and re-layouts: 8.76 us -> 4.19 us
  Pallas kernels: 8.76 us -> 10.5 us
    unnamed x12 -> x6, local copies, waits for them, and re-layouts: 6.11 us -> 1.54 us
    pallas_call x1, Pallas kernels: 4.53 us -> 6.27 us  [on_device(): pl.pallas_call(functools.partial(query_side, factor=factor, tile=tile), g...]
where the time goes in v7:
time: 114 us; the launch traced here: 113 us
  waiting for transfers between devices  53.6 us (47%)
  blocking collectives  16.6 us (15%)
  between operations  14.2 us (12%)
  Pallas kernels  10.5 us (9%)
  starting transfers between devices  9.9 us (9%)
  local copies, waits for them, and re-layouts  4.19 us (4%)
  other arithmetic  3.8 us (3%)
    all_gather x1, waiting for transfers between devices, on_device(): band = lax.all_gather(jnp.stack(four), 'hb')  52.8 us
    all_gather x1, blocking collectives, on_device(): all_stats = lax.all_gather(stats, 'hb')  16.6 us
    ppermute x4, starting transfers between devices, neighbours(): return (lax.ppermute(last, axis, up), lax.ppermute(first, axis, down))  9.86 us
    pallas_call x1, Pallas kernels, on_device(): pl.pallas_call(functools.partial(query_side, factor=factor, tile=tile), g...  6.27 us
    pallas_call x1, Pallas kernels, on_device(): pl.pallas_call(functools.partial(key_side, factor=factor, tile=tile), in_...  4.25 us
  transfers between devices with their start and end apart: 5, of which 2 were waited for; matrix products, arithmetic and copies ran while one was open for 5% of the time, Pallas kernels for 0%

profile of v7, /device:TPU:1, one launch (start us, length us, event | category | flops | bytes accessed | tf_op | source)
XLA Modules:
  0.0 112.8 jit_solution(6435345907682271406)
XLA Ops:
  7.2 0.0 all-gather.4.cloned.1.call-start
  7.2 1.9 %pad_maximum_fusion = bf16[4,3,128,128]{3,2,1,0:T(8,128)(2,1)} fusion(bf16[1,3,128,128]{3,2,1,0:T(8,128)(2,1)} %bitcast.59, bf16[1,3,128,128]{3,2,1,0:T(8,128)(2,1)} %bitcast.61, bf16[1,3,128,128]{3,2,1,0:T(8,128)(2,1)} %bitcast.47, bf16[1,3,128,128]{3,2,1,0:T(8,128)(2,1)} %bitcast.50), kind=kLoop, calls=%fused_computation | loop fusion | flops 589824 | bytes 786432 | tf_op jit(solution)/shard_map/stack | solution.py:198
  9.1 0.0 all-gather.4.cloned.1.call-update
  9.1 0.9 slice_bitcast_fusion.2
  10.0 0.9 slice_bitcast_fusion
  10.9 4.1 %collective-permute-start = (bf16[4,3,64,128]{3,2,1,0:T(8,128)(2,1)S(1)}, bf16[4,3,64,128]{3,2,1,0:T(8,128)(2,1)S(1)}, u32[]{:S(2)}, u32[]{:S(2)}) collective-permute-start(bf16[4,3,64,128]{3,2,1,0:T(8,128)(2,1)S(1)} %pad_maximum_fusion.1), channel_id=1, source_target_pairs={{0,8},{8,16},{16,24},{24,32},{32,40},{40,48},{48,56},{1,9},{9,17},... | collective-permute-start | bytes 589832 | tf_op jit(solution)/shard_map/ppermute | solution.py:177
  15.1 1.3 %collective-permute-start.1 = (bf16[4,3,64,128]{3,2,1,0:T(8,128)(2,1)S(1)}, bf16[4,3,64,128]{3,2,1,0:T(8,128)(2,1)S(1)}, u32[]{:S(2)}, u32[]{:S(2)}) collective-permute-start(bf16[4,3,64,128]{3,2,1,0:T(8,128)(2,1)S(1)} %pad_maximum_fusion.2), channel_id=1, source_target_pairs={{8,0},{16,8},{24,16},{32,24},{40,32},{48,40},{56,48},{9,1},{17,9},... | collective-permute-start | bytes 589832 | tf_op jit(solution)/shard_map/ppermute | solution.py:177
  16.4 0.8 copy.35
  17.2 0.8 copy.36
  17.9 0.1 lt.35
  18.0 0.1 iota_compare_fusion.1
  18.1 0.2 fusion.1
  18.3 0.1 copy.37
  18.4 0.1 abs_add_fusion
  18.5 0.7 compare_or_fusion
  19.2 0.1 dynamic-slice_select_fusion
  19.3 0.1 copy.38
  19.4 0.1 broadcast_in_dim.52
  19.5 0.1 reshape.169.bias_ref
  19.6 0.7 and_bitcast_fusion.1
  20.3 0.1 copy.33
  20.4 0.1 copy.34
  20.5 0.1 broadcast_in_dim.55
  20.6 0.1 reshape.171.bias_ref
  20.7 0.1 add_select_fusion.edge_ref
  20.8 0.0 collective-permute-done.left_ref
  20.8 0.8 collective-permute-done.1.right_ref
  21.5 52.8 %all-gather.4.cloned.1.call-done = bf16[64,3,128,128]{3,2,1,0:T(8,128)(2,1)} async-done(((bf16[4,3,128,128]{3,2,1,0:T(8,128)(2,1)}), bf16[64,3,128,128]{3,2,1,0:T(8,128)(2,1)}) %all-gather.4.cloned.1.call-update) | async-done | bytes 6291472 | tf_op jit(solution)/shard_map/all_gather | solution.py:198
  74.4 0.0 copy-start
  74.4 0.0 copy-start.1
  74.4 6.3 %query_side.1 = (bf16[3,128,128]{2,1,0:T(8,128)(2,1)}, f32[3,2,128]{2,1,0:T(2,128)S(1)}, bf16[3,2,16,128,128]{4,3,2,1,0:T(8,128)(2,1)S(1)}) custom-call(s32[1]{0:T(128)} %bitcast.place_ref, f32[3,2]{1,0:T(4,128)S(1)} %add_select_fusion.edge_ref, bf16[16,4,3,128,128]{4,3,2,1,0:T(8,128)(2,1)} %bitcast.54, bf16[16,4,3,128,128]{4,3,2,1,0:T(8,128)(2,1)} %bitcast.55, ...), custom_call_target="tpu_custom_call" | custom-call | tf_op jit(solution)/shard_map/query_side/pallas_call | solution.py:234
  80.6 3.1 %collective-permute-start.2 = (f32[3,2,128]{2,1,0:T(2,128)S(1)}, f32[3,2,128]{2,1,0:T(2,128)S(1)}, u32[]{:S(2)}, u32[]{:S(2)}) collective-permute-start(f32[3,2,128]{2,1,0:T(2,128)S(1)} %get-tuple-element.10), channel_id=1, source_target_pairs={{0,8},{8,16},{16,24},{24,32},{32,40},{40,48},{48,56},{1,9},{9,17},... | collective-permute-start | bytes 9224 | tf_op jit(solution)/shard_map/ppermute | solution.py:177
  83.8 1.3 %collective-permute-start.3 = (f32[3,2,128]{2,1,0:T(2,128)S(1)}, f32[3,2,128]{2,1,0:T(2,128)S(1)}, u32[]{:S(2)}, u32[]{:S(2)}) collective-permute-start(f32[3,2,128]{2,1,0:T(2,128)S(1)} %get-tuple-element.10), channel_id=1, source_target_pairs={{8,0},{16,8},{24,16},{32,24},{40,32},{48,40},{56,48},{9,1},{17,9},... | collective-permute-start | bytes 9224 | tf_op jit(solution)/shard_map/ppermute | solution.py:177
  85.1 16.6 %all-gather.1 = f32[48,2,128]{2,1,0:T(2,128)S(1)} all-gather(f32[3,2,128]{2,1,0:T(2,128)S(1)} %get-tuple-element.10), channel_id=3, replica_groups=mesh['hb'=16,'wb'=8,'hd'=8] {'hb'}, dimensions={0}, use_global_device_ids=true | all-gather | bytes 52224 | tf_op jit(solution)/shard_map/all_gather | solution.py:250
  101.7 0.0 collective-permute-done.2.left_stats_ref
  101.7 0.0 collective-permute-done.3.right_stats_ref
  101.7 0.0 copy-done
  101.7 0.0 copy-done.1
  101.7 4.2 %key_side.1 = (bf16[3,128,128]{2,1,0:T(8,128)(2,1)}, bf16[3,128,128]{2,1,0:T(8,128)(2,1)}) custom-call(f32[3,2]{1,0:T(4,128)S(1)} %add_select_fusion.edge_ref, bf16[3,2,16,128,128]{4,3,2,1,0:T(8,128)(2,1)S(1)} %get-tuple-element.9.asked_ref, f32[16,3,2,128]{3,2,1,0:T(2,128)S(1)} %bitcast.53, bf16[3,128,128]{2,1,0:T(8,128)(2,1)S(1)} %bitcast.52, ...), custom_call_target="tpu_custom_call" | custom-call | tf_op jit(solution)/shard_map/key_side/pallas_call | solution.py:252
  (4 shorter events, 0.1 us)
Async XLA Ops:
  7.2 67.2 %all-gather.4.cloned.1.call-start = ((), (), s32[]{:S(2)}) async-start(), calls=%async_computation | async-start | bytes 6684672 | tf_op jit(solution)/shard_map/all_gather | solution.py:198
  10.9 9.8 %collective-permute-start = (bf16[4,3,64,128]{3,2,1,0:T(8,128)(2,1)S(1)}, bf16[4,3,64,128]{3,2,1,0:T(8,128)(2,1)S(1)}, u32[]{:S(2)}, u32[]{:S(2)}) collective-permute-start(bf16[4,3,64,128]{3,2,1,0:T(8,128)(2,1)S(1)} %pad_maximum_fusion.1), channel_id=1, source_target_pairs={{0,8},{8,16},{16,24},{24,32},{32,40},{40,48},{48,56},{1,9},{9,17},... | collective-permute-start | bytes 589832 | tf_op jit(solution)/shard_map/ppermute | solution.py:177
  15.1 6.4 %collective-permute-start.1 = (bf16[4,3,64,128]{3,2,1,0:T(8,128)(2,1)S(1)}, bf16[4,3,64,128]{3,2,1,0:T(8,128)(2,1)S(1)}, u32[]{:S(2)}, u32[]{:S(2)}) collective-permute-start(bf16[4,3,64,128]{3,2,1,0:T(8,128)(2,1)S(1)} %pad_maximum_fusion.2), channel_id=1, source_target_pairs={{8,0},{16,8},{24,16},{32,24},{40,32},{48,40},{56,48},{9,1},{17,9},... | collective-permute-start | bytes 589832 | tf_op jit(solution)/shard_map/ppermute | solution.py:177
  74.4 27.3 %copy-start = (bf16[3,1,2,64,128]{4,3,2,1,0:T(8,128)(2,1)S(1)}, bf16[3,1,2,64,128]{4,3,2,1,0:T(8,128)(2,1)}, u32[]{:S(2)}) copy-start(bf16[3,1,2,64,128]{4,3,2,1,0:T(8,128)(2,1)} %param.9) | copy-start | bytes 294916
  74.4 27.3 %copy-start.1 = (bf16[3,1,2,64,128]{4,3,2,1,0:T(8,128)(2,1)S(1)}, bf16[3,1,2,64,128]{4,3,2,1,0:T(8,128)(2,1)}, u32[]{:S(2)}) copy-start(bf16[3,1,2,64,128]{4,3,2,1,0:T(8,128)(2,1)} %param.8) | copy-start | bytes 294916
  80.6 21.0 %collective-permute-start.2 = (f32[3,2,128]{2,1,0:T(2,128)S(1)}, f32[3,2,128]{2,1,0:T(2,128)S(1)}, u32[]{:S(2)}, u32[]{:S(2)}) collective-permute-start(f32[3,2,128]{2,1,0:T(2,128)S(1)} %get-tuple-element.10), channel_id=1, source_target_pairs={{0,8},{8,16},{16,24},{24,32},{32,40},{40,48},{48,56},{1,9},{9,17},... | collective-permute-start | bytes 9224 | tf_op jit(solution)/shard_map/ppermute | solution.py:177
  83.8 17.9 %collective-permute-start.3 = (f32[3,2,128]{2,1,0:T(2,128)S(1)}, f32[3,2,128]{2,1,0:T(2,128)S(1)}, u32[]{:S(2)}, u32[]{:S(2)}) collective-permute-start(f32[3,2,128]{2,1,0:T(2,128)S(1)} %get-tuple-element.10), channel_id=1, source_target_pairs={{8,0},{16,8},{24,16},{32,24},{40,32},{48,40},{56,48},{9,1},{17,9},... | collective-permute-start | bytes 9224 | tf_op jit(solution)/shard_map/ppermute | solution.py:177
Sparse Core Ops, SparseCore 0:
  10.7 63.6 all-gather.3
